TPU v7x, 512 devices: a whole 4x8x8 slice. The times are simulated.
512 devices in a mesh: outer: 2 (over core), row: 256 (over y, z, x).
Axes of the slice: x: 4, y: 8, z: 8, core: 2. Of those that a mesh axis runs over, the one named last changes fastest.
Arguments:
- grad_gate: bfloat16 [2, 8192, 14336], P('outer', 'row'), may hold values from -24 to 24
- grad_up: bfloat16 [2, 8192, 14336], P('outer', 'row'), may hold values from -24 to 24
- basis_gate: bfloat16 [32, 14336], P(None, 'row'), may hold values from -0.046875 to 0.046875
- basis_up: bfloat16 [32, 14336], P(None, 'row'), may hold values from -0.046875 to 0.046875
Outputs:
- next_gate: float32 [32, 14336], P(None, 'row')
- next_up: float32 [32, 14336], P(None, 'row')
- factor_gate: float32 [8192, 32], P('row')
- factor_up: float32 [8192, 32], P('row')
- resid_gate: bfloat16 [2, 8192, 14336], P('outer', 'row')
- resid_up: bfloat16 [2, 8192, 14336], P('outer', 'row')
All inputs are finite; a program needn't handle non-finite values.
Results may differ from a plain program's by a relative error of at most 0.005.
Values may be sent and summed in bfloat16 or wider, within the bound.
No kernel may reach another device: no remote copies, remote signals or barrier semaphores. Data moves between devices by JAX's collectives and lax.ppermute only.
A program may use at most 64 MiB of HBM per device.

v0:
```python
import jax
import jax.numpy as jnp
from jax import lax
from jax.sharding import Mesh
from jax.sharding import PartitionSpec as P

ROW = ("row_0", "row_1", "row_2")
OUTER_ROW = ("outer", "row_0", "row_1", "row_2")


def gather_turned(arrays, axis, dims):
    turned = [jnp.moveaxis(a, dim, 0) for a, dim in zip(arrays, dims)]
    widths = [t[0].size for t in turned]
    both = jnp.concatenate([t.reshape(-1, w) for t, w in zip(turned, widths)], axis=1)
    out = lax.all_gather(both, axis, axis=0, tiled=True)
    tiles = jnp.split(out, [sum(widths[:k]) for k in range(1, len(widths))], axis=1)
    return tuple(
        (
            jnp.moveaxis(b.reshape(-1, *t.shape[1:]), 0, dim)
            for b, t, dim in zip(tiles, turned, dims)
        )
    )


def copy_for_each(x, axis):
    peers = lax.axis_size(axis)
    return lax.all_to_all(jnp.broadcast_to(x[None], (peers, *x.shape)), axis, 0, 0, tiled=True)


def taken_together(x, axis):
    everything = copy_for_each(x, axis)
    return jnp.sum(everything, axis=0)


def together(arrays, axis):
    line, at, finished = (jnp.concatenate([a.reshape(-1) for a in arrays]), 0, [])
    so_far = taken_together(line, axis)
    for a in arrays:
        finished.append(so_far[at : at + a.size].reshape(a.shape))
        at += a.size
    return tuple(finished)


def over_axes(x, axes):
    for axis in axes:
        x = lax.psum(x, axis)
    return x


def forward_solve(lower_matrix, right_hand):
    return jax.scipy.linalg.solve_triangular(lower_matrix, right_hand, lower=True)


def contract_cols(left, right):
    return lax.dot_general(
        left, right, (((1,), (1,)), ((), ())), preferred_element_type=jnp.float32
    )


def contract_rows(left, right):
    return lax.dot_general(
        left, right, (((0,), (0,)), ((), ())), preferred_element_type=jnp.float32
    )


def local(grad_gate, grad_up, basis_gate, basis_up):
    pod_count = lax.axis_size("outer")
    gate_rows = grad_gate[0]
    up_rows = grad_up[0]
    full_cols = gate_rows.shape[1]
    pieces = gather_turned((basis_gate, basis_up), ROW, (1, 1))
    summed = together(
        (contract_cols(gate_rows, pieces[0]), contract_cols(up_rows, pieces[1])), "outer"
    )
    round_gate = (summed[0] / pod_count).astype(jnp.bfloat16)
    round_up = (summed[1] / pod_count).astype(jnp.bfloat16)
    gram_pair = (
        over_axes(contract_rows(round_gate, round_gate), ROW),
        over_axes(contract_rows(round_up, round_up), ROW),
    )
    lower_gate = jnp.linalg.cholesky(gram_pair[0])
    lower_up = jnp.linalg.cholesky(gram_pair[1])
    products = (contract_rows(round_gate, gate_rows), contract_rows(round_up, up_rows))
    shard_cols = full_cols // lax.axis_size(ROW)
    shard_start = lax.axis_index(ROW) * shard_cols
    totals = lax.psum((products[0], products[1]), OUTER_ROW)
    full_gate = forward_solve(lower_gate, totals[0] / pod_count)
    full_up = forward_solve(lower_up, totals[1] / pod_count)
    next_gate = lax.dynamic_slice_in_dim(full_gate, shard_start, shard_cols, 1)
    next_up = lax.dynamic_slice_in_dim(full_up, shard_start, shard_cols, 1)
    factor_gate = forward_solve(lower_gate, round_gate.astype(jnp.float32).T).T
    factor_up = forward_solve(lower_up, round_up.astype(jnp.float32).T).T
    resid_gate = (
        gate_rows - jnp.dot(factor_gate, full_gate, precision=lax.Precision.HIGHEST)
    ).astype(jnp.bfloat16)
    resid_up = (up_rows - jnp.dot(factor_up, full_up, precision=lax.Precision.HIGHEST)).astype(
        jnp.bfloat16
    )
    return (next_gate, next_up, factor_gate, factor_up, resid_gate[None], resid_up[None])


def solution(mesh):
    finer = Mesh(
        mesh.devices.reshape(mesh.shape["outer"], 8, 8, 4), ("outer", "row_0", "row_1", "row_2")
    )
    placed = (P("outer", ROW, None), P("outer", ROW, None), P(None, ROW), P(None, ROW))
    return jax.shard_map(
        local,
        mesh=finer,
        in_specs=placed,
        out_specs=(
            P(None, ROW),
            P(None, ROW),
            P(ROW, None),
            P(ROW, None),
            P("outer", ROW, None),
            P("outer", ROW, None),
        ),
        check_vma=False,
    )
```

profile of v0, /device:TPU:1, one launch (start us, length us, event | category | flops | bytes accessed | tf_op | source)
XLA Modules:
  0.0 461.2 jit_solution(15747736612643531091)
XLA Ops:
  7.2 0.8 copy.45
  8.0 0.8 copy.44
  8.8 0.7 pad_maximum_fusion
  9.6 131.7 %all-gather.2.cloned.1.call-done = bf16[14336,64]{1,0:T(8,128)(2,1)} async-done(((bf16[56,64]{1,0:T(8,128)(2,1)}), bf16[14336,64]{1,0:T(8,128)(2,1)}) %all-gather.2.cloned.1.call-update) | async-done | bytes 1835024 | tf_op jit(solution)/shard_map/all_gather | solution.py:15
  141.2 4.3 fusion.15
  145.7 3.1 fusion.12
  149.1 8.5 %all_to_all.6 = f32[2,1,2048]{2,1,0:T(1,128)S(1)} all-to-all(f32[2,1,2048]{2,1,0:T(1,128)S(1)} %broadcast_in_dim.7), channel_id=1, replica_groups=mesh['outer'=2,'row_0'=8,'row_1'=8,'row_2'=4] {'outer'}, dimensions={0} | all-to-all | bytes 32768 | tf_op jit(solution)/shard_map/all_to_all | solution.py:27
  157.7 1.7 fusion.21
  159.5 1.7 fusion.18
  161.2 0.2 fusion.44
  161.6 22.9 %all-reduce.2 = (f32[32,32]{0,1:T(8,128)S(1)}, f32[32,32]{0,1:T(8,128)S(1)}) all-reduce(f32[32,32]{0,1:T(8,128)S(1)} %fusion.44, f32[32,32]{0,1:T(8,128)S(1)} %fusion.45), channel_id=1, replica_groups=mesh['outer'=2,'row_0'=8,'row_1'=8,'row_2'=4] {'row_0'}, use_global_device_ids=true, to_apply=%region_1.0 | all-reduce | flops 2048 | bytes 16384 | tf_op jit(solution)/shard_map/psum | solution.py:46
  184.5 22.5 %all-reduce.1 = (f32[32,32]{0,1:T(8,128)S(1)}, f32[32,32]{0,1:T(8,128)S(1)}) all-reduce(f32[32,32]{0,1:T(8,128)S(1)} %get-tuple-element.43, f32[32,32]{0,1:T(8,128)S(1)} %get-tuple-element.44), channel_id=1, replica_groups=mesh['outer'=2,'row_0'=8,'row_1'=8,'row_2'=4] {'row_1'}, use_global_device_ids=true, to_apply=%region_2.0 | all-reduce | flops 2048 | bytes 16384 | tf_op jit(solution)/shard_map/psum | solution.py:46
  207.0 12.3 %all-reduce.3 = (f32[32,32]{0,1:T(8,128)S(1)}, f32[32,32]{0,1:T(8,128)S(1)}) all-reduce(f32[32,32]{0,1:T(8,128)S(1)} %get-tuple-element.41, f32[32,32]{0,1:T(8,128)S(1)} %get-tuple-element.42), channel_id=1, replica_groups=mesh['outer'=2,'row_0'=8,'row_1'=8,'row_2'=4] {'row_2'}, use_global_device_ids=true, to_apply=%region_3.0 | all-reduce | flops 2048 | bytes 16384 | tf_op jit(solution)/shard_map/psum | solution.py:46
  219.4 2.9 cholesky.44
  222.4 0.6 compare_reduce_fusion.1
  223.0 0.7 fusion.26
  223.7 2.4 custom-call.10
  226.1 2.9 cholesky.55
  229.1 0.6 compare_reduce_fusion
  229.7 0.7 fusion.27
  230.4 2.4 custom-call.11
  232.8 0.2 fusion.30
  233.0 0.7 copy.53
  233.7 0.2 fusion.28
  233.9 0.7 copy.54
  234.6 208.2 %all-reduce.6.cloned.1.call-done = (f32[32,14336]{1,0:T(8,128)}, f32[32,14336]{1,0:T(8,128)}) async-done(((f32[32,14336]{1,0:T(8,128)}, f32[32,14336]{1,0:T(8,128)}), (f32[32,14336]{1,0:T(8,128)}, f32[32,14336]{1,0:T(8,128)})) %all-reduce.6.cloned.1.call-update) | async-done | bytes 3670032 | tf_op jit(solution)/shard_map/psum | solution.py:86
  442.9 3.1 fusion.10
  446.0 2.7 fusion.3
  448.7 0.7 constant_dynamic-slice_fusion.1
  449.4 1.6 fusion.8
  451.0 0.7 constant_dynamic-slice_fusion
  451.7 2.6 fusion.2
  (26 shorter events, 1.1 us)
Async XLA Ops:
  7.2 134.1 %all-gather.2.cloned.1.call-start = ((), (), s32[]{:S(2)}) async-start(), calls=%async_computation.1 | async-start | bytes 3684352 | tf_op jit(solution)/shard_map/all_gather | solution.py:15
  9.5 433.4 %all-reduce.6.cloned.1.call-start = ((), (), s32[]{:S(2)}) async-start(), calls=%async_computation.2 | async-start | bytes 7340032 | tf_op jit(solution)/shard_map/psum | solution.py:86
  9.6 136.2 %copy-start = (bf16[1,32,14336]{2,1,0:T(8,128)(2,1)S(1)}, bf16[1,32,14336]{2,1,0:T(8,128)(2,1)}, u32[]{:S(2)}) copy-start(bf16[1,32,14336]{2,1,0:T(8,128)(2,1)} %param.9) | copy-start | bytes 2752516
  148.9 10.6 %copy-start.1 = (bf16[1,32,14336]{2,1,0:T(8,128)(2,1)S(1)}, bf16[1,32,14336]{2,1,0:T(8,128)(2,1)}, u32[]{:S(2)}) copy-start(bf16[1,32,14336]{2,1,0:T(8,128)(2,1)} %param.10) | copy-start | bytes 2752516
  446.0 3.3 copy-start.2
Sparse Core Ops, SparseCore 0:
  13.0 128.2 all-gather.1
  161.3 281.5 all-reduce.5
where the time goes:
time: 462 us; the launch traced here: 461 us
  waiting for transfers between devices  340 us (74%)
  blocking collectives  66.2 us (14%)
  matrix products  21.8 us (5%)
  other arithmetic  14.1 us (3%)
  between operations  14.1 us (3%)
  local copies, waits for them, and re-layouts  4.98 us (1%)
    psum x1, waiting for transfers between devices, local(): totals = lax.psum((products[0], products[1]), OUTER_ROW)  208 us
    all_gather x1, waiting for transfers between devices, gather_turned(): out = lax.all_gather(both, axis, axis=0, tiled=True)  132 us
    psum x3, blocking collectives, over_axes(): x = lax.psum(x, axis)  57.7 us
  transfers between devices with their start and end apart: 2, of which 2 were waited for; matrix products, arithmetic and copies ran while one was open for 3% of the time, Pallas kernels for 0%

commit v1 on v0

v1 whole, which is shorter than its diff:
```python
import functools

import jax
import jax.numpy as jnp
from jax import lax
from jax.experimental import pallas as pl
from jax.experimental.pallas import tpu as pltpu
from jax.sharding import Mesh
from jax.sharding import PartitionSpec as P

ROW = ("yq", "yp", "zq", "zp", "x")
NEAR = ("yp", "zp", "x")
FAR = ("yq", "zq")
BF = jnp.bfloat16
F32 = jnp.float32
R = 32
W = 56
TILE = 8
PERIOD = 16 * W
INTERPRET = False


def place(d, sizes):
    _, yp, zq, zp, x = sizes
    at_x, d = d % x, d // x
    at_zp, d = d % zp, d // zp
    at_zq, d = d % zq, d // zq
    at_yp, at_yq = d % yp, d // yp
    near = (at_yp * zp + at_zp) * x + at_x
    return (near * sizes[0] + at_yq) * zq + at_zq


def groups(shape):
    return lax.broadcasted_iota(jnp.int32, shape, 1) // R


def three_terms(x):
    high = x.astype(BF).astype(F32)
    middle = (x - high).astype(BF).astype(F32)
    low = (x - high - middle).astype(BF).astype(F32)
    return high, middle, low


def dot(a, b, ca, cb, precision=None):
    return lax.dot_general(
        a, b, (((ca,), (cb,)), ((), ())), precision=precision, preferred_element_type=F32
    )


def prepare_kernel(bg_ref, bu_ref, gg_ref, gu_ref, block_ref, send_ref, sem):
    core = lax.axis_index("outer")

    @pl.when(core == 0)
    def _():
        pltpu.make_async_copy(gu_ref.at[0], send_ref, sem).start()

    @pl.when(core != 0)
    def _():
        pltpu.make_async_copy(gg_ref.at[0], send_ref, sem).start()

    mine = jnp.where(core == 0, bg_ref[...].astype(F32), bu_ref[...].astype(F32))
    turned = mine.T
    empty = jnp.zeros((TILE, R), F32)
    rows = []
    for h in range(2):
        tiles = [turned[8 * t : 8 * t + 8] if t < 7 else empty for t in range(4 * h, 4 * h + 4)]
        rows.append(jnp.concatenate(tiles, axis=1))
    block = jnp.concatenate(rows, axis=0).astype(BF)
    block_ref[...] = jnp.broadcast_to(block[None], block_ref.shape)
    pltpu.make_async_copy(gg_ref.at[0], send_ref, sem).wait()


def pack_kernel(sizes, gg_ref, gu_ref, other_ref, packed_ref, turned_ref, both, sem):
    core = lax.axis_index("outer")

    @pl.when(core == 0)
    def _():
        pltpu.make_async_copy(gg_ref.at[0], both.at[0], sem.at[0]).start()

    @pl.when(core != 0)
    def _():
        pltpu.make_async_copy(gu_ref.at[0], both.at[0], sem.at[0]).start()

    second = pltpu.make_async_copy(other_ref, both.at[1], sem.at[1])
    second.start()
    pltpu.make_async_copy(gg_ref.at[0], both.at[0], sem.at[0]).wait()
    second.wait()
    empty = jnp.zeros((TILE, 2 * R), F32)

    @pl.loop(0, packed_ref.shape[0] // 256)
    def _(k):
        columns = pl.ds(pl.multiple_of(k * PERIOD, 128), PERIOD)
        x = jnp.concatenate(
            [both.at[0][:, columns].astype(F32), both.at[1][:, columns].astype(F32)], axis=0
        )
        xt = x.T
        first = place(16 * k, sizes)
        for d in range(16):
            rows = []
            for h in range(2):
                tiles = []
                for t in range(4 * h, 4 * h + 4):
                    at = 8 * (7 * d + t)
                    tiles.append(xt[at : at + 8] if t < 7 else empty)
                rows.append(jnp.concatenate(tiles, axis=1))
            to = pl.multiple_of(16 * (first + place(d, sizes)), 16)
            packed_ref[pl.ds(to, 16), :] = jnp.concatenate(rows, axis=0).astype(BF)

    @pl.loop(0, packed_ref.shape[0] // 256)
    def _(k):
        part = pl.ds(pl.multiple_of(k * 256, 256), 256)
        turned_ref[:, part] = packed_ref[part, :].astype(F32).T.astype(BF)


def products_kernel(basis_ref, turned_ref, packed_ref, sums_ref, left_ref, extra):
    partial = dot(turned_ref[...], basis_ref[...], 1, 0)
    group = groups((R, 128))
    total = jnp.zeros((R, 128), F32)
    for q in range(4):
        slab = partial[64 * q : 64 * q + R] + partial[64 * q + R : 64 * q + 64]
        total = total + jnp.where(group == q, slab, 0.0)
    total = total + pltpu.roll(total, 64, 1)
    total = total + pltpu.roll(total, 32, 1)
    left = (0.5 * total).astype(BF)
    left_ref[...] = left
    wide = left.astype(F32)
    pieces = []
    for q in range(4):
        one = jnp.where(group == q, wide, 0.0)
        pieces += [one, one]
    spread = jnp.concatenate(pieces, axis=0).astype(BF)
    gram = dot(left, left, 0, 0)[0:R]
    gram = jnp.where(group == 3, gram, 0.0)
    extra[...] = jnp.zeros_like(extra)
    for s, term in enumerate(three_terms(gram)):
        extra[pl.ds(8 + s, R, stride=16), :] = term
    step = 512
    for k in range(packed_ref.shape[0] // step):
        out = dot(packed_ref[pl.ds(k * step, step), :], spread, 1, 0)
        if k == 0:
            out = out + extra[...]
        sums_ref[pl.ds(k * step, step), :] = out.astype(BF)


def summed(parts_ref, scale):
    count, rows, _ = parts_ref.shape

    def add(k, acc):
        return acc + parts_ref[k].astype(F32)

    acc = lax.fori_loop(0, count, add, jnp.zeros((rows, 128), F32), unroll=4)
    acc = acc.reshape(rows // 16, 16, 128)
    gram = acc[:, 8:9] + acc[:, 9:10] + acc[:, 10:11]
    row = lax.broadcasted_iota(jnp.int32, acc.shape, 1)
    lane = lax.broadcasted_iota(jnp.int32, acc.shape, 2)
    high, middle, low = three_terms(gram)
    term = jnp.where(row == 8, high, jnp.where(row == 9, middle, jnp.where(row == 10, low, 0.0)))
    out = jnp.where((row >= 8) & (lane >= 96), term, scale * acc)
    return out.reshape(rows, 128)


def halfway_kernel(parts_ref, out_ref):
    out_ref[...] = summed(parts_ref, 1.0).astype(BF)


def total_kernel(parts_ref, left_ref, block_ref, kept_ref):
    out = summed(parts_ref, 0.5)
    block_ref[...] = jnp.broadcast_to(out.astype(BF)[None], block_ref.shape)
    kept_ref[0:16] = out
    kept_ref[16:48] = left_ref[...].astype(F32)


def last_kernel(
    sizes, own_ref, other_ref, kept_ref, kept_other_ref, gg_ref, gu_ref,
    ng_ref, nu_ref, fg_ref, fu_ref, rg_ref, ru_ref,
    grads, resid, spread, sem_in, sem_out,
):
    core = lax.axis_index("outer")
    loads = [
        pltpu.make_async_copy(ref.at[0], grads.at[k], sem_in.at[k])
        for k, ref in enumerate((gg_ref, gu_ref))
    ]
    for load in loads:
        load.start()
    high = lax.Precision.HIGHEST
    group = groups((R, 128))
    row = lax.broadcasted_iota(jnp.int32, (R, 128), 0)
    lane = lax.broadcasted_iota(jnp.int32, (R, 128), 1)
    grams = []
    for j, ref in enumerate((own_ref, other_ref)):
        spread[j] = ref[pl.ds(0, 512), :].astype(F32)
        gram = spread.at[j][pl.ds(8, R, stride=16), :]
        gram = gram + spread.at[j][pl.ds(9, R, stride=16), :]
        gram = gram + spread.at[j][pl.ds(10, R, stride=16), :]
        grams.append(pltpu.roll(gram, 32 if j == 0 else 96, 1))
    m = jnp.where(group == 0, grams[0], jnp.where(group == 2, grams[1], 0.0))
    m = jnp.where((group % 2 == 1) & (row == lane % R), 1.0, m)
    scale = jnp.zeros((R, 128), F32)
    for k in range(R):
        pivot_row = m[k : k + 1]
        first = jnp.broadcast_to(m[:, k : k + 1], (R, 128))
        second = jnp.broadcast_to(m[:, 64 + k : 65 + k], (R, 128))
        column = jnp.where(lane < 64, first, second)
        pivot = column[k : k + 1]
        scale = jnp.where(row == k, lax.rsqrt(pivot), scale)
        if k < R - 1:
            m = m - jnp.where(row > k, column / pivot, 0.0) * pivot_row
    inverse = m * scale
    kept = (kept_ref[...], kept_other_ref[...])
    nexts, factors, sides = [], [], []
    for j in range(2):
        at = 1 if j == 0 else 3
        one = jnp.where(group == at, inverse, 0.0)
        one = one + pltpu.roll(one, 64, 1)
        one = one + pltpu.roll(one, 32, 1)
        u = kept[j][0:16]
        left = kept[j][16:48]
        tiles = []
        for t in range(7):
            h, q = divmod(t, 4)
            tiles.append(jnp.where(groups((8, 128)) == q, u[8 * h : 8 * h + 8], 0.0))
        nexts.append(dot(one, jnp.concatenate(tiles, axis=0), 1, 1, high))
        factor = dot(jnp.where(group == 0, left, 0.0), one, 1, 1, high)
        factors.append(factor)
        side = dot(factor, one, 1, 0, high)
        top = side.astype(BF)
        rest = (side - top.astype(F32)).astype(BF)
        sides.append(jnp.concatenate([top, rest], axis=0))
    swap = core != 0
    ng_ref[...] = jnp.where(swap, nexts[1], nexts[0])
    nu_ref[...] = jnp.where(swap, nexts[0], nexts[1])
    fg_ref[...] = jnp.where(swap, factors[1], factors[0])
    fu_ref[...] = jnp.where(swap, factors[0], factors[1])
    for load in loads:
        load.wait()
    tile_group = groups((8, 128))
    stores = [
        pltpu.make_async_copy(resid.at[k], ref.at[0], sem_out.at[k])
        for k, ref in enumerate((rg_ref, ru_ref))
    ]
    for j, ref in enumerate((own_ref, other_ref)):
        at = core if j == 0 else 1 - core
        side = sides[j]

        @pl.loop(0, ref.shape[0] // 256)
        def _(k):
            first = place(16 * k, sizes)
            rows = []
            for d in range(16):
                at_d = pl.multiple_of(16 * (first + place(d, sizes)), 16)
                x = ref[pl.ds(at_d, 16), :].astype(F32)
                for t in range(7):
                    h, q = divmod(t, 4)
                    tile = x[8 * h : 8 * h + 8]
                    rows.append(jnp.where(tile_group == q, tile, 0.0))
            right = jnp.concatenate(rows, axis=0).astype(BF)
            both = dot(side, right, 1, 1)
            columns = pl.ds(pl.multiple_of(k * PERIOD, 128), PERIOD)
            value = grads.at[at][:, columns].astype(F32) - (both[0:R] + both[R : 2 * R])
            resid.at[at][:, columns] = value.astype(BF)

        @pl.when(at == 0)
        def _():
            stores[0].start()

        @pl.when(at != 0)
        def _():
            stores[1].start()

    for store in stores:
        store.wait()


def call(kernel, outs, scratch, spaces_in, spaces_out, cost, limit):
    any_space, vmem = pl.BlockSpec(memory_space=pl.ANY), pl.BlockSpec(memory_space=pltpu.VMEM)
    pick = lambda s: any_space if s == "a" else vmem
    return pl.pallas_call(
        kernel,
        out_shape=outs,
        in_specs=[pick(s) for s in spaces_in],
        out_specs=tuple(pick(s) for s in spaces_out) if len(spaces_out) > 1 else pick(spaces_out),
        scratch_shapes=scratch,
        cost_estimate=pl.CostEstimate(flops=cost, bytes_accessed=cost // 16, transcendentals=0),
        compiler_params=pltpu.CompilerParams(vmem_limit_bytes=limit << 20),
        interpret=INTERPRET,
    )


def shape(dims, dtype):
    return jax.ShapeDtypeStruct(dims, dtype)


def local(grad_gate, grad_up, basis_gate, basis_up):
    sizes = tuple(lax.axis_size(a) for a in ROW)
    near, far = lax.axis_size(NEAR), lax.axis_size(FAR)
    columns = grad_gate.shape[2]
    packed_rows = 16 * near * far
    swap = [(0, 1), (1, 0)]
    dma = pltpu.SemaphoreType.DMA

    def exchange(x, axes):
        return lax.all_to_all(x, axes, 0, 0, tiled=True)

    def gather(block):
        line = exchange(block, FAR).reshape(16 * far, 128)
        copies = jnp.broadcast_to(line[None], (near, 16 * far, 128))
        return exchange(copies, NEAR).reshape(packed_rows, 128)

    block, send = call(
        prepare_kernel,
        (shape((far, 16, 128), BF), shape((R, columns), BF)),
        [dma],
        "vvaa",
        "vv",
        1 << 20,
        6,
    )(basis_gate, basis_up, grad_gate, grad_up)
    other = lax.ppermute(send, "outer", swap)
    basis = gather(block)
    packed, turned = call(
        functools.partial(pack_kernel, sizes),
        (shape((packed_rows, 256), BF), shape((256, packed_rows), BF)),
        [pltpu.VMEM((2, R, columns), BF), dma((2,))],
        "aaa",
        "vv",
        1 << 26,
        16,
    )(grad_gate, grad_up, other)
    sums, left = call(
        products_kernel,
        (shape((packed_rows, 128), BF), shape((R, 128), BF)),
        [pltpu.VMEM((512, 128), F32)],
        "vvv",
        "vv",
        1 << 26,
        16,
    )(basis, turned, packed)
    parts = exchange(sums.reshape(near, 16 * far, 128), NEAR)
    halfway = call(halfway_kernel, shape((16 * far, 128), BF), [], "v", "v", 1 << 20, 8)(parts)
    parts = exchange(halfway.reshape(far, 16, 128), FAR)
    block, kept = call(
        total_kernel,
        (shape((far, 16, 128), BF), shape((48, 128), F32)),
        [],
        "vv",
        "vv",
        1 << 20,
        4,
    )(parts, left)
    kept_other = lax.ppermute(kept, "outer", swap)
    own = gather(block)
    theirs = lax.ppermute(own, "outer", swap)
    outs = call(
        functools.partial(last_kernel, sizes),
        (
            shape((R, W), F32), shape((R, W), F32), shape((R, R), F32), shape((R, R), F32),
            shape(grad_gate.shape, BF), shape(grad_gate.shape, BF),
        ),
        [
            pltpu.VMEM((2, R, columns), BF), pltpu.VMEM((2, R, columns), BF),
            pltpu.VMEM((2, 512, 128), F32), dma((2,)), dma((2,)),
        ],
        "vvvvaa",
        "vvvvaa",
        1 << 27,
        16,
    )(own, theirs, kept, kept_other, grad_gate, grad_up)
    return tuple(outs)


def solution(mesh):
    rows = mesh.shape["row"]
    sizes = (4, 2, 4, 2, 4) if rows == 256 else (2, 2, 2, 2, rows // 16)
    finer = Mesh(mesh.devices.reshape(mesh.shape["outer"], *sizes), ("outer", *ROW))
    return jax.shard_map(
        local,
        mesh=finer,
        in_specs=(P("outer", ROW, None), P("outer", ROW, None), P(None, ROW), P(None, ROW)),
        out_specs=(
            P(None, ROW), P(None, ROW), P(ROW, None), P(ROW, None),
            P("outer", ROW, None), P("outer", ROW, None),
        ),
        check_vma=False,
    )
```

time: 462 us -> 148 us (0.32)
  waiting for transfers between devices: 340 us -> 3.61 us
  blocking collectives: 66.2 us -> 93 us
  matrix products: 21.8 us -> 0 us
  Pallas kernels: 0 us -> 20.5 us
  starting transfers between devices: 0.08 us -> 17.9 us
  other arithmetic: 14.1 us -> 0 us
  between operations: 14.1 us -> 0.73 us
  local copies, waits for them, and re-layouts: 4.98 us -> 11.9 us
    psum x1 -> x0, waiting for transfers between devices: 208 us -> none  [local(): totals = lax.psum((products[0], products[1]), OUTER_ROW)]
    all_gather x1 -> x0, waiting for transfers between devices: 132 us -> none  [gather_turned(): out = lax.all_gather(both, axis, axis=0, tiled=True)]
    all_to_all x1 -> x5, blocking collectives: 8.52 us -> 93 us  [exchange(): return lax.all_to_all(x, axes, 0, 0, tiled=True)]
    psum x3 -> x0, blocking collectives: 57.7 us -> none  [over_axes(): x = lax.psum(x, axis)]
    pallas_call x0 -> x6, Pallas kernels: none -> 20.5 us  [the longest x1 12.6 us: local(): call(functools.partial(last_kernel, sizes), (shape((R, W), F32), shape((R...]
    dot_general x8 -> x0, matrix products: 16.6 us -> none  [the longest x2 7.48 us: contract_cols(): lax.dot_general(left, right, (((1,), (1,)), ((), ())), preferred_element_...]
    another operation x10 -> x0, other arithmetic: 13.4 us -> none  [the longest x4 6.17 us: forward_solve(): jax.scipy.linalg.solve_triangular(lower_matrix, right_hand, lower=True)]
    ppermute x0 -> x3, starting transfers between devices: none -> 12.7 us  [the longest x1 6.56 us: local(): theirs = lax.ppermute(own, 'outer', swap)]
  transfers between devices with their start and end apart: 2 -> 4, of which waited for: 2 -> 3; matrix products, arithmetic and copies ran while one was open for 3% -> 0% of each run, Pallas kernels for 0% -> 4%
where the time goes in v1:
time: 148 us
  blocking collectives  93 us (63%)
  Pallas kernels  20.5 us (14%)
  starting transfers between devices  17.9 us (12%)
  local copies, waits for them, and re-layouts  11.9 us (8%)
  waiting for transfers between devices  3.61 us (2%)
    all_to_all x5, blocking collectives, exchange(): return lax.all_to_all(x, axes, 0, 0, tiled=True)  93 us
    pallas_call x1, Pallas kernels, local(): call(functools.partial(last_kernel, sizes), (shape((R, W), F32), shape((R...  12.6 us
    unnamed x22, local copies, waits for them, and re-layouts  10.5 us
    ppermute x1, starting transfers between devices, local(): theirs = lax.ppermute(own, 'outer', swap)  6.56 us
    pallas_call x1, Pallas kernels, local(): call(functools.partial(pack_kernel, sizes), (shape((packed_rows, 256), BF...  5.58 us
    all_to_all x1, starting transfers between devices, exchange(): return lax.all_to_all(x, axes, 0, 0, tiled=True)  5.18 us
    ppermute x1, starting transfers between devices, local(): other = lax.ppermute(send, 'outer', swap)  4.25 us
  transfers between devices with their start and end apart: 4, of which 3 were waited for; matrix products, arithmetic and copies ran while one was open for 0% of the time, Pallas kernels for 4%

profile of v1, /device:TPU:1, one launch (start us, length us, event | category | flops | bytes accessed | tf_op | source)
XLA Modules:
  0.0 147.6 jit_solution(9091215302533292628)
XLA Ops:
  0.6 0.0 copy-start
  0.6 1.2 copy-done
  1.8 1.2 copy-done.2
  3.0 0.7 copy-done.8
  3.7 0.7 copy-done.9
  4.4 0.4 shard_map.91
  4.8 0.0 copy-start.10
  4.8 0.9 copy-done.10
  5.7 27.5 %all_to_all.30 = bf16[16,16,128]{2,1,0:T(8,128)(2,1)S(1)} all-to-all(bf16[16,16,128]{2,1,0:T(8,128)(2,1)S(1)} %get-tuple-element.14), channel_id=1, replica_groups=mesh['outer'=2,'yq'=4,'yp'=2,'zq'=4,'zp'=2,'x'=4] {'yq','zq'}, dimensions={0} | all-to-all | bytes 131072 | tf_op jit(solution)/shard_map/all_to_all | solution.py:302
  33.2 1.2 broadcast_in_dim.15
  34.4 5.2 %all-to-all-start.1 = ((bf16[16,256,128]{2,1,0:T(8,128)(2,1)}), bf16[16,256,128]{2,1,0:T(8,128)(2,1)S(1)}, u32[]{:S(2)}, u32[]{:S(2)}) async-start(bf16[16,256,128]{2,1,0:T(8,128)(2,1)} %broadcast_in_dim.15), calls=%async_computation.1 | async-start | bytes 2097152 | tf_op jit(solution)/shard_map/all_to_all | solution.py:302
  39.5 4.2 %collective-permute-start = (bf16[32,14336]{1,0:T(8,128)(2,1)}, bf16[32,14336]{1,0:T(8,128)(2,1)S(1)}, u32[]{:S(2)}, u32[]{:S(2)}) collective-permute-start(bf16[32,14336]{1,0:T(8,128)(2,1)} %copy-done.10), channel_id=1, source_target_pairs={{0,256},{256,0},{1,257},{257,1},{2,258},{258,2},{3,259},{259,3},{4... | collective-permute-start | bytes 2752520 | tf_op jit(solution)/shard_map/ppermute | solution.py:318
  43.8 2.3 %collective-permute-done.other_ref = bf16[32,14336]{1,0:T(8,128)(2,1)S(1)} collective-permute-done((bf16[32,14336]{1,0:T(8,128)(2,1)}, bf16[32,14336]{1,0:T(8,128)(2,1)S(1)}, u32[]{:S(2)}, u32[]{:S(2)}) %collective-permute-start) | collective-permute-done | bytes 917536 | tf_op jit(solution)/shard_map/ppermute | solution.py:318
  46.1 0.0 copy-done.1
  46.1 5.6 %shard_map.92 = (bf16[4096,256]{1,0:T(8,128)(2,1)S(1)}, bf16[256,4096]{1,0:T(8,128)(2,1)S(1)}) custom-call(bf16[1,32,14336]{2,1,0:T(8,128)(2,1)S(1)} %copy-done.1, bf16[1,32,14336]{2,1,0:T(8,128)(2,1)S(1)} %copy-done.3, bf16[32,14336]{1,0:T(8,128)(2,1)S(1)} %collective-permute-done.other_ref), custom_call_target="tpu_custom_call" | custom-call | flops 67108864 | bytes 4194304 | tf_op jit(solution)/shard_map/pallas_call | solution.py:320
  51.7 1.3 copy-done.4
  53.0 1.3 copy-done.6
  54.3 0.2 all-to-all-done.1
  54.5 1.6 %copy-done.5 = bf16[4096,256]{1,0:T(8,128)(2,1)S(1)} copy-done((bf16[4096,256]{1,0:T(8,128)(2,1)S(1)}, bf16[4096,256]{1,0:T(8,128)(2,1)}, u32[]{:S(2)}) %copy-start.5) | copy-done | bytes 2097176
  56.1 1.6 %copy-done.7 = bf16[256,4096]{1,0:T(8,128)(2,1)S(1)} copy-done((bf16[256,4096]{1,0:T(8,128)(2,1)S(1)}, bf16[256,4096]{1,0:T(8,128)(2,1)}, u32[]{:S(2)}) %copy-start.7) | copy-done | bytes 2097176
  57.7 1.6 %shard_map.93 = (bf16[4096,128]{1,0:T(8,128)(2,1)S(1)}, bf16[32,128]{1,0:T(8,128)(2,1)S(1)}) custom-call(bf16[4096,128]{1,0:T(8,128)(2,1)S(1)} %bitcast.6, bf16[256,4096]{1,0:T(8,128)(2,1)S(1)} %copy-done.7, bf16[4096,256]{1,0:T(8,128)(2,1)S(1)} %copy-done.5), custom_call_target="tpu_custom_call" | custom-call | flops 67108864 | bytes 4194304 | tf_op jit(solution)/shard_map/pallas_call | solution.py:329
  59.3 22.1 %all_to_all.31.parts_ref = bf16[16,256,128]{2,1,0:T(8,128)(2,1)S(1)} all-to-all(bf16[16,256,128]{2,1,0:T(8,128)(2,1)S(1)} %bitcast.9), channel_id=1, replica_groups=mesh['outer'=2,'yq'=4,'yp'=2,'zq'=4,'zp'=2,'x'=4] {'yp','zp','x'}, dimensions={0} | all-to-all | bytes 2097152 | tf_op jit(solution)/shard_map/all_to_all | solution.py:302
  81.4 0.3 shard_map.94
  81.6 13.9 %all_to_all.32.parts_ref = bf16[16,16,128]{2,1,0:T(8,128)(2,1)S(1)} all-to-all(bf16[16,16,128]{2,1,0:T(8,128)(2,1)S(1)} %bitcast.10), channel_id=1, replica_groups=mesh['outer'=2,'yq'=4,'yp'=2,'zq'=4,'zp'=2,'x'=4] {'yq','zq'}, dimensions={0} | all-to-all | bytes 131072 | tf_op jit(solution)/shard_map/all_to_all | solution.py:302
  95.6 13.9 %all_to_all.33 = bf16[16,16,128]{2,1,0:T(8,128)(2,1)S(1)} all-to-all(bf16[16,16,128]{2,1,0:T(8,128)(2,1)S(1)} %get-tuple-element.20), channel_id=1, replica_groups=mesh['outer'=2,'yq'=4,'yp'=2,'zq'=4,'zp'=2,'x'=4] {'yq','zq'}, dimensions={0} | all-to-all | bytes 131072 | tf_op jit(solution)/shard_map/all_to_all | solution.py:302
  109.5 0.2 broadcast_in_dim.17
  109.7 15.7 %all_to_all.34 = bf16[16,256,128]{2,1,0:T(8,128)(2,1)S(1)} all-to-all(bf16[16,256,128]{2,1,0:T(8,128)(2,1)S(1)} %broadcast_in_dim.17), channel_id=1, replica_groups=mesh['outer'=2,'yq'=4,'yp'=2,'zq'=4,'zp'=2,'x'=4] {'yp','zp','x'}, dimensions={0} | all-to-all | bytes 2097152 | tf_op jit(solution)/shard_map/all_to_all | solution.py:302
  125.4 6.6 %collective-permute-start.1 = (bf16[4096,128]{1,0:T(8,128)(2,1)S(1)}, bf16[4096,128]{1,0:T(8,128)(2,1)S(1)}, u32[]{:S(2)}, u32[]{:S(2)}) collective-permute-start(bf16[4096,128]{1,0:T(8,128)(2,1)S(1)} %bitcast.7), channel_id=1, source_target_pairs={{0,256},{256,0},{1,257},{257,1},{2,258},{258,2},{3,259},{259,3},{4... | collective-permute-start | bytes 3145736 | tf_op jit(solution)/shard_map/ppermute | solution.py:352
  132.0 1.9 %collective-permute-start.2 = (f32[48,128]{1,0:T(8,128)S(1)}, f32[48,128]{1,0:T(8,128)S(1)}, u32[]{:S(2)}, u32[]{:S(2)}) collective-permute-start(f32[48,128]{1,0:T(8,128)S(1)} %get-tuple-element.21.kept_ref), channel_id=1, source_target_pairs={{0,256},{256,0},{1,257},{257,1},{2,258},{258,2},{3,259},{259,3},{4... | collective-permute-start | bytes 73736 | tf_op jit(solution)/shard_map/ppermute | solution.py:350
  133.9 1.2 collective-permute-done.2.kept_other_ref
  135.0 0.0 collective-permute-done.1.other_ref
  135.1 12.6 %shard_map.96 = (f32[32,56]{1,0:T(8,128)}, f32[32,56]{1,0:T(8,128)}, f32[32,32]{1,0:T(8,128)}, f32[32,32]{1,0:T(8,128)}, bf16[1,32,14336]{2,1,0:T(8,128)(2,1)}, /*index=5*/bf16[1,32,14336]{2,1,0:T(8,128)(2,1)}) custom-call(bf16[4096,128]{1,0:T(8,128)(2,1)S(1)} %bitcast.8, bf16[4096,128]{1,0:T(8,128)(2,1)S(1)} %collective-permute-done.1.other_ref, ...), custom_call_target="tpu_custom_call" | custom-call | flops 134217728 | bytes 8388608 | tf_op jit(solution)/shard_map/pallas_call | solution.py:353
  (11 shorter events, 0.1 us)
Async XLA Ops:
  0.6 1.2 copy-start
  1.8 1.2 copy-start.2
  3.0 0.7 copy-start.8
  3.7 0.7 copy-start.9
  4.8 0.9 copy-start.10
  5.7 40.4 %copy-start.1 = (bf16[1,32,14336]{2,1,0:T(8,128)(2,1)S(1)}, bf16[1,32,14336]{2,1,0:T(8,128)(2,1)}, u32[]{:S(2)}) copy-start(bf16[1,32,14336]{2,1,0:T(8,128)(2,1)} %gg_ref.5) | copy-start | bytes 2752516
  5.7 40.4 %copy-start.3 = (bf16[1,32,14336]{2,1,0:T(8,128)(2,1)S(1)}, bf16[1,32,14336]{2,1,0:T(8,128)(2,1)}, u32[]{:S(2)}) copy-start(bf16[1,32,14336]{2,1,0:T(8,128)(2,1)} %gu_ref.5) | copy-start | bytes 2752516
  34.4 20.1 %all-to-all-start.1 = ((bf16[16,256,128]{2,1,0:T(8,128)(2,1)}), bf16[16,256,128]{2,1,0:T(8,128)(2,1)S(1)}, u32[]{:S(2)}, u32[]{:S(2)}) async-start(bf16[16,256,128]{2,1,0:T(8,128)(2,1)} %broadcast_in_dim.15), calls=%async_computation.1 | async-start | bytes 2097152 | tf_op jit(solution)/shard_map/all_to_all | solution.py:302
  39.5 6.5 %collective-permute-start = (bf16[32,14336]{1,0:T(8,128)(2,1)}, bf16[32,14336]{1,0:T(8,128)(2,1)S(1)}, u32[]{:S(2)}, u32[]{:S(2)}) collective-permute-start(bf16[32,14336]{1,0:T(8,128)(2,1)} %copy-done.10), channel_id=1, source_target_pairs={{0,256},{256,0},{1,257},{257,1},{2,258},{258,2},{3,259},{259,3},{4... | collective-permute-start | bytes 2752520 | tf_op jit(solution)/shard_map/ppermute | solution.py:318
  51.7 1.3 copy-start.4
  53.0 1.3 copy-start.6
  54.5 1.6 %copy-start.5 = (bf16[4096,256]{1,0:T(8,128)(2,1)S(1)}, bf16[4096,256]{1,0:T(8,128)(2,1)}, u32[]{:S(2)}) copy-start(bf16[4096,256]{1,0:T(8,128)(2,1)} %copy-done.4) | copy-start | bytes 6291460
  56.1 1.6 %copy-start.7 = (bf16[256,4096]{1,0:T(8,128)(2,1)S(1)}, bf16[256,4096]{1,0:T(8,128)(2,1)}, u32[]{:S(2)}) copy-start(bf16[256,4096]{1,0:T(8,128)(2,1)} %copy-done.6) | copy-start | bytes 6291460
  125.4 9.7 %collective-permute-start.1 = (bf16[4096,128]{1,0:T(8,128)(2,1)S(1)}, bf16[4096,128]{1,0:T(8,128)(2,1)S(1)}, u32[]{:S(2)}, u32[]{:S(2)}) collective-permute-start(bf16[4096,128]{1,0:T(8,128)(2,1)S(1)} %bitcast.7), channel_id=1, source_target_pairs={{0,256},{256,0},{1,257},{257,1},{2,258},{258,2},{3,259},{259,3},{4... | collective-permute-start | bytes 3145736 | tf_op jit(solution)/shard_map/ppermute | solution.py:352
  132.0 3.1 %collective-permute-start.2 = (f32[48,128]{1,0:T(8,128)S(1)}, f32[48,128]{1,0:T(8,128)S(1)}, u32[]{:S(2)}, u32[]{:S(2)}) collective-permute-start(f32[48,128]{1,0:T(8,128)S(1)} %get-tuple-element.21.kept_ref), channel_id=1, source_target_pairs={{0,256},{256,0},{1,257},{257,1},{2,258},{258,2},{3,259},{259,3},{4... | collective-permute-start | bytes 73736 | tf_op jit(solution)/shard_map/ppermute | solution.py:350

commit v2 on v1

--- a/solution.py
+++ b/solution.py
@@ -15,6 +15,7 @@
 F32 = jnp.float32
 R = 32
 W = 56
+BLOCK = 4
 TILE = 8
 PERIOD = 16 * W
 INTERPRET = False
@@ -47,19 +48,21 @@
     )
 
 
-def prepare_kernel(bg_ref, bu_ref, gg_ref, gu_ref, block_ref, send_ref, sem):
+def prepare_kernel(bg_ref, bu_ref, gg_ref, gu_ref, block_ref, send_ref, basis, sem):
     core = lax.axis_index("outer")
 
     @pl.when(core == 0)
     def _():
-        pltpu.make_async_copy(gu_ref.at[0], send_ref, sem).start()
+        pltpu.make_async_copy(bg_ref, basis, sem.at[0]).start()
+        pltpu.make_async_copy(gu_ref.at[0], send_ref, sem.at[1]).start()
 
     @pl.when(core != 0)
     def _():
-        pltpu.make_async_copy(gg_ref.at[0], send_ref, sem).start()
-
-    mine = jnp.where(core == 0, bg_ref[...].astype(F32), bu_ref[...].astype(F32))
-    turned = mine.T
+        pltpu.make_async_copy(bu_ref, basis, sem.at[0]).start()
+        pltpu.make_async_copy(gg_ref.at[0], send_ref, sem.at[1]).start()
+
+    pltpu.make_async_copy(bg_ref, basis, sem.at[0]).wait()
+    turned = basis[...].astype(F32).T
     empty = jnp.zeros((TILE, R), F32)
     rows = []
     for h in range(2):
@@ -67,31 +70,28 @@
         rows.append(jnp.concatenate(tiles, axis=1))
     block = jnp.concatenate(rows, axis=0).astype(BF)
     block_ref[...] = jnp.broadcast_to(block[None], block_ref.shape)
-    pltpu.make_async_copy(gg_ref.at[0], send_ref, sem).wait()
-
-
-def pack_kernel(sizes, gg_ref, gu_ref, other_ref, packed_ref, turned_ref, both, sem):
+    pltpu.make_async_copy(gg_ref.at[0], send_ref, sem.at[1]).wait()
+
+
+def pack_kernel(sizes, gg_ref, gu_ref, other_ref, packed_ref, turned_ref, own, work, sem):
     core = lax.axis_index("outer")
 
     @pl.when(core == 0)
     def _():
-        pltpu.make_async_copy(gg_ref.at[0], both.at[0], sem.at[0]).start()
+        pltpu.make_async_copy(gg_ref.at[0], own, sem.at[0]).start()
 
     @pl.when(core != 0)
     def _():
-        pltpu.make_async_copy(gu_ref.at[0], both.at[0], sem.at[0]).start()
-
-    second = pltpu.make_async_copy(other_ref, both.at[1], sem.at[1])
-    second.start()
-    pltpu.make_async_copy(gg_ref.at[0], both.at[0], sem.at[0]).wait()
-    second.wait()
+        pltpu.make_async_copy(gu_ref.at[0], own, sem.at[0]).start()
+
+    pltpu.make_async_copy(gg_ref.at[0], own, sem.at[0]).wait()
     empty = jnp.zeros((TILE, 2 * R), F32)
 
     @pl.loop(0, packed_ref.shape[0] // 256)
     def _(k):
         columns = pl.ds(pl.multiple_of(k * PERIOD, 128), PERIOD)
         x = jnp.concatenate(
-            [both.at[0][:, columns].astype(F32), both.at[1][:, columns].astype(F32)], axis=0
+            [own[:, columns].astype(F32), other_ref[:, columns].astype(F32)], axis=0
         )
         xt = x.T
         first = place(16 * k, sizes)
@@ -104,15 +104,26 @@
                     tiles.append(xt[at : at + 8] if t < 7 else empty)
                 rows.append(jnp.concatenate(tiles, axis=1))
             to = pl.multiple_of(16 * (first + place(d, sizes)), 16)
-            packed_ref[pl.ds(to, 16), :] = jnp.concatenate(rows, axis=0).astype(BF)
+            work[pl.ds(to, 16), :] = jnp.concatenate(rows, axis=0).astype(BF)
+
+    keep = pltpu.make_async_copy(work, packed_ref, sem.at[1])
+    keep.start()
 
     @pl.loop(0, packed_ref.shape[0] // 256)
     def _(k):
         part = pl.ds(pl.multiple_of(k * 256, 256), 256)
-        turned_ref[:, part] = packed_ref[part, :].astype(F32).T.astype(BF)
-
-
-def products_kernel(basis_ref, turned_ref, packed_ref, sums_ref, left_ref, extra):
+        turned_ref[:, part] = work[part, :].astype(F32).T.astype(BF)
+
+    keep.wait()
+
+
+def products_kernel(basis_ref, turned_ref, packed_ref, sums_ref, left_ref, extra, packed, sem):
+    step = 512
+    loads = []
+    for k in range(packed_ref.shape[0] // step):
+        part = pl.ds(k * step, step)
+        loads.append(pltpu.make_async_copy(packed_ref.at[part], packed.at[part], sem.at[k]))
+        loads[-1].start()
     partial = dot(turned_ref[...], basis_ref[...], 1, 0)
     group = groups((R, 128))
     total = jnp.zeros((R, 128), F32)
@@ -134,9 +145,9 @@
     extra[...] = jnp.zeros_like(extra)
     for s, term in enumerate(three_terms(gram)):
         extra[pl.ds(8 + s, R, stride=16), :] = term
-    step = 512
-    for k in range(packed_ref.shape[0] // step):
-        out = dot(packed_ref[pl.ds(k * step, step), :], spread, 1, 0)
+    for k, load in enumerate(loads):
+        load.wait()
+        out = dot(packed[pl.ds(k * step, step), :], spread, 1, 0)
         if k == 0:
             out = out + extra[...]
         sums_ref[pl.ds(k * step, step), :] = out.astype(BF)
@@ -195,16 +206,26 @@
         grams.append(pltpu.roll(gram, 32 if j == 0 else 96, 1))
     m = jnp.where(group == 0, grams[0], jnp.where(group == 2, grams[1], 0.0))
     m = jnp.where((group % 2 == 1) & (row == lane % R), 1.0, m)
-    scale = jnp.zeros((R, 128), F32)
-    for k in range(R):
-        pivot_row = m[k : k + 1]
-        first = jnp.broadcast_to(m[:, k : k + 1], (R, 128))
-        second = jnp.broadcast_to(m[:, 64 + k : 65 + k], (R, 128))
-        column = jnp.where(lane < 64, first, second)
-        pivot = column[k : k + 1]
-        scale = jnp.where(row == k, lax.rsqrt(pivot), scale)
-        if k < R - 1:
-            m = m - jnp.where(row > k, column / pivot, 0.0) * pivot_row
+    pivots = jnp.ones((R, 128), F32)
+    for first in range(0, R, BLOCK):
+        columns = []
+        for k in range(first, first + BLOCK):
+            left = jnp.broadcast_to(m[:, k : k + 1], (R, 128))
+            right = jnp.broadcast_to(m[:, 64 + k : 65 + k], (R, 128))
+            columns.append(jnp.where(lane < 64, left, right))
+        rows = [m[k : k + 1] for k in range(first, first + BLOCK)]
+        for i in range(BLOCK):
+            k = first + i
+            pivot = columns[i][k : k + 1]
+            pivots = jnp.where(row == k, pivot, pivots)
+            factor = jnp.where(row > k, columns[i] * (1.0 / pivot), 0.0)
+            for j in range(i + 1, BLOCK):
+                columns[j] = columns[j] - factor * columns[j][k : k + 1]
+                at = first + j
+                rows[j] = rows[j] - factor[at : at + 1] * rows[i]
+            m = m - factor * rows[i]
+    scale = lax.rsqrt(pivots)
+    scale = scale * (1.5 - 0.5 * pivots * scale * scale)
     inverse = m * scale
     kept = (kept_ref[...], kept_other_ref[...])
     nexts, factors, sides = [], [], []
@@ -233,57 +254,88 @@
     fu_ref[...] = jnp.where(swap, factors[0], factors[1])
     for load in loads:
         load.wait()
-    tile_group = groups((8, 128))
+    pair_group = groups((16, 128))
+    second = lax.broadcasted_iota(jnp.int32, (16, 128), 0) >= 8
+    masks = []
+    for v in range(7):
+        a, b = (2 * v) % 7, (2 * v + 1) % 7
+        masks.append(jnp.where(pair_group == jnp.where(second, b % 4, a % 4), 1.0, 0.0).astype(BF))
+    outs = (rg_ref, ru_ref)
+    steps = own_ref.shape[0] // 256
+    cuts = 2
     stores = [
-        pltpu.make_async_copy(resid.at[k], ref.at[0], sem_out.at[k])
-        for k, ref in enumerate((rg_ref, ru_ref))
+        [
+            pltpu.make_async_copy(
+                resid.at[k, :, pl.ds(c * steps // cuts * PERIOD, steps // cuts * PERIOD)],
+                ref.at[0, :, pl.ds(c * steps // cuts * PERIOD, steps // cuts * PERIOD)],
+                sem_out.at[k, c],
+            )
+            for c in range(cuts)
+        ]
+        for k, ref in enumerate(outs)
     ]
     for j, ref in enumerate((own_ref, other_ref)):
         at = core if j == 0 else 1 - core
         side = sides[j]
-
-        @pl.loop(0, ref.shape[0] // 256)
-        def _(k):
-            first = place(16 * k, sizes)
-            rows = []
-            for d in range(16):
-                at_d = pl.multiple_of(16 * (first + place(d, sizes)), 16)
-                x = ref[pl.ds(at_d, 16), :].astype(F32)
-                for t in range(7):
-                    h, q = divmod(t, 4)
-                    tile = x[8 * h : 8 * h + 8]
-                    rows.append(jnp.where(tile_group == q, tile, 0.0))
-            right = jnp.concatenate(rows, axis=0).astype(BF)
-            both = dot(side, right, 1, 1)
-            columns = pl.ds(pl.multiple_of(k * PERIOD, 128), PERIOD)
-            value = grads.at[at][:, columns].astype(F32) - (both[0:R] + both[R : 2 * R])
-            resid.at[at][:, columns] = value.astype(BF)
-
-        @pl.when(at == 0)
-        def _():
-            stores[0].start()
-
-        @pl.when(at != 0)
-        def _():
-            stores[1].start()
-
-    for store in stores:
-        store.wait()
+        for cut in range(cuts):
+
+            @pl.loop(cut * steps // cuts, (cut + 1) * steps // cuts)
+            def _(k):
+                first = place(16 * k, sizes)
+                tiles = []
+                for d in range(16):
+                    at_d = pl.multiple_of(16 * (first + place(d, sizes)), 16)
+                    x = ref[pl.ds(at_d, 16), :]
+                    tiles += [x[0:8]] * 4 + [x[8:16]] * 3
+                rows = []
+                for v in range(56):
+                    pair = jnp.concatenate(tiles[2 * v : 2 * v + 2], axis=0)
+                    rows.append(pair * masks[v % 7])
+                right = jnp.concatenate(rows, axis=0)
+                both = dot(side, right, 1, 1)
+                columns = pl.ds(pl.multiple_of(k * PERIOD, 128), PERIOD)
+                value = grads.at[at][:, columns].astype(F32) - (both[0:R] + both[R : 2 * R])
+                resid.at[at][:, columns] = value.astype(BF)
+
+            @pl.when(at == 0)
+            def _():
+                stores[0][cut].start()
+
+            @pl.when(at != 0)
+            def _():
+                stores[1][cut].start()
+
+    for line in stores:
+        for store in line:
+            store.wait()
 
 
 def call(kernel, outs, scratch, spaces_in, spaces_out, cost, limit):
-    any_space, vmem = pl.BlockSpec(memory_space=pl.ANY), pl.BlockSpec(memory_space=pltpu.VMEM)
-    pick = lambda s: any_space if s == "a" else vmem
-    return pl.pallas_call(
+    space = {"h": pltpu.HBM, "v": pltpu.VMEM}
+    specs_out = tuple(pl.BlockSpec(memory_space=space[s]) for s in spaces_out)
+    run = pl.pallas_call(
         kernel,
-        out_shape=outs,
-        in_specs=[pick(s) for s in spaces_in],
-        out_specs=tuple(pick(s) for s in spaces_out) if len(spaces_out) > 1 else pick(spaces_out),
+        out_shape=[
+            pltpu.HBM(o.shape, o.dtype) if s == "h" and not INTERPRET else o
+            for s, o in zip(spaces_out, outs)
+        ],
+        in_specs=[pl.BlockSpec(memory_space=space[s]) for s in spaces_in],
+        out_specs=specs_out,
         scratch_shapes=scratch,
         cost_estimate=pl.CostEstimate(flops=cost, bytes_accessed=cost // 16, transcendentals=0),
         compiler_params=pltpu.CompilerParams(vmem_limit_bytes=limit << 20),
         interpret=INTERPRET,
     )
+
+    def pinned(*args):
+        return run(
+            *(
+                pltpu.with_memory_space_constraint(x, pltpu.HBM) if s == "h" and not INTERPRET else x
+                for s, x in zip(spaces_in, args)
+            )
+        )
+
+    return pinned
 
 
 def shape(dims, dtype):
@@ -309,8 +361,8 @@
     block, send = call(
         prepare_kernel,
         (shape((far, 16, 128), BF), shape((R, columns), BF)),
-        [dma],
-        "vvaa",
+        [pltpu.VMEM((R, W), BF), dma((2,))],
+        "hhhh",
         "vv",
         1 << 20,
         6,
@@ -320,23 +372,26 @@
     packed, turned = call(
         functools.partial(pack_kernel, sizes),
         (shape((packed_rows, 256), BF), shape((256, packed_rows), BF)),
-        [pltpu.VMEM((2, R, columns), BF), dma((2,))],
-        "aaa",
-        "vv",
+        [pltpu.VMEM((R, columns), BF), pltpu.VMEM((packed_rows, 256), BF), dma((2,))],
+        "hhv",
+        "hv",
         1 << 26,
         16,
     )(grad_gate, grad_up, other)
     sums, left = call(
         products_kernel,
         (shape((packed_rows, 128), BF), shape((R, 128), BF)),
-        [pltpu.VMEM((512, 128), F32)],
-        "vvv",
+        [
+            pltpu.VMEM((512, 128), F32), pltpu.VMEM((packed_rows, 256), BF),
+            dma((packed_rows // 512,)),
+        ],
+        "vvh",
         "vv",
         1 << 26,
         16,
     )(basis, turned, packed)
     parts = exchange(sums.reshape(near, 16 * far, 128), NEAR)
-    halfway = call(halfway_kernel, shape((16 * far, 128), BF), [], "v", "v", 1 << 20, 8)(parts)
+    (halfway,) = call(halfway_kernel, (shape((16 * far, 128), BF),), [], "v", "v", 1 << 20, 8)(parts)
     parts = exchange(halfway.reshape(far, 16, 128), FAR)
     block, kept = call(
         total_kernel,
@@ -358,10 +413,10 @@
         ),
         [
             pltpu.VMEM((2, R, columns), BF), pltpu.VMEM((2, R, columns), BF),
-            pltpu.VMEM((2, 512, 128), F32), dma((2,)), dma((2,)),
+            pltpu.VMEM((2, 512, 128), F32), dma((2,)), dma((2, 2)),
         ],
-        "vvvvaa",
-        "vvvvaa",
+        "vvvvhh",
+        "vvvvhh",
         1 << 27,
         16,
     )(own, theirs, kept, kept_other, grad_gate, grad_up)

time: 148 us -> 138 us (0.932)
  local copies, waits for them, and re-layouts: 11.9 us -> 1.38 us
  blocking collectives: 93 us -> 88 us
  Pallas kernels: 20.5 us -> 22.8 us
  waiting for transfers between devices: 3.61 us -> 5.55 us
  starting transfers between devices: 17.9 us -> 19.4 us
    unnamed x22 -> x0, local copies, waits for them, and re-layouts: 10.5 us -> none
    all_to_all x5, blocking collectives: 93 us -> 88 us  [exchange(): return lax.all_to_all(x, axes, 0, 0, tiled=True)]
    pallas_call x6, Pallas kernels: 20.5 us -> 22.8 us  [pinned(): run(*(pltpu.with_memory_space_constraint(x, pltpu.HBM) if s == 'h' and (n...]
    all_to_all x1, waiting for transfers between devices: 0.16 us -> 2.31 us  [exchange(): return lax.all_to_all(x, axes, 0, 0, tiled=True)]
    ppermute x1, starting transfers between devices: 6.56 us -> 8.1 us  [local(): theirs = lax.ppermute(own, 'outer', swap)]
  transfers between devices with their start and end apart: 4 -> 4, of which waited for: 3 -> 3; matrix products, arithmetic and copies ran while one was open for 0% -> 0% of each run, Pallas kernels for 4% -> 5%
where the time goes in v2:
time: 138 us
  blocking collectives  88 us (64%)
  Pallas kernels  22.8 us (17%)
  starting transfers between devices  19.4 us (14%)
  waiting for transfers between devices  5.55 us (4%)
    all_to_all x5, blocking collectives, exchange(): return lax.all_to_all(x, axes, 0, 0, tiled=True)  88 us
    pallas_call x6, Pallas kernels, pinned(): run(*(pltpu.with_memory_space_constraint(x, pltpu.HBM) if s == 'h' and (n...  22.8 us
    ppermute x1, starting transfers between devices, local(): theirs = lax.ppermute(own, 'outer', swap)  8.1 us
    all_to_all x1, starting transfers between devices, exchange(): return lax.all_to_all(x, axes, 0, 0, tiled=True)  5.18 us
    ppermute x1, starting transfers between devices, local(): other = lax.ppermute(send, 'outer', swap)  4.24 us
  transfers between devices with their start and end apart: 4, of which 3 were waited for; matrix products, arithmetic and copies ran while one was open for 0% of the time, Pallas kernels for 5%

profile of v2, /device:TPU:1, one launch (start us, length us, event | category | flops | bytes accessed | tf_op | source)
XLA Modules:
  0.0 137.9 jit_solution(8291827195314745980)
XLA Ops:
  0.6 1.2 shard_map.91
  1.9 27.3 %all_to_all.30 = bf16[16,16,128]{2,1,0:T(8,128)(2,1)S(1)} all-to-all(bf16[16,16,128]{2,1,0:T(8,128)(2,1)S(1)} %get-tuple-element.14), channel_id=1, replica_groups=mesh['outer'=2,'yq'=4,'yp'=2,'zq'=4,'zp'=2,'x'=4] {'yq','zq'}, dimensions={0} | all-to-all | bytes 131072 | tf_op jit(solution)/shard_map/all_to_all | solution.py:354
  29.2 1.2 broadcast_in_dim.15
  30.4 5.2 %all-to-all-start.1 = ((bf16[16,256,128]{2,1,0:T(8,128)(2,1)}), bf16[16,256,128]{2,1,0:T(8,128)(2,1)S(1)}, u32[]{:S(2)}, u32[]{:S(2)}) async-start(bf16[16,256,128]{2,1,0:T(8,128)(2,1)} %broadcast_in_dim.15), calls=%async_computation.1 | async-start | bytes 2097152 | tf_op jit(solution)/shard_map/all_to_all | solution.py:354
  35.6 4.2 %collective-permute-start = (bf16[32,14336]{1,0:T(8,128)(2,1)S(1)}, bf16[32,14336]{1,0:T(8,128)(2,1)S(1)}, u32[]{:S(2)}, u32[]{:S(2)}) collective-permute-start(bf16[32,14336]{1,0:T(8,128)(2,1)S(1)} %get-tuple-element.15), channel_id=1, source_target_pairs={{0,256},{256,0},{1,257},{257,1},{2,258},{258,2},{3,259},{259,3},{4... | collective-permute-start | bytes 2752520 | tf_op jit(solution)/shard_map/ppermute | solution.py:370
  39.8 2.1 %collective-permute-done.other_ref = bf16[32,14336]{1,0:T(8,128)(2,1)S(1)} collective-permute-done((bf16[32,14336]{1,0:T(8,128)(2,1)S(1)}, bf16[32,14336]{1,0:T(8,128)(2,1)S(1)}, u32[]{:S(2)}, u32[]{:S(2)}) %collective-permute-start) | collective-permute-done | bytes 917536 | tf_op jit(solution)/shard_map/ppermute | solution.py:370
  41.9 6.3 %shard_map.92 = (bf16[4096,256]{1,0:T(8,128)(2,1)}, bf16[256,4096]{1,0:T(8,128)(2,1)S(1)}) custom-call(bf16[1,32,14336]{2,1,0:T(8,128)(2,1)} %gg_ref.5, bf16[1,32,14336]{2,1,0:T(8,128)(2,1)} %gu_ref.5, bf16[32,14336]{1,0:T(8,128)(2,1)S(1)} %collective-permute-done.other_ref), custom_call_target="tpu_custom_call" | custom-call | flops 67108864 | bytes 4194304 | tf_op jit(solution)/shard_map/pallas_call | solution.py:331
  48.2 2.3 %all-to-all-done.1 = bf16[16,256,128]{2,1,0:T(8,128)(2,1)S(1)} async-done(((bf16[16,256,128]{2,1,0:T(8,128)(2,1)}), bf16[16,256,128]{2,1,0:T(8,128)(2,1)S(1)}, u32[]{:S(2)}, u32[]{:S(2)}) %all-to-all-start.1) | async-done | bytes 1048608 | tf_op jit(solution)/shard_map/all_to_all | solution.py:354
  50.5 4.1 %shard_map.93 = (bf16[4096,128]{1,0:T(8,128)(2,1)S(1)}, bf16[32,128]{1,0:T(8,128)(2,1)S(1)}) custom-call(bf16[4096,128]{1,0:T(8,128)(2,1)S(1)} %bitcast.6, bf16[256,4096]{1,0:T(8,128)(2,1)S(1)} %get-tuple-element.16.turned_ref, bf16[4096,256]{1,0:T(8,128)(2,1)} %get-tuple-element.17.packed_ref), custom_call_target="tpu_custom_call" | custom-call | flops 67108864 | bytes 4194304 | tf_op jit(solution)/shard_map/pallas_call | solution.py:331
  54.7 18.6 %all_to_all.31.parts_ref = bf16[16,256,128]{2,1,0:T(8,128)(2,1)S(1)} all-to-all(bf16[16,256,128]{2,1,0:T(8,128)(2,1)S(1)} %bitcast.9), channel_id=1, replica_groups=mesh['outer'=2,'yq'=4,'yp'=2,'zq'=4,'zp'=2,'x'=4] {'yp','zp','x'}, dimensions={0} | all-to-all | bytes 2097152 | tf_op jit(solution)/shard_map/all_to_all | solution.py:354
  73.3 0.3 shard_map.94
  73.6 13.9 %all_to_all.32.parts_ref = bf16[16,16,128]{2,1,0:T(8,128)(2,1)S(1)} all-to-all(bf16[16,16,128]{2,1,0:T(8,128)(2,1)S(1)} %bitcast.10), channel_id=1, replica_groups=mesh['outer'=2,'yq'=4,'yp'=2,'zq'=4,'zp'=2,'x'=4] {'yq','zq'}, dimensions={0} | all-to-all | bytes 131072 | tf_op jit(solution)/shard_map/all_to_all | solution.py:354
  87.5 13.9 %all_to_all.33 = bf16[16,16,128]{2,1,0:T(8,128)(2,1)S(1)} all-to-all(bf16[16,16,128]{2,1,0:T(8,128)(2,1)S(1)} %get-tuple-element.20), channel_id=1, replica_groups=mesh['outer'=2,'yq'=4,'yp'=2,'zq'=4,'zp'=2,'x'=4] {'yq','zq'}, dimensions={0} | all-to-all | bytes 131072 | tf_op jit(solution)/shard_map/all_to_all | solution.py:354
  101.4 0.2 broadcast_in_dim.17
  101.6 14.3 %all_to_all.34 = bf16[16,256,128]{2,1,0:T(8,128)(2,1)S(1)} all-to-all(bf16[16,256,128]{2,1,0:T(8,128)(2,1)S(1)} %broadcast_in_dim.17), channel_id=1, replica_groups=mesh['outer'=2,'yq'=4,'yp'=2,'zq'=4,'zp'=2,'x'=4] {'yp','zp','x'}, dimensions={0} | all-to-all | bytes 2097152 | tf_op jit(solution)/shard_map/all_to_all | solution.py:354
  115.9 8.1 %collective-permute-start.1 = (bf16[4096,128]{1,0:T(8,128)(2,1)S(1)}, bf16[4096,128]{1,0:T(8,128)(2,1)S(1)}, u32[]{:S(2)}, u32[]{:S(2)}) collective-permute-start(bf16[4096,128]{1,0:T(8,128)(2,1)S(1)} %bitcast.7), channel_id=1, source_target_pairs={{0,256},{256,0},{1,257},{257,1},{2,258},{258,2},{3,259},{259,3},{4... | collective-permute-start | bytes 3145736 | tf_op jit(solution)/shard_map/ppermute | solution.py:407
  124.0 1.9 %collective-permute-start.2 = (f32[48,128]{1,0:T(8,128)S(1)}, f32[48,128]{1,0:T(8,128)S(1)}, u32[]{:S(2)}, u32[]{:S(2)}) collective-permute-start(f32[48,128]{1,0:T(8,128)S(1)} %get-tuple-element.21.kept_ref), channel_id=1, source_target_pairs={{0,256},{256,0},{1,257},{257,1},{2,258},{258,2},{3,259},{259,3},{4... | collective-permute-start | bytes 73736 | tf_op jit(solution)/shard_map/ppermute | solution.py:405
  125.9 1.2 collective-permute-done.2.kept_other_ref
  127.1 0.0 collective-permute-done.1.other_ref
  127.1 10.8 %shard_map.96 = (f32[32,56]{1,0:T(8,128)}, f32[32,56]{1,0:T(8,128)}, f32[32,32]{1,0:T(8,128)}, f32[32,32]{1,0:T(8,128)}, bf16[1,32,14336]{2,1,0:T(8,128)(2,1)}, /*index=5*/bf16[1,32,14336]{2,1,0:T(8,128)(2,1)}) custom-call(bf16[4096,128]{1,0:T(8,128)(2,1)S(1)} %bitcast.8, bf16[4096,128]{1,0:T(8,128)(2,1)S(1)} %collective-permute-done.1.other_ref, ...), custom_call_target="tpu_custom_call" | custom-call | flops 134217728 | bytes 8388608 | tf_op jit(solution)/shard_map/pallas_call | solution.py:331
  (1 shorter events, 0.0 us)
Async XLA Ops:
  30.4 20.2 %all-to-all-start.1 = ((bf16[16,256,128]{2,1,0:T(8,128)(2,1)}), bf16[16,256,128]{2,1,0:T(8,128)(2,1)S(1)}, u32[]{:S(2)}, u32[]{:S(2)}) async-start(bf16[16,256,128]{2,1,0:T(8,128)(2,1)} %broadcast_in_dim.15), calls=%async_computation.1 | async-start | bytes 2097152 | tf_op jit(solution)/shard_map/all_to_all | solution.py:354
  35.6 6.3 %collective-permute-start = (bf16[32,14336]{1,0:T(8,128)(2,1)S(1)}, bf16[32,14336]{1,0:T(8,128)(2,1)S(1)}, u32[]{:S(2)}, u32[]{:S(2)}) collective-permute-start(bf16[32,14336]{1,0:T(8,128)(2,1)S(1)} %get-tuple-element.15), channel_id=1, source_target_pairs={{0,256},{256,0},{1,257},{257,1},{2,258},{258,2},{3,259},{259,3},{4... | collective-permute-start | bytes 2752520 | tf_op jit(solution)/shard_map/ppermute | solution.py:370
  115.9 11.2 %collective-permute-start.1 = (bf16[4096,128]{1,0:T(8,128)(2,1)S(1)}, bf16[4096,128]{1,0:T(8,128)(2,1)S(1)}, u32[]{:S(2)}, u32[]{:S(2)}) collective-permute-start(bf16[4096,128]{1,0:T(8,128)(2,1)S(1)} %bitcast.7), channel_id=1, source_target_pairs={{0,256},{256,0},{1,257},{257,1},{2,258},{258,2},{3,259},{259,3},{4... | collective-permute-start | bytes 3145736 | tf_op jit(solution)/shard_map/ppermute | solution.py:407
  124.0 3.1 %collective-permute-start.2 = (f32[48,128]{1,0:T(8,128)S(1)}, f32[48,128]{1,0:T(8,128)S(1)}, u32[]{:S(2)}, u32[]{:S(2)}) collective-permute-start(f32[48,128]{1,0:T(8,128)S(1)} %get-tuple-element.21.kept_ref), channel_id=1, source_target_pairs={{0,256},{256,0},{1,257},{257,1},{2,258},{258,2},{3,259},{259,3},{4... | collective-permute-start | bytes 73736 | tf_op jit(solution)/shard_map/ppermute | solution.py:405

commit v3 on v2

--- a/solution.py
+++ b/solution.py
@@ -117,7 +117,7 @@
     keep.wait()
 
 
-def products_kernel(basis_ref, turned_ref, packed_ref, sums_ref, left_ref, extra, packed, sem):
+def products_kernel(far, basis_ref, turned_ref, packed_ref, sums_ref, left_ref, packed, sem):
     step = 512
     loads = []
     for k in range(packed_ref.shape[0] // step):
@@ -140,17 +140,25 @@
         one = jnp.where(group == q, wide, 0.0)
         pieces += [one, one]
     spread = jnp.concatenate(pieces, axis=0).astype(BF)
+    for load in loads:
+        load.wait()
     gram = dot(left, left, 0, 0)[0:R]
-    gram = jnp.where(group == 3, gram, 0.0)
-    extra[...] = jnp.zeros_like(extra)
-    for s, term in enumerate(three_terms(gram)):
-        extra[pl.ds(8 + s, R, stride=16), :] = term
-    for k, load in enumerate(loads):
-        load.wait()
+    terms = three_terms(jnp.where(group == 3, gram, 0.0))
+    row = lax.broadcasted_iota(jnp.int32, (TILE, 128), 0)
+    empty = jnp.zeros((TILE, 128), F32)
+    extra = []
+    for a in range(R // 2):
+        tile = empty
+        for s in range(6):
+            at = 2 * a + s // 3
+            tile = jnp.where(row == s, terms[s % 3][at : at + 1], tile)
+        extra.append(tile)
+    for k in range(len(loads)):
         out = dot(packed[pl.ds(k * step, step), :], spread, 1, 0)
-        if k == 0:
-            out = out + extra[...]
-        sums_ref[pl.ds(k * step, step), :] = out.astype(BF)
+        tiles = []
+        for e in range(k * 32, k * 32 + 32):
+            tiles += [empty, extra[e // far]]
+        sums_ref[pl.ds(k * step, step), :] = (out + jnp.concatenate(tiles, axis=0)).astype(BF)
 
 
 def summed(parts_ref, scale):
@@ -161,11 +169,13 @@
 
     acc = lax.fori_loop(0, count, add, jnp.zeros((rows, 128), F32), unroll=4)
     acc = acc.reshape(rows // 16, 16, 128)
-    gram = acc[:, 8:9] + acc[:, 9:10] + acc[:, 10:11]
     row = lax.broadcasted_iota(jnp.int32, acc.shape, 1)
     lane = lax.broadcasted_iota(jnp.int32, acc.shape, 2)
-    high, middle, low = three_terms(gram)
-    term = jnp.where(row == 8, high, jnp.where(row == 9, middle, jnp.where(row == 10, low, 0.0)))
+    term = jnp.zeros_like(acc)
+    for first in (8, 11):
+        gram = acc[:, first : first + 1] + acc[:, first + 1 : first + 2] + acc[:, first + 2 : first + 3]
+        for s, part in enumerate(three_terms(gram)):
+            term = jnp.where(row == first + s, part, term)
     out = jnp.where((row >= 8) & (lane >= 96), term, scale * acc)
     return out.reshape(rows, 128)
 
@@ -181,30 +191,103 @@
     kept_ref[16:48] = left_ref[...].astype(F32)
 
 
-def last_kernel(
-    sizes, own_ref, other_ref, kept_ref, kept_other_ref, gg_ref, gu_ref,
-    ng_ref, nu_ref, fg_ref, fu_ref, rg_ref, ru_ref,
-    grads, resid, spread, sem_in, sem_out,
+def copies_kernel(line_ref, token_ref, out_ref):
+    del token_ref
+    out_ref[...] = jnp.broadcast_to(line_ref[...][None], out_ref.shape)
+
+
+def copies_with_gram_kernel(line_ref, kept_other_ref, out_ref):
+    line = line_ref[...]
+    row = lax.broadcasted_iota(jnp.int32, (16, 128), 0)
+    spare = (row >= 8) & (groups((16, 128)) == 3)
+    second = jnp.where(spare, kept_other_ref[0:16], line[16:32].astype(F32)).astype(BF)
+    line = jnp.concatenate([line[0:16], second, line[32:]], axis=0)
+    out_ref[...] = jnp.broadcast_to(line[None], out_ref.shape)
+
+
+def pick(core, first, second, to, sem, start):
+    if not start:
+        pltpu.make_async_copy(first, to, sem).wait()
+        return
+
+    @pl.when(core == 0)
+    def _():
+        pltpu.make_async_copy(first, to, sem).start()
+
+    @pl.when(core != 0)
+    def _():
+        pltpu.make_async_copy(second, to, sem).start()
+
+
+def residual(sizes, sums_ref, side, grad, resid, gate, up, at, sem):
+    pair_group = groups((16, 128))
+    second = lax.broadcasted_iota(jnp.int32, (16, 128), 0) >= 8
+    masks = []
+    for v in range(7):
+        a, b = (2 * v) % 7, (2 * v + 1) % 7
+        masks.append(jnp.where(pair_group == jnp.where(second, b % 4, a % 4), 1.0, 0.0).astype(BF))
+    steps = sums_ref.shape[0] // 256
+    cuts = 2
+    for cut in range(cuts):
+
+        @pl.loop(cut * steps // cuts, (cut + 1) * steps // cuts)
+        def _(k):
+            first = place(16 * k, sizes)
+            tiles = []
+            for d in range(16):
+                at_d = pl.multiple_of(16 * (first + place(d, sizes)), 16)
+                x = sums_ref[pl.ds(at_d, 16), :]
+                tiles += [x[0:8]] * 4 + [x[8:16]] * 3
+            rows = []
+            for v in range(56):
+                pair = jnp.concatenate(tiles[2 * v : 2 * v + 2], axis=0)
+                rows.append(pair * masks[v % 7])
+            right = jnp.concatenate(rows, axis=0)
+            both = dot(side, right, 1, 1)
+            columns = pl.ds(pl.multiple_of(k * PERIOD, 128), PERIOD)
+            value = grad[:, columns].astype(F32) - (both[0:R] + both[R : 2 * R])
+            resid[:, columns] = value.astype(BF)
+
+        part = pl.ds(cut * steps // cuts * PERIOD, steps // cuts * PERIOD)
+
+        @pl.when(at == 0)
+        def _():
+            pltpu.make_async_copy(resid.at[:, part], gate.at[0, :, part], sem.at[cut]).start()
+
+        @pl.when(at != 0)
+        def _():
+            pltpu.make_async_copy(resid.at[:, part], up.at[0, :, part], sem.at[cut]).start()
+
+    for cut in range(cuts):
+        part = pl.ds(cut * steps // cuts * PERIOD, steps // cuts * PERIOD)
+        pltpu.make_async_copy(resid.at[:, part], gate.at[0, :, part], sem.at[cut]).wait()
+
+
+def solve_kernel(
+    sizes, own_ref, kept_ref, kept_other_ref, gg_ref, gu_ref,
+    ng_ref, nu_ref, fg_ref, fu_ref, sides_ref, rg_ref, ru_ref,
+    grad, resid, tiles, grams, sem_in, sem_out,
 ):
     core = lax.axis_index("outer")
-    loads = [
-        pltpu.make_async_copy(ref.at[0], grads.at[k], sem_in.at[k])
-        for k, ref in enumerate((gg_ref, gu_ref))
-    ]
-    for load in loads:
-        load.start()
+    pick(core, gg_ref.at[0], gu_ref.at[0], grad, sem_in, True)
+    far = sizes[0] * sizes[2]
     high = lax.Precision.HIGHEST
     group = groups((R, 128))
     row = lax.broadcasted_iota(jnp.int32, (R, 128), 0)
     lane = lax.broadcasted_iota(jnp.int32, (R, 128), 1)
-    grams = []
-    for j, ref in enumerate((own_ref, other_ref)):
-        spread[j] = ref[pl.ds(0, 512), :].astype(F32)
-        gram = spread.at[j][pl.ds(8, R, stride=16), :]
-        gram = gram + spread.at[j][pl.ds(9, R, stride=16), :]
-        gram = gram + spread.at[j][pl.ds(10, R, stride=16), :]
-        grams.append(pltpu.roll(gram, 32 if j == 0 else 96, 1))
-    m = jnp.where(group == 0, grams[0], jnp.where(group == 2, grams[1], 0.0))
+    half = R // 2
+    for j in range(2):
+        for a in range(half):
+            at = 16 * (far * a + j)
+            tiles[j, 8 * a : 8 * a + 8] = own_ref[at : at + 16].astype(F32)[8:16]
+        for odd in range(2):
+            gram = tiles.at[j][pl.ds(3 * odd, half, stride=8), :]
+            for s in range(1, 3):
+                gram = gram + tiles.at[j][pl.ds(3 * odd + s, half, stride=8), :]
+            grams.at[j][pl.ds(odd, half, stride=2), :] = gram
+    own_gram = pltpu.roll(grams[0], 32, 1)
+    other_gram = pltpu.roll(grams[1], 96, 1)
+    m = jnp.where(group == 0, own_gram, jnp.where(group == 2, other_gram, 0.0))
     m = jnp.where((group % 2 == 1) & (row == lane % R), 1.0, m)
     pivots = jnp.ones((R, 128), F32)
     for first in range(0, R, BLOCK):
@@ -228,7 +311,7 @@
     scale = scale * (1.5 - 0.5 * pivots * scale * scale)
     inverse = m * scale
     kept = (kept_ref[...], kept_other_ref[...])
-    nexts, factors, sides = [], [], []
+    nexts, factors = [], []
     for j in range(2):
         at = 1 if j == 0 else 3
         one = jnp.where(group == at, inverse, 0.0)
@@ -236,81 +319,39 @@
         one = one + pltpu.roll(one, 32, 1)
         u = kept[j][0:16]
         left = kept[j][16:48]
-        tiles = []
+        rows = []
         for t in range(7):
             h, q = divmod(t, 4)
-            tiles.append(jnp.where(groups((8, 128)) == q, u[8 * h : 8 * h + 8], 0.0))
-        nexts.append(dot(one, jnp.concatenate(tiles, axis=0), 1, 1, high))
+            rows.append(jnp.where(groups((TILE, 128)) == q, u[8 * h : 8 * h + 8], 0.0))
+        nexts.append(dot(one, jnp.concatenate(rows, axis=0), 1, 1, high))
         factor = dot(jnp.where(group == 0, left, 0.0), one, 1, 1, high)
         factors.append(factor)
         side = dot(factor, one, 1, 0, high)
         top = side.astype(BF)
         rest = (side - top.astype(F32)).astype(BF)
-        sides.append(jnp.concatenate([top, rest], axis=0))
+        sides_ref[j, 0:R] = top
+        sides_ref[j, R : 2 * R] = rest
     swap = core != 0
     ng_ref[...] = jnp.where(swap, nexts[1], nexts[0])
     nu_ref[...] = jnp.where(swap, nexts[0], nexts[1])
     fg_ref[...] = jnp.where(swap, factors[1], factors[0])
     fu_ref[...] = jnp.where(swap, factors[0], factors[1])
-    for load in loads:
-        load.wait()
-    pair_group = groups((16, 128))
-    second = lax.broadcasted_iota(jnp.int32, (16, 128), 0) >= 8
-    masks = []
-    for v in range(7):
-        a, b = (2 * v) % 7, (2 * v + 1) % 7
-        masks.append(jnp.where(pair_group == jnp.where(second, b % 4, a % 4), 1.0, 0.0).astype(BF))
-    outs = (rg_ref, ru_ref)
-    steps = own_ref.shape[0] // 256
-    cuts = 2
-    stores = [
-        [
-            pltpu.make_async_copy(
-                resid.at[k, :, pl.ds(c * steps // cuts * PERIOD, steps // cuts * PERIOD)],
-                ref.at[0, :, pl.ds(c * steps // cuts * PERIOD, steps // cuts * PERIOD)],
-                sem_out.at[k, c],
-            )
-            for c in range(cuts)
-        ]
-        for k, ref in enumerate(outs)
-    ]
-    for j, ref in enumerate((own_ref, other_ref)):
-        at = core if j == 0 else 1 - core
-        side = sides[j]
-        for cut in range(cuts):
-
-            @pl.loop(cut * steps // cuts, (cut + 1) * steps // cuts)
-            def _(k):
-                first = place(16 * k, sizes)
-                tiles = []
-                for d in range(16):
-                    at_d = pl.multiple_of(16 * (first + place(d, sizes)), 16)
-                    x = ref[pl.ds(at_d, 16), :]
-                    tiles += [x[0:8]] * 4 + [x[8:16]] * 3
-                rows = []
-                for v in range(56):
-                    pair = jnp.concatenate(tiles[2 * v : 2 * v + 2], axis=0)
-                    rows.append(pair * masks[v % 7])
-                right = jnp.concatenate(rows, axis=0)
-                both = dot(side, right, 1, 1)
-                columns = pl.ds(pl.multiple_of(k * PERIOD, 128), PERIOD)
-                value = grads.at[at][:, columns].astype(F32) - (both[0:R] + both[R : 2 * R])
-                resid.at[at][:, columns] = value.astype(BF)
-
-            @pl.when(at == 0)
-            def _():
-                stores[0][cut].start()
-
-            @pl.when(at != 0)
-            def _():
-                stores[1][cut].start()
-
-    for line in stores:
-        for store in line:
-            store.wait()
-
-
-def call(kernel, outs, scratch, spaces_in, spaces_out, cost, limit):
+    pick(core, gg_ref.at[0], gu_ref.at[0], grad, sem_in, False)
+    residual(sizes, own_ref, sides_ref[0], grad, resid, rg_ref, ru_ref, core, sem_out)
+
+
+def other_kernel(
+    sizes, sums_ref, sides_ref, gg_ref, gu_ref, rg_in, ru_in, rg_ref, ru_ref,
+    grad, resid, sem_in, sem_out,
+):
+    del rg_in, ru_in
+    core = lax.axis_index("outer")
+    pick(core, gu_ref.at[0], gg_ref.at[0], grad, sem_in, True)
+    pick(core, gu_ref.at[0], gg_ref.at[0], grad, sem_in, False)
+    residual(sizes, sums_ref, sides_ref[1], grad, resid, rg_ref, ru_ref, 1 - core, sem_out)
+
+
+def call(kernel, outs, scratch, spaces_in, spaces_out, cost, limit, aliases={}):
     space = {"h": pltpu.HBM, "v": pltpu.VMEM}
     specs_out = tuple(pl.BlockSpec(memory_space=space[s]) for s in spaces_out)
     run = pl.pallas_call(
@@ -322,6 +363,7 @@
         in_specs=[pl.BlockSpec(memory_space=space[s]) for s in spaces_in],
         out_specs=specs_out,
         scratch_shapes=scratch,
+        input_output_aliases=aliases,
         cost_estimate=pl.CostEstimate(flops=cost, bytes_accessed=cost // 16, transcendentals=0),
         compiler_params=pltpu.CompilerParams(vmem_limit_bytes=limit << 20),
         interpret=INTERPRET,
@@ -353,9 +395,11 @@
     def exchange(x, axes):
         return lax.all_to_all(x, axes, 0, 0, tiled=True)
 
-    def gather(block):
+    def gather(block, kernel, other):
         line = exchange(block, FAR).reshape(16 * far, 128)
-        copies = jnp.broadcast_to(line[None], (near, 16 * far, 128))
+        outs = (shape((near, 16 * far, 128), BF),)
+        space = "h" if other.dtype == BF else "v"
+        (copies,) = call(kernel, outs, [], "v" + space, "v", 1 << 20, 4)(line, other)
         return exchange(copies, NEAR).reshape(packed_rows, 128)
 
     block, send = call(
@@ -368,7 +412,6 @@
         6,
     )(basis_gate, basis_up, grad_gate, grad_up)
     other = lax.ppermute(send, "outer", swap)
-    basis = gather(block)
     packed, turned = call(
         functools.partial(pack_kernel, sizes),
         (shape((packed_rows, 256), BF), shape((256, packed_rows), BF)),
@@ -378,13 +421,11 @@
         1 << 26,
         16,
     )(grad_gate, grad_up, other)
+    basis = gather(block, copies_kernel, packed)
     sums, left = call(
-        products_kernel,
+        functools.partial(products_kernel, far),
         (shape((packed_rows, 128), BF), shape((R, 128), BF)),
-        [
-            pltpu.VMEM((512, 128), F32), pltpu.VMEM((packed_rows, 256), BF),
-            dma((packed_rows // 512,)),
-        ],
+        [pltpu.VMEM((packed_rows, 256), BF), dma((packed_rows // 512,))],
         "vvh",
         "vv",
         1 << 26,
@@ -403,29 +444,38 @@
         4,
     )(parts, left)
     kept_other = lax.ppermute(kept, "outer", swap)
-    own = gather(block)
+    own = gather(block, copies_with_gram_kernel, kept_other)
     theirs = lax.ppermute(own, "outer", swap)
-    outs = call(
-        functools.partial(last_kernel, sizes),
+    working = [pltpu.VMEM((R, columns), BF), pltpu.VMEM((R, columns), BF)]
+    resids = (shape(grad_gate.shape, BF), shape(grad_gate.shape, BF))
+    *small, sides, rg, ru = call(
+        functools.partial(solve_kernel, sizes),
         (
             shape((R, W), F32), shape((R, W), F32), shape((R, R), F32), shape((R, R), F32),
-            shape(grad_gate.shape, BF), shape(grad_gate.shape, BF),
+            shape((2, 2 * R, 128), BF), *resids,
         ),
-        [
-            pltpu.VMEM((2, R, columns), BF), pltpu.VMEM((2, R, columns), BF),
-            pltpu.VMEM((2, 512, 128), F32), dma((2,)), dma((2, 2)),
-        ],
-        "vvvvhh",
-        "vvvvhh",
+        [*working, pltpu.VMEM((2, 128, 128), F32), pltpu.VMEM((2, R, 128), F32), dma, dma((2,))],
+        "vvvhh",
+        "vvvvvhh",
         1 << 27,
-        16,
-    )(own, theirs, kept, kept_other, grad_gate, grad_up)
-    return tuple(outs)
+        12,
+    )(own, kept, kept_other, grad_gate, grad_up)
+    rg, ru = call(
+        functools.partial(other_kernel, sizes),
+        resids,
+        [*working, dma, dma((2,))],
+        "vvhhhh",
+        "hh",
+        1 << 26,
+        12,
+        {4: 0, 5: 1},
+    )(theirs, sides, grad_gate, grad_up, rg, ru)
+    return (*small, rg, ru)
 
 
 def solution(mesh):
     rows = mesh.shape["row"]
-    sizes = (4, 2, 4, 2, 4) if rows == 256 else (2, 2, 2, 2, rows // 16)
+    sizes = (4, 2, 4, 2, 4) if rows == 256 else (2, 2, 1, 2, rows // 8)
     finer = Mesh(mesh.devices.reshape(mesh.shape["outer"], *sizes), ("outer", *ROW))
     return jax.shard_map(
         local,

time: 138 us -> 144 us (1.043)
  blocking collectives: 88 us -> 70.5 us
  starting transfers between devices: 19.4 us -> 36.6 us
  waiting for transfers between devices: 5.55 us -> 10.1 us
  Pallas kernels: 22.8 us -> 25.4 us
    all_to_all x5 -> x4, blocking collectives: 88 us -> 70.5 us  [exchange(): return lax.all_to_all(x, axes, 0, 0, tiled=True)]
    all_to_all x1 -> x2, starting transfers between devices: 5.18 us -> 13.6 us  [exchange(): return lax.all_to_all(x, axes, 0, 0, tiled=True)]
    all_to_all x1 -> x2, waiting for transfers between devices: 2.31 us -> 9.3 us  [exchange(): return lax.all_to_all(x, axes, 0, 0, tiled=True)]
    ppermute x1, starting transfers between devices: 4.24 us -> 8.75 us  [local(): other = lax.ppermute(send, 'outer', swap)]
    ppermute x1, starting transfers between devices: 1.92 us -> 6.22 us  [local(): kept_other = lax.ppermute(kept, 'outer', swap)]
    pallas_call x6 -> x9, Pallas kernels: 22.8 us -> 25.4 us  [pinned(): run(*(pltpu.with_memory_space_constraint(x, pltpu.HBM) if s == 'h' and (n...]
    ppermute x1, waiting for transfers between devices: 2.08 us -> 0.01 us  [local(): other = lax.ppermute(send, 'outer', swap)]
  transfers between devices with their start and end apart: 4 -> 5, of which waited for: 3 -> 3; matrix products, arithmetic and copies ran while one was open for 0% -> 0% of each run, Pallas kernels for 5% -> 10%
where the time goes in v3:
time: 144 us; the launch traced here: 143 us
  blocking collectives  70.5 us (49%)
  starting transfers between devices  36.6 us (25%)
  Pallas kernels  25.4 us (18%)
  waiting for transfers between devices  10.1 us (7%)
    all_to_all x4, blocking collectives, exchange(): return lax.all_to_all(x, axes, 0, 0, tiled=True)  70.5 us
    pallas_call x9, Pallas kernels, pinned(): run(*(pltpu.with_memory_space_constraint(x, pltpu.HBM) if s == 'h' and (n...  25.4 us
    all_to_all x2, starting transfers between devices, exchange(): return lax.all_to_all(x, axes, 0, 0, tiled=True)  13.6 us
    all_to_all x2, waiting for transfers between devices, exchange(): return lax.all_to_all(x, axes, 0, 0, tiled=True)  9.3 us
    ppermute x1, starting transfers between devices, local(): other = lax.ppermute(send, 'outer', swap)  8.75 us
    ppermute x1, starting transfers between devices, local(): theirs = lax.ppermute(own, 'outer', swap)  8.1 us
    ppermute x1, starting transfers between devices, local(): kept_other = lax.ppermute(kept, 'outer', swap)  6.22 us
  transfers between devices with their start and end apart: 5, of which 3 were waited for; matrix products, arithmetic and copies ran while one was open for 0% of the time, Pallas kernels for 10%

profile of v3, /device:TPU:1, one launch (start us, length us, event | category | flops | bytes accessed | tf_op | source)
XLA Modules:
  0.0 143.4 jit_solution(13676526035454455999)
XLA Ops:
  0.6 1.9 %shard_map.91 = (bf16[16,16,128]{2,1,0:T(8,128)(2,1)}, bf16[32,14336]{1,0:T(8,128)(2,1)S(1)}) custom-call(bf16[32,56]{1,0:T(8,128)(2,1)} %bg_ref.1, bf16[32,56]{1,0:T(8,128)(2,1)} %bu_ref.1, bf16[1,32,14336]{2,1,0:T(8,128)(2,1)} %gg_ref.7, bf16[1,32,14336]{2,1,0:T(8,128)(2,1)} %gu_ref.7), custom_call_target="tpu_custom_call" | custom-call | flops 1048576 | bytes 65536 | tf_op jit(solution)/shard_map/pallas_call | solution.py:373
  2.5 8.7 %collective-permute-start = (bf16[32,14336]{1,0:T(8,128)(2,1)S(1)}, bf16[32,14336]{1,0:T(8,128)(2,1)S(1)}, u32[]{:S(2)}, u32[]{:S(2)}) collective-permute-start(bf16[32,14336]{1,0:T(8,128)(2,1)S(1)} %get-tuple-element.24), channel_id=1, source_target_pairs={{0,256},{256,0},{1,257},{257,1},{2,258},{258,2},{3,259},{259,3},{4... | collective-permute-start | bytes 2752520 | tf_op jit(solution)/shard_map/ppermute | solution.py:414
  11.2 10.1 %all-to-all-start = ((bf16[16,16,128]{2,1,0:T(8,128)(2,1)}), bf16[16,16,128]{2,1,0:T(8,128)(2,1)S(1)}, u32[]{:S(2)}, u32[]{:S(2)}) async-start(bf16[16,16,128]{2,1,0:T(8,128)(2,1)} %get-tuple-element.23), calls=%async_computation | async-start | bytes 131072 | tf_op jit(solution)/shard_map/all_to_all | solution.py:396
  21.3 0.0 collective-permute-done.other_ref
  21.3 6.3 %shard_map.92 = (bf16[4096,256]{1,0:T(8,128)(2,1)}, bf16[256,4096]{1,0:T(8,128)(2,1)S(1)}) custom-call(bf16[1,32,14336]{2,1,0:T(8,128)(2,1)} %gg_ref.7, bf16[1,32,14336]{2,1,0:T(8,128)(2,1)} %gu_ref.7, bf16[32,14336]{1,0:T(8,128)(2,1)S(1)} %collective-permute-done.other_ref), custom_call_target="tpu_custom_call" | custom-call | flops 67108864 | bytes 4194304 | tf_op jit(solution)/shard_map/pallas_call | solution.py:373
  27.7 5.1 %all-to-all-done = bf16[16,16,128]{2,1,0:T(8,128)(2,1)S(1)} async-done(((bf16[16,16,128]{2,1,0:T(8,128)(2,1)}), bf16[16,16,128]{2,1,0:T(8,128)(2,1)S(1)}, u32[]{:S(2)}, u32[]{:S(2)}) %all-to-all-start) | async-done | bytes 65568 | tf_op jit(solution)/shard_map/all_to_all | solution.py:396
  32.7 0.2 shard_map.93
  32.9 19.9 %all_to_all.30 = bf16[16,256,128]{2,1,0:T(8,128)(2,1)S(1)} all-to-all(bf16[16,256,128]{2,1,0:T(8,128)(2,1)S(1)} %shard_map.93), channel_id=1, replica_groups=mesh['outer'=2,'yq'=4,'yp'=2,'zq'=4,'zp'=2,'x'=4] {'yp','zp','x'}, dimensions={0} | all-to-all | bytes 2097152 | tf_op jit(solution)/shard_map/all_to_all | solution.py:396
  52.9 2.8 %shard_map.94 = (bf16[4096,128]{1,0:T(8,128)(2,1)S(1)}, bf16[32,128]{1,0:T(8,128)(2,1)S(1)}) custom-call(bf16[4096,128]{1,0:T(8,128)(2,1)S(1)} %bitcast.6, bf16[256,4096]{1,0:T(8,128)(2,1)S(1)} %get-tuple-element.26.turned_ref, bf16[4096,256]{1,0:T(8,128)(2,1)} %get-tuple-element.25.token_ref.packed_ref), custom_call_target="tpu_custom_call" | custom-call | flops 67108864 | bytes 4194304 | tf_op jit(solution)/shard_map/pallas_call | solution.py:373
  55.7 16.8 %all_to_all.31.parts_ref = bf16[16,256,128]{2,1,0:T(8,128)(2,1)S(1)} all-to-all(bf16[16,256,128]{2,1,0:T(8,128)(2,1)S(1)} %bitcast.9), channel_id=1, replica_groups=mesh['outer'=2,'yq'=4,'yp'=2,'zq'=4,'zp'=2,'x'=4] {'yp','zp','x'}, dimensions={0} | all-to-all | bytes 2097152 | tf_op jit(solution)/shard_map/all_to_all | solution.py:396
  72.6 0.3 shard_map.95
  72.8 19.2 %all_to_all.32.parts_ref = bf16[16,16,128]{2,1,0:T(8,128)(2,1)S(1)} all-to-all(bf16[16,16,128]{2,1,0:T(8,128)(2,1)S(1)} %bitcast.12), channel_id=1, replica_groups=mesh['outer'=2,'yq'=4,'yp'=2,'zq'=4,'zp'=2,'x'=4] {'yq','zq'}, dimensions={0} | all-to-all | bytes 131072 | tf_op jit(solution)/shard_map/all_to_all | solution.py:396
  92.0 0.7 shard_map.96
  92.7 3.5 %all-to-all-start.4 = ((bf16[16,16,128]{2,1,0:T(8,128)(2,1)}), bf16[16,16,128]{2,1,0:T(8,128)(2,1)S(1)}, u32[]{:S(2)}, u32[]{:S(2)}) async-start(bf16[16,16,128]{2,1,0:T(8,128)(2,1)} %get-tuple-element.29), calls=%async_computation.4 | async-start | bytes 131072 | tf_op jit(solution)/shard_map/all_to_all | solution.py:396
  96.2 6.2 %collective-permute-start.1 = (f32[48,128]{1,0:T(8,128)S(1)}, f32[48,128]{1,0:T(8,128)S(1)}, u32[]{:S(2)}, u32[]{:S(2)}) collective-permute-start(f32[48,128]{1,0:T(8,128)S(1)} %get-tuple-element.30.kept_ref), channel_id=1, source_target_pairs={{0,256},{256,0},{1,257},{257,1},{2,258},{258,2},{3,259},{259,3},{4... | collective-permute-start | bytes 73736 | tf_op jit(solution)/shard_map/ppermute | solution.py:446
  102.4 0.8 collective-permute-done.1.kept_other_ref
  103.2 4.2 %all-to-all-done.4 = bf16[16,16,128]{2,1,0:T(8,128)(2,1)S(1)} async-done(((bf16[16,16,128]{2,1,0:T(8,128)(2,1)}), bf16[16,16,128]{2,1,0:T(8,128)(2,1)S(1)}, u32[]{:S(2)}, u32[]{:S(2)}) %all-to-all-start.4) | async-done | bytes 65568 | tf_op jit(solution)/shard_map/all_to_all | solution.py:396
  107.5 0.2 shard_map.97
  107.7 14.6 %all_to_all.33 = bf16[16,256,128]{2,1,0:T(8,128)(2,1)S(1)} all-to-all(bf16[16,256,128]{2,1,0:T(8,128)(2,1)S(1)} %shard_map.97), channel_id=1, replica_groups=mesh['outer'=2,'yq'=4,'yp'=2,'zq'=4,'zp'=2,'x'=4] {'yp','zp','x'}, dimensions={0} | all-to-all | bytes 2097152 | tf_op jit(solution)/shard_map/all_to_all | solution.py:396
  122.2 8.1 %collective-permute-start.2 = (bf16[4096,128]{1,0:T(8,128)(2,1)S(1)}, bf16[4096,128]{1,0:T(8,128)(2,1)S(1)}, u32[]{:S(2)}, u32[]{:S(2)}) collective-permute-start(bf16[4096,128]{1,0:T(8,128)(2,1)S(1)} %bitcast.7), channel_id=1, source_target_pairs={{0,256},{256,0},{1,257},{257,1},{2,258},{258,2},{3,259},{259,3},{4... | collective-permute-start | bytes 3145736 | tf_op jit(solution)/shard_map/ppermute | solution.py:448
  130.3 7.6 %shard_map.98 = (f32[32,56]{1,0:T(8,128)}, f32[32,56]{1,0:T(8,128)}, f32[32,32]{1,0:T(8,128)}, f32[32,32]{1,0:T(8,128)}, bf16[2,64,128]{2,1,0:T(8,128)(2,1)S(1)}...) custom-call(bf16[4096,128]{1,0:T(8,128)(2,1)S(1)} %bitcast.8, f32[48,128]{1,0:T(8,128)S(1)} %get-tuple-element.30.kept_ref, ...), custom_call_target="tpu_custom_call" | custom-call | flops 134217728 | bytes 8388608 | tf_op jit(solution)/shard_map/pallas_call | solution.py:373
  137.9 0.0 collective-permute-done.2.sums_ref
  137.9 5.5 %shard_map.99 = (bf16[1,32,14336]{2,1,0:T(8,128)(2,1)}, bf16[1,32,14336]{2,1,0:T(8,128)(2,1)}) custom-call(bf16[4096,128]{1,0:T(8,128)(2,1)S(1)} %collective-permute-done.2.sums_ref, bf16[2,64,128]{2,1,0:T(8,128)(2,1)S(1)} %get-tuple-element.35.sides_ref, bf16[1,32,14336]{2,1,0:T(8,128)(2,1)} %gg_ref.7, ...), custom_call_target="tpu_custom_call", output_to_operand_aliasing={{0}: (4, {}), {1}: (5, {})} | custom-call | flops 67108864 | bytes 4194304 | tf_op jit(solution)/shard_map/pallas_call | solution.py:373
Async XLA Ops:
  2.5 18.8 %collective-permute-start = (bf16[32,14336]{1,0:T(8,128)(2,1)S(1)}, bf16[32,14336]{1,0:T(8,128)(2,1)S(1)}, u32[]{:S(2)}, u32[]{:S(2)}) collective-permute-start(bf16[32,14336]{1,0:T(8,128)(2,1)S(1)} %get-tuple-element.24), channel_id=1, source_target_pairs={{0,256},{256,0},{1,257},{257,1},{2,258},{258,2},{3,259},{259,3},{4... | collective-permute-start | bytes 2752520 | tf_op jit(solution)/shard_map/ppermute | solution.py:414
  11.2 21.5 %all-to-all-start = ((bf16[16,16,128]{2,1,0:T(8,128)(2,1)}), bf16[16,16,128]{2,1,0:T(8,128)(2,1)S(1)}, u32[]{:S(2)}, u32[]{:S(2)}) async-start(bf16[16,16,128]{2,1,0:T(8,128)(2,1)} %get-tuple-element.23), calls=%async_computation | async-start | bytes 131072 | tf_op jit(solution)/shard_map/all_to_all | solution.py:396
  92.7 14.8 %all-to-all-start.4 = ((bf16[16,16,128]{2,1,0:T(8,128)(2,1)}), bf16[16,16,128]{2,1,0:T(8,128)(2,1)S(1)}, u32[]{:S(2)}, u32[]{:S(2)}) async-start(bf16[16,16,128]{2,1,0:T(8,128)(2,1)} %get-tuple-element.29), calls=%async_computation.4 | async-start | bytes 131072 | tf_op jit(solution)/shard_map/all_to_all | solution.py:396
  96.2 7.1 %collective-permute-start.1 = (f32[48,128]{1,0:T(8,128)S(1)}, f32[48,128]{1,0:T(8,128)S(1)}, u32[]{:S(2)}, u32[]{:S(2)}) collective-permute-start(f32[48,128]{1,0:T(8,128)S(1)} %get-tuple-element.30.kept_ref), channel_id=1, source_target_pairs={{0,256},{256,0},{1,257},{257,1},{2,258},{258,2},{3,259},{259,3},{4... | collective-permute-start | bytes 73736 | tf_op jit(solution)/shard_map/ppermute | solution.py:446
  122.2 15.7 %collective-permute-start.2 = (bf16[4096,128]{1,0:T(8,128)(2,1)S(1)}, bf16[4096,128]{1,0:T(8,128)(2,1)S(1)}, u32[]{:S(2)}, u32[]{:S(2)}) collective-permute-start(bf16[4096,128]{1,0:T(8,128)(2,1)S(1)} %bitcast.7), channel_id=1, source_target_pairs={{0,256},{256,0},{1,257},{257,1},{2,258},{258,2},{3,259},{259,3},{4... | collective-permute-start | bytes 3145736 | tf_op jit(solution)/shard_map/ppermute | solution.py:448

commit v4 on v3

--- a/solution.py
+++ b/solution.py
@@ -153,12 +153,13 @@
             at = 2 * a + s // 3
             tile = jnp.where(row == s, terms[s % 3][at : at + 1], tile)
         extra.append(tile)
+    tiles = []
+    for e in range(step // 16):
+        tiles += [empty, extra[e % far]]
+    added = jnp.concatenate(tiles, axis=0)
     for k in range(len(loads)):
         out = dot(packed[pl.ds(k * step, step), :], spread, 1, 0)
-        tiles = []
-        for e in range(k * 32, k * 32 + 32):
-            tiles += [empty, extra[e // far]]
-        sums_ref[pl.ds(k * step, step), :] = (out + jnp.concatenate(tiles, axis=0)).astype(BF)
+        sums_ref[pl.ds(k * step, step), :] = (out + added).astype(BF)
 
 
 def summed(parts_ref, scale):
@@ -184,25 +185,10 @@
     out_ref[...] = summed(parts_ref, 1.0).astype(BF)
 
 
-def total_kernel(parts_ref, left_ref, block_ref, kept_ref):
+def total_kernel(parts_ref, block_ref, kept_ref):
     out = summed(parts_ref, 0.5)
     block_ref[...] = jnp.broadcast_to(out.astype(BF)[None], block_ref.shape)
-    kept_ref[0:16] = out
-    kept_ref[16:48] = left_ref[...].astype(F32)
-
-
-def copies_kernel(line_ref, token_ref, out_ref):
-    del token_ref
-    out_ref[...] = jnp.broadcast_to(line_ref[...][None], out_ref.shape)
-
-
-def copies_with_gram_kernel(line_ref, kept_other_ref, out_ref):
-    line = line_ref[...]
-    row = lax.broadcasted_iota(jnp.int32, (16, 128), 0)
-    spare = (row >= 8) & (groups((16, 128)) == 3)
-    second = jnp.where(spare, kept_other_ref[0:16], line[16:32].astype(F32)).astype(BF)
-    line = jnp.concatenate([line[0:16], second, line[32:]], axis=0)
-    out_ref[...] = jnp.broadcast_to(line[None], out_ref.shape)
+    kept_ref[...] = out
 
 
 def pick(core, first, second, to, sem, start):
@@ -219,7 +205,61 @@
         pltpu.make_async_copy(second, to, sem).start()
 
 
+def solve_kernel(line_ref, kept_ref, left_ref, out_ref, tiles, grams):
+    high = lax.Precision.HIGHEST
+    group = groups((R, 128))
+    row = lax.broadcasted_iota(jnp.int32, (R, 128), 0)
+    lane = lax.broadcasted_iota(jnp.int32, (R, 128), 1)
+    half = R // 2
+    for f in range(half):
+        tiles[8 * f : 8 * f + 8] = line_ref[16 * f : 16 * f + 16].astype(F32)[8:16]
+    for odd in range(2):
+        gram = tiles[pl.ds(3 * odd, half, stride=8), :]
+        for s in range(1, 3):
+            gram = gram + tiles[pl.ds(3 * odd + s, half, stride=8), :]
+        grams[pl.ds(odd, half, stride=2), :] = gram
+    m = jnp.where(group == 0, pltpu.roll(grams[...], 32, 1), 0.0)
+    m = jnp.where((group == 1) & (row == lane % R), 1.0, m)
+    pivots = jnp.ones((R, 128), F32)
+    for first in range(0, R, BLOCK):
+        columns = [jnp.broadcast_to(m[:, k : k + 1], (R, 128)) for k in range(first, first + BLOCK)]
+        rows = [m[k : k + 1] for k in range(first, first + BLOCK)]
+        for i in range(BLOCK):
+            k = first + i
+            pivot = columns[i][k : k + 1]
+            pivots = jnp.where(row == k, pivot, pivots)
+            factor = jnp.where(row > k, columns[i] * (1.0 / pivot), 0.0)
+            for j in range(i + 1, BLOCK):
+                columns[j] = columns[j] - factor * columns[j][k : k + 1]
+                at = first + j
+                rows[j] = rows[j] - factor[at : at + 1] * rows[i]
+            m = m - factor * rows[i]
+    scale = lax.rsqrt(pivots)
+    scale = scale * (1.5 - 0.5 * pivots * scale * scale)
+    one = jnp.where(group == 1, m * scale, 0.0)
+    one = one + pltpu.roll(one, 64, 1)
+    one = one + pltpu.roll(one, 32, 1)
+    u = kept_ref[...]
+    rows = []
+    for t in range(7):
+        h, q = divmod(t, 4)
+        rows.append(jnp.where(groups((TILE, 128)) == q, u[8 * h : 8 * h + 8], 0.0))
+    rows.append(jnp.zeros((128 - W, 128), F32))
+    nexts = dot(one, jnp.concatenate(rows, axis=0), 1, 1, high)
+    left = jnp.where(group == 0, left_ref[...].astype(F32), 0.0)
+    tall = jnp.concatenate([one, one, one, one], axis=0)
+    factors = dot(left, tall, 1, 1, high)
+    out_ref[0:R] = jnp.where(lane < 64, nexts, factors)
+    out_ref[R : 2 * R] = dot(factors[:, 0:R], one, 1, 0, high)
+
+
+CUTS = 4
+
+
 def residual(sizes, sums_ref, side, grad, resid, gate, up, at, sem):
+    top = side.astype(BF)
+    rest = (side - top.astype(F32)).astype(BF)
+    side = jnp.concatenate([top, rest], axis=0)
     pair_group = groups((16, 128))
     second = lax.broadcasted_iota(jnp.int32, (16, 128), 0) >= 8
     masks = []
@@ -227,8 +267,9 @@
         a, b = (2 * v) % 7, (2 * v + 1) % 7
         masks.append(jnp.where(pair_group == jnp.where(second, b % 4, a % 4), 1.0, 0.0).astype(BF))
     steps = sums_ref.shape[0] // 256
-    cuts = 2
-    for cut in range(cuts):
+    cuts = min(CUTS, steps)
+    parts = [pl.ds(c * steps // cuts * PERIOD, steps // cuts * PERIOD) for c in range(cuts)]
+    for cut, part in enumerate(parts):
 
         @pl.loop(cut * steps // cuts, (cut + 1) * steps // cuts)
         def _(k):
@@ -248,8 +289,6 @@
             value = grad[:, columns].astype(F32) - (both[0:R] + both[R : 2 * R])
             resid[:, columns] = value.astype(BF)
 
-        part = pl.ds(cut * steps // cuts * PERIOD, steps // cuts * PERIOD)
-
         @pl.when(at == 0)
         def _():
             pltpu.make_async_copy(resid.at[:, part], gate.at[0, :, part], sem.at[cut]).start()
@@ -258,97 +297,33 @@
         def _():
             pltpu.make_async_copy(resid.at[:, part], up.at[0, :, part], sem.at[cut]).start()
 
-    for cut in range(cuts):
-        part = pl.ds(cut * steps // cuts * PERIOD, steps // cuts * PERIOD)
+    for cut, part in enumerate(parts):
         pltpu.make_async_copy(resid.at[:, part], gate.at[0, :, part], sem.at[cut]).wait()
 
 
-def solve_kernel(
-    sizes, own_ref, kept_ref, kept_other_ref, gg_ref, gu_ref,
-    ng_ref, nu_ref, fg_ref, fu_ref, sides_ref, rg_ref, ru_ref,
-    grad, resid, tiles, grams, sem_in, sem_out,
+def own_kernel(
+    sizes, sums_ref, own_ref, other_ref, gg_ref, gu_ref,
+    ng_ref, nu_ref, fg_ref, fu_ref, other_grad_ref, rg_ref, ru_ref,
+    grad, resid, sem_in, sem_out,
 ):
     core = lax.axis_index("outer")
-    pick(core, gg_ref.at[0], gu_ref.at[0], grad, sem_in, True)
-    far = sizes[0] * sizes[2]
-    high = lax.Precision.HIGHEST
-    group = groups((R, 128))
-    row = lax.broadcasted_iota(jnp.int32, (R, 128), 0)
-    lane = lax.broadcasted_iota(jnp.int32, (R, 128), 1)
-    half = R // 2
-    for j in range(2):
-        for a in range(half):
-            at = 16 * (far * a + j)
-            tiles[j, 8 * a : 8 * a + 8] = own_ref[at : at + 16].astype(F32)[8:16]
-        for odd in range(2):
-            gram = tiles.at[j][pl.ds(3 * odd, half, stride=8), :]
-            for s in range(1, 3):
-                gram = gram + tiles.at[j][pl.ds(3 * odd + s, half, stride=8), :]
-            grams.at[j][pl.ds(odd, half, stride=2), :] = gram
-    own_gram = pltpu.roll(grams[0], 32, 1)
-    other_gram = pltpu.roll(grams[1], 96, 1)
-    m = jnp.where(group == 0, own_gram, jnp.where(group == 2, other_gram, 0.0))
-    m = jnp.where((group % 2 == 1) & (row == lane % R), 1.0, m)
-    pivots = jnp.ones((R, 128), F32)
-    for first in range(0, R, BLOCK):
-        columns = []
-        for k in range(first, first + BLOCK):
-            left = jnp.broadcast_to(m[:, k : k + 1], (R, 128))
-            right = jnp.broadcast_to(m[:, 64 + k : 65 + k], (R, 128))
-            columns.append(jnp.where(lane < 64, left, right))
-        rows = [m[k : k + 1] for k in range(first, first + BLOCK)]
-        for i in range(BLOCK):
-            k = first + i
-            pivot = columns[i][k : k + 1]
-            pivots = jnp.where(row == k, pivot, pivots)
-            factor = jnp.where(row > k, columns[i] * (1.0 / pivot), 0.0)
-            for j in range(i + 1, BLOCK):
-                columns[j] = columns[j] - factor * columns[j][k : k + 1]
-                at = first + j
-                rows[j] = rows[j] - factor[at : at + 1] * rows[i]
-            m = m - factor * rows[i]
-    scale = lax.rsqrt(pivots)
-    scale = scale * (1.5 - 0.5 * pivots * scale * scale)
-    inverse = m * scale
-    kept = (kept_ref[...], kept_other_ref[...])
-    nexts, factors = [], []
-    for j in range(2):
-        at = 1 if j == 0 else 3
-        one = jnp.where(group == at, inverse, 0.0)
-        one = one + pltpu.roll(one, 64, 1)
-        one = one + pltpu.roll(one, 32, 1)
-        u = kept[j][0:16]
-        left = kept[j][16:48]
-        rows = []
-        for t in range(7):
-            h, q = divmod(t, 4)
-            rows.append(jnp.where(groups((TILE, 128)) == q, u[8 * h : 8 * h + 8], 0.0))
-        nexts.append(dot(one, jnp.concatenate(rows, axis=0), 1, 1, high))
-        factor = dot(jnp.where(group == 0, left, 0.0), one, 1, 1, high)
-        factors.append(factor)
-        side = dot(factor, one, 1, 0, high)
-        top = side.astype(BF)
-        rest = (side - top.astype(F32)).astype(BF)
-        sides_ref[j, 0:R] = top
-        sides_ref[j, R : 2 * R] = rest
-    swap = core != 0
-    ng_ref[...] = jnp.where(swap, nexts[1], nexts[0])
-    nu_ref[...] = jnp.where(swap, nexts[0], nexts[1])
-    fg_ref[...] = jnp.where(swap, factors[1], factors[0])
-    fu_ref[...] = jnp.where(swap, factors[0], factors[1])
-    pick(core, gg_ref.at[0], gu_ref.at[0], grad, sem_in, False)
-    residual(sizes, own_ref, sides_ref[0], grad, resid, rg_ref, ru_ref, core, sem_out)
-
-
-def other_kernel(
-    sizes, sums_ref, sides_ref, gg_ref, gu_ref, rg_in, ru_in, rg_ref, ru_ref,
-    grad, resid, sem_in, sem_out,
-):
+    pick(core, gg_ref.at[0], gu_ref.at[0], grad, sem_in.at[0], True)
+    pick(core, gu_ref.at[0], gg_ref.at[0], other_grad_ref, sem_in.at[1], True)
+    own, other = own_ref[0:R], other_ref[0:R]
+    gate, up = jnp.where(core == 0, own, other), jnp.where(core == 0, other, own)
+    ng_ref[...] = gate[:, 0:W]
+    nu_ref[...] = up[:, 0:W]
+    fg_ref[...] = gate[:, 64 : 64 + R]
+    fu_ref[...] = up[:, 64 : 64 + R]
+    pick(core, gg_ref.at[0], gu_ref.at[0], grad, sem_in.at[0], False)
+    residual(sizes, sums_ref, own_ref[R : 2 * R], grad, resid, rg_ref, ru_ref, core, sem_out)
+    pick(core, gu_ref.at[0], gg_ref.at[0], other_grad_ref, sem_in.at[1], False)
+
+
+def other_kernel(sizes, sums_ref, other_ref, grad, rg_in, ru_in, rg_ref, ru_ref, resid, sem_out):
     del rg_in, ru_in
     core = lax.axis_index("outer")
-    pick(core, gu_ref.at[0], gg_ref.at[0], grad, sem_in, True)
-    pick(core, gu_ref.at[0], gg_ref.at[0], grad, sem_in, False)
-    residual(sizes, sums_ref, sides_ref[1], grad, resid, rg_ref, ru_ref, 1 - core, sem_out)
+    residual(sizes, sums_ref, other_ref[R : 2 * R], grad, resid, rg_ref, ru_ref, 1 - core, sem_out)
 
 
 def call(kernel, outs, scratch, spaces_in, spaces_out, cost, limit, aliases={}):
@@ -395,11 +370,11 @@
     def exchange(x, axes):
         return lax.all_to_all(x, axes, 0, 0, tiled=True)
 
-    def gather(block, kernel, other):
-        line = exchange(block, FAR).reshape(16 * far, 128)
-        outs = (shape((near, 16 * far, 128), BF),)
-        space = "h" if other.dtype == BF else "v"
-        (copies,) = call(kernel, outs, [], "v" + space, "v", 1 << 20, 4)(line, other)
+    def gather_far(block):
+        return exchange(block, FAR).reshape(16 * far, 128)
+
+    def gather_near(line):
+        copies = jnp.broadcast_to(line[None], (near, 16 * far, 128))
         return exchange(copies, NEAR).reshape(packed_rows, 128)
 
     block, send = call(
@@ -421,7 +396,7 @@
         1 << 26,
         16,
     )(grad_gate, grad_up, other)
-    basis = gather(block, copies_kernel, packed)
+    basis = gather_near(gather_far(block))
     sums, left = call(
         functools.partial(products_kernel, far),
         (shape((packed_rows, 128), BF), shape((R, 128), BF)),
@@ -436,46 +411,56 @@
     parts = exchange(halfway.reshape(far, 16, 128), FAR)
     block, kept = call(
         total_kernel,
-        (shape((far, 16, 128), BF), shape((48, 128), F32)),
+        (shape((far, 16, 128), BF), shape((16, 128), F32)),
         [],
-        "vv",
+        "v",
         "vv",
         1 << 20,
         4,
-    )(parts, left)
-    kept_other = lax.ppermute(kept, "outer", swap)
-    own = gather(block, copies_with_gram_kernel, kept_other)
-    theirs = lax.ppermute(own, "outer", swap)
-    working = [pltpu.VMEM((R, columns), BF), pltpu.VMEM((R, columns), BF)]
+    )(parts)
+    line = gather_far(block)
+    (own,) = call(
+        solve_kernel,
+        (shape((2 * R, 128), F32),),
+        [pltpu.VMEM((128, 128), F32), pltpu.VMEM((R, 128), F32)],
+        "vvv",
+        "v",
+        1 << 26,
+        4,
+    )(line, kept, left)
+    other = lax.ppermute(own, "outer", swap)
+    sums, other = lax.optimization_barrier((gather_near(line), other))
+    sums_other = lax.ppermute(sums, "outer", swap)
+    working = pltpu.VMEM((R, columns), BF)
     resids = (shape(grad_gate.shape, BF), shape(grad_gate.shape, BF))
-    *small, sides, rg, ru = call(
-        functools.partial(solve_kernel, sizes),
+    *small, other_grad, rg, ru = call(
+        functools.partial(own_kernel, sizes),
         (
             shape((R, W), F32), shape((R, W), F32), shape((R, R), F32), shape((R, R), F32),
-            shape((2, 2 * R, 128), BF), *resids,
+            shape((R, columns), BF), *resids,
         ),
-        [*working, pltpu.VMEM((2, 128, 128), F32), pltpu.VMEM((2, R, 128), F32), dma, dma((2,))],
+        [working, working, dma((2,)), dma((CUTS,))],
         "vvvhh",
         "vvvvvhh",
-        1 << 27,
+        1 << 26,
         12,
-    )(own, kept, kept_other, grad_gate, grad_up)
+    )(sums, own, other, grad_gate, grad_up)
     rg, ru = call(
         functools.partial(other_kernel, sizes),
         resids,
-        [*working, dma, dma((2,))],
-        "vvhhhh",
+        [working, dma((CUTS,))],
+        "vvvhh",
         "hh",
         1 << 26,
         12,
-        {4: 0, 5: 1},
-    )(theirs, sides, grad_gate, grad_up, rg, ru)
+        {3: 0, 4: 1},
+    )(sums_other, other, other_grad, rg, ru)
     return (*small, rg, ru)
 
 
 def solution(mesh):
     rows = mesh.shape["row"]
-    sizes = (4, 2, 4, 2, 4) if rows == 256 else (2, 2, 1, 2, rows // 8)
+    sizes = (4, 2, 4, 2, 4) if rows == 256 else (4, 1, 4, 1, rows // 16)
     finer = Mesh(mesh.devices.reshape(mesh.shape["outer"], *sizes), ("outer", *ROW))
     return jax.shard_map(
         local,

time: 144 us -> 136 us (0.944)
  starting transfers between devices: 36.6 us -> 27.7 us
  blocking collectives: 70.5 us -> 73.8 us
  waiting for transfers between devices: 10.1 us -> 7.57 us
  Pallas kernels: 25.4 us -> 22.9 us
  local copies, waits for them, and re-layouts: 0 us -> 2.36 us
    all_to_all x2, starting transfers between devices: 13.6 us -> 8.84 us  [exchange(): return lax.all_to_all(x, axes, 0, 0, tiled=True)]
    all_to_all x2, waiting for transfers between devices: 9.3 us -> 4.65 us  [exchange(): return lax.all_to_all(x, axes, 0, 0, tiled=True)]
    ppermute x1, starting transfers between devices: 8.75 us -> 4.24 us  [local(): other = lax.ppermute(send, 'outer', swap)]
    all_to_all x4, blocking collectives: 70.5 us -> 73.8 us  [exchange(): return lax.all_to_all(x, axes, 0, 0, tiled=True)]
    pallas_call x9 -> x8, Pallas kernels: 25.4 us -> 22.9 us  [pinned(): run(*(pltpu.with_memory_space_constraint(x, pltpu.HBM) if s == 'h' and (n...]
    broadcast_in_dim x0 -> x2, local copies, waits for them, and re-layouts: none -> 2.36 us  [gather_near(): copies = jnp.broadcast_to(line[None], (near, 16 * far, 128))]
    ppermute x1, waiting for transfers between devices: 0.01 us -> 2.08 us  [local(): other = lax.ppermute(send, 'outer', swap)]
  transfers between devices with their start and end apart: 5 -> 5, of which waited for: 3 -> 4; matrix products, arithmetic and copies ran while one was open for 0% -> 0% of each run, Pallas kernels for 10% -> 11%
where the time goes in v4:
time: 136 us; the launch traced here: 135 us
  blocking collectives  73.8 us (54%)
  starting transfers between devices  27.7 us (20%)
  Pallas kernels  22.9 us (17%)
  waiting for transfers between devices  7.57 us (6%)
  local copies, waits for them, and re-layouts  2.36 us (2%)
    all_to_all x4, blocking collectives, exchange(): return lax.all_to_all(x, axes, 0, 0, tiled=True)  73.8 us
    pallas_call x8, Pallas kernels, pinned(): run(*(pltpu.with_memory_space_constraint(x, pltpu.HBM) if s == 'h' and (n...  22.9 us
    all_to_all x2, starting transfers between devices, exchange(): return lax.all_to_all(x, axes, 0, 0, tiled=True)  8.84 us
    ppermute x1, starting transfers between devices, local(): sums_other = lax.ppermute(sums, 'outer', swap)  7.49 us
    ppermute x1, starting transfers between devices, local(): other = lax.ppermute(own, 'outer', swap)  7.15 us
    all_to_all x2, waiting for transfers between devices, exchange(): return lax.all_to_all(x, axes, 0, 0, tiled=True)  4.65 us
    ppermute x1, starting transfers between devices, local(): other = lax.ppermute(send, 'outer', swap)  4.24 us
  transfers between devices with their start and end apart: 5, of which 4 were waited for; matrix products, arithmetic and copies ran while one was open for 0% of the time, Pallas kernels for 11%

profile of v4, /device:TPU:1, one launch (start us, length us, event | category | flops | bytes accessed | tf_op | source)
XLA Modules:
  0.0 135.0 jit_solution(4971744543806144564)
XLA Ops:
  0.6 1.2 shard_map.91
  1.9 27.3 %all_to_all.30 = bf16[16,16,128]{2,1,0:T(8,128)(2,1)S(1)} all-to-all(bf16[16,16,128]{2,1,0:T(8,128)(2,1)S(1)} %get-tuple-element.25), channel_id=1, replica_groups=mesh['outer'=2,'yq'=4,'yp'=2,'zq'=4,'zp'=2,'x'=4] {'yq','zq'}, dimensions={0} | all-to-all | bytes 131072 | tf_op jit(solution)/shard_map/all_to_all | solution.py:371
  29.2 1.2 broadcast_in_dim.15
  30.4 5.2 %all-to-all-start.1 = ((bf16[16,256,128]{2,1,0:T(8,128)(2,1)}), bf16[16,256,128]{2,1,0:T(8,128)(2,1)S(1)}, u32[]{:S(2)}, u32[]{:S(2)}) async-start(bf16[16,256,128]{2,1,0:T(8,128)(2,1)} %broadcast_in_dim.15), calls=%async_computation.1 | async-start | bytes 2097152 | tf_op jit(solution)/shard_map/all_to_all | solution.py:371
  35.6 4.2 %collective-permute-start = (bf16[32,14336]{1,0:T(8,128)(2,1)S(1)}, bf16[32,14336]{1,0:T(8,128)(2,1)S(1)}, u32[]{:S(2)}, u32[]{:S(2)}) collective-permute-start(bf16[32,14336]{1,0:T(8,128)(2,1)S(1)} %get-tuple-element.26), channel_id=1, source_target_pairs={{0,256},{256,0},{1,257},{257,1},{2,258},{258,2},{3,259},{259,3},{4... | collective-permute-start | bytes 2752520 | tf_op jit(solution)/shard_map/ppermute | solution.py:389
  39.8 2.1 %collective-permute-done.other_ref = bf16[32,14336]{1,0:T(8,128)(2,1)S(1)} collective-permute-done((bf16[32,14336]{1,0:T(8,128)(2,1)S(1)}, bf16[32,14336]{1,0:T(8,128)(2,1)S(1)}, u32[]{:S(2)}, u32[]{:S(2)}) %collective-permute-start) | collective-permute-done | bytes 917536 | tf_op jit(solution)/shard_map/ppermute | solution.py:389
  41.9 6.3 %shard_map.92 = (bf16[4096,256]{1,0:T(8,128)(2,1)}, bf16[256,4096]{1,0:T(8,128)(2,1)S(1)}) custom-call(bf16[1,32,14336]{2,1,0:T(8,128)(2,1)} %gg_ref.5, bf16[1,32,14336]{2,1,0:T(8,128)(2,1)} %gu_ref.5, bf16[32,14336]{1,0:T(8,128)(2,1)S(1)} %collective-permute-done.other_ref), custom_call_target="tpu_custom_call" | custom-call | flops 67108864 | bytes 4194304 | tf_op jit(solution)/shard_map/pallas_call | solution.py:348
  48.2 2.3 %all-to-all-done.1 = bf16[16,256,128]{2,1,0:T(8,128)(2,1)S(1)} async-done(((bf16[16,256,128]{2,1,0:T(8,128)(2,1)}), bf16[16,256,128]{2,1,0:T(8,128)(2,1)S(1)}, u32[]{:S(2)}, u32[]{:S(2)}) %all-to-all-start.1) | async-done | bytes 1048608 | tf_op jit(solution)/shard_map/all_to_all | solution.py:371
  50.5 2.8 %shard_map.93 = (bf16[4096,128]{1,0:T(8,128)(2,1)S(1)}, bf16[32,128]{1,0:T(8,128)(2,1)S(1)}) custom-call(bf16[4096,128]{1,0:T(8,128)(2,1)S(1)} %bitcast.8, bf16[256,4096]{1,0:T(8,128)(2,1)S(1)} %get-tuple-element.27.turned_ref, bf16[4096,256]{1,0:T(8,128)(2,1)} %get-tuple-element.28.packed_ref), custom_call_target="tpu_custom_call" | custom-call | flops 67108864 | bytes 4194304 | tf_op jit(solution)/shard_map/pallas_call | solution.py:348
  53.4 18.6 %all_to_all.31.parts_ref = bf16[16,256,128]{2,1,0:T(8,128)(2,1)S(1)} all-to-all(bf16[16,256,128]{2,1,0:T(8,128)(2,1)S(1)} %bitcast.9), channel_id=1, replica_groups=mesh['outer'=2,'yq'=4,'yp'=2,'zq'=4,'zp'=2,'x'=4] {'yp','zp','x'}, dimensions={0} | all-to-all | bytes 2097152 | tf_op jit(solution)/shard_map/all_to_all | solution.py:371
  72.0 0.3 shard_map.94
  72.3 13.9 %all_to_all.32.parts_ref = bf16[16,16,128]{2,1,0:T(8,128)(2,1)S(1)} all-to-all(bf16[16,16,128]{2,1,0:T(8,128)(2,1)S(1)} %bitcast.12), channel_id=1, replica_groups=mesh['outer'=2,'yq'=4,'yp'=2,'zq'=4,'zp'=2,'x'=4] {'yq','zq'}, dimensions={0} | all-to-all | bytes 131072 | tf_op jit(solution)/shard_map/all_to_all | solution.py:371
  86.2 13.9 %all_to_all.33 = bf16[16,16,128]{2,1,0:T(8,128)(2,1)S(1)} all-to-all(bf16[16,16,128]{2,1,0:T(8,128)(2,1)S(1)} %get-tuple-element.30), channel_id=1, replica_groups=mesh['outer'=2,'yq'=4,'yp'=2,'zq'=4,'zp'=2,'x'=4] {'yq','zq'}, dimensions={0} | all-to-all | bytes 131072 | tf_op jit(solution)/shard_map/all_to_all | solution.py:371
  100.1 1.2 broadcast_in_dim.17
  101.3 3.7 %all-to-all-start.5 = ((bf16[16,256,128]{2,1,0:T(8,128)(2,1)}), bf16[16,256,128]{2,1,0:T(8,128)(2,1)S(1)}, u32[]{:S(2)}, u32[]{:S(2)}) async-start(bf16[16,256,128]{2,1,0:T(8,128)(2,1)} %broadcast_in_dim.17), calls=%async_computation.5 | async-start | bytes 2097152 | tf_op jit(solution)/shard_map/all_to_all | solution.py:371
  105.0 1.9 %shard_map.96.own_ref = f32[64,128]{1,0:T(8,128)S(1)} custom-call(bf16[256,128]{1,0:T(8,128)(2,1)S(1)} %bitcast.11, f32[16,128]{1,0:T(8,128)S(1)} %get-tuple-element.31.kept_ref, bf16[32,128]{1,0:T(8,128)(2,1)S(1)} %get-tuple-element.32.left_ref), custom_call_target="tpu_custom_call" | custom-call | flops 67108864 | bytes 4194304 | tf_op jit(solution)/shard_map/pallas_call | solution.py:348
  106.9 7.2 %collective-permute-start.1 = (f32[64,128]{1,0:T(8,128)S(1)}, f32[64,128]{1,0:T(8,128)S(1)}, u32[]{:S(2)}, u32[]{:S(2)}) collective-permute-start(f32[64,128]{1,0:T(8,128)S(1)} %shard_map.96.own_ref), channel_id=1, source_target_pairs={{0,256},{256,0},{1,257},{257,1},{2,258},{258,2},{3,259},{259,3},{4... | collective-permute-start | bytes 98312 | tf_op jit(solution)/shard_map/ppermute | solution.py:431
  114.0 0.8 collective-permute-done.1.other_ref
  114.9 2.3 %all-to-all-done.5 = bf16[16,256,128]{2,1,0:T(8,128)(2,1)S(1)} async-done(((bf16[16,256,128]{2,1,0:T(8,128)(2,1)}), bf16[16,256,128]{2,1,0:T(8,128)(2,1)S(1)}, u32[]{:S(2)}, u32[]{:S(2)}) %all-to-all-start.5) | async-done | bytes 1048608 | tf_op jit(solution)/shard_map/all_to_all | solution.py:371
  117.2 7.5 %collective-permute-start.2 = (bf16[4096,128]{1,0:T(8,128)(2,1)S(1)}, bf16[4096,128]{1,0:T(8,128)(2,1)S(1)}, u32[]{:S(2)}, u32[]{:S(2)}) collective-permute-start(bf16[4096,128]{1,0:T(8,128)(2,1)S(1)} %bitcast.6), channel_id=1, source_target_pairs={{0,256},{256,0},{1,257},{257,1},{2,258},{258,2},{3,259},{259,3},{4... | collective-permute-start | bytes 3145736 | tf_op jit(solution)/shard_map/ppermute | solution.py:433
  124.7 6.0 %shard_map.97 = (f32[32,56]{1,0:T(8,128)}, f32[32,56]{1,0:T(8,128)}, f32[32,32]{1,0:T(8,128)}, f32[32,32]{1,0:T(8,128)}, bf16[32,14336]{1,0:T(8,128)(2,1)S(1)}, ...) custom-call(bf16[4096,128]{1,0:T(8,128)(2,1)S(1)} %bitcast.7, f32[64,128]{1,0:T(8,128)S(1)} %shard_map.96.own_ref, ...), custom_call_target="tpu_custom_call" | custom-call | flops 67108864 | bytes 4194304 | tf_op jit(solution)/shard_map/pallas_call | solution.py:348
  130.7 0.0 collective-permute-done.2.sums_ref
  130.8 4.2 %shard_map.98 = (bf16[1,32,14336]{2,1,0:T(8,128)(2,1)}, bf16[1,32,14336]{2,1,0:T(8,128)(2,1)}) custom-call(bf16[4096,128]{1,0:T(8,128)(2,1)S(1)} %collective-permute-done.2.sums_ref, f32[64,128]{1,0:T(8,128)S(1)} %collective-permute-done.1.other_ref, bf16[32,14336]{1,0:T(8,128)(2,1)S(1)} %get-tuple-element.39.grad, ...), custom_call_target="tpu_custom_call", output_to_operand_aliasing={{0}: (3, {}), {1}: (4, {})} | custom-call | flops 67108864 | bytes 4194304 | tf_op jit(solution)/shard_map/pallas_call | solution.py:348
  (1 shorter events, 0.0 us)
Async XLA Ops:
  30.4 20.2 %all-to-all-start.1 = ((bf16[16,256,128]{2,1,0:T(8,128)(2,1)}), bf16[16,256,128]{2,1,0:T(8,128)(2,1)S(1)}, u32[]{:S(2)}, u32[]{:S(2)}) async-start(bf16[16,256,128]{2,1,0:T(8,128)(2,1)} %broadcast_in_dim.15), calls=%async_computation.1 | async-start | bytes 2097152 | tf_op jit(solution)/shard_map/all_to_all | solution.py:371
  35.6 6.3 %collective-permute-start = (bf16[32,14336]{1,0:T(8,128)(2,1)S(1)}, bf16[32,14336]{1,0:T(8,128)(2,1)S(1)}, u32[]{:S(2)}, u32[]{:S(2)}) collective-permute-start(bf16[32,14336]{1,0:T(8,128)(2,1)S(1)} %get-tuple-element.26), channel_id=1, source_target_pairs={{0,256},{256,0},{1,257},{257,1},{2,258},{258,2},{3,259},{259,3},{4... | collective-permute-start | bytes 2752520 | tf_op jit(solution)/shard_map/ppermute | solution.py:389
  101.3 15.9 %all-to-all-start.5 = ((bf16[16,256,128]{2,1,0:T(8,128)(2,1)}), bf16[16,256,128]{2,1,0:T(8,128)(2,1)S(1)}, u32[]{:S(2)}, u32[]{:S(2)}) async-start(bf16[16,256,128]{2,1,0:T(8,128)(2,1)} %broadcast_in_dim.17), calls=%async_computation.5 | async-start | bytes 2097152 | tf_op jit(solution)/shard_map/all_to_all | solution.py:371
  106.9 8.0 %collective-permute-start.1 = (f32[64,128]{1,0:T(8,128)S(1)}, f32[64,128]{1,0:T(8,128)S(1)}, u32[]{:S(2)}, u32[]{:S(2)}) collective-permute-start(f32[64,128]{1,0:T(8,128)S(1)} %shard_map.96.own_ref), channel_id=1, source_target_pairs={{0,256},{256,0},{1,257},{257,1},{2,258},{258,2},{3,259},{259,3},{4... | collective-permute-start | bytes 98312 | tf_op jit(solution)/shard_map/ppermute | solution.py:431
  117.2 13.5 %collective-permute-start.2 = (bf16[4096,128]{1,0:T(8,128)(2,1)S(1)}, bf16[4096,128]{1,0:T(8,128)(2,1)S(1)}, u32[]{:S(2)}, u32[]{:S(2)}) collective-permute-start(bf16[4096,128]{1,0:T(8,128)(2,1)S(1)} %bitcast.6), channel_id=1, source_target_pairs={{0,256},{256,0},{1,257},{257,1},{2,258},{258,2},{3,259},{259,3},{4... | collective-permute-start | bytes 3145736 | tf_op jit(solution)/shard_map/ppermute | solution.py:433

commit v5 on v4

--- a/solution.py
+++ b/solution.py
@@ -205,7 +205,12 @@
         pltpu.make_async_copy(second, to, sem).start()
 
 
-def solve_kernel(line_ref, kept_ref, left_ref, out_ref, tiles, grams):
+def solve_kernel(
+    line_ref, kept_ref, left_ref, gg_ref, gu_ref, out_ref, grad_ref, other_grad_ref, tiles, grams, sem
+):
+    core = lax.axis_index("outer")
+    pick(core, gg_ref.at[0], gu_ref.at[0], grad_ref, sem.at[0], True)
+    pick(core, gu_ref.at[0], gg_ref.at[0], other_grad_ref, sem.at[1], True)
     high = lax.Precision.HIGHEST
     group = groups((R, 128))
     row = lax.broadcasted_iota(jnp.int32, (R, 128), 0)
@@ -251,43 +256,51 @@
     factors = dot(left, tall, 1, 1, high)
     out_ref[0:R] = jnp.where(lane < 64, nexts, factors)
     out_ref[R : 2 * R] = dot(factors[:, 0:R], one, 1, 0, high)
-
-
-CUTS = 4
+    pick(core, gg_ref.at[0], gu_ref.at[0], grad_ref, sem.at[0], False)
+    pick(core, gu_ref.at[0], gg_ref.at[0], other_grad_ref, sem.at[1], False)
+
+
+CUTS = (4, 7, 8)
 
 
 def residual(sizes, sums_ref, side, grad, resid, gate, up, at, sem):
     top = side.astype(BF)
     rest = (side - top.astype(F32)).astype(BF)
     side = jnp.concatenate([top, rest], axis=0)
+    none = jnp.zeros_like(side)
+    side = jnp.concatenate(
+        [jnp.concatenate([side, none], axis=1), jnp.concatenate([none, side], axis=1)], axis=0
+    )
     pair_group = groups((16, 128))
     second = lax.broadcasted_iota(jnp.int32, (16, 128), 0) >= 8
     masks = []
     for v in range(7):
         a, b = (2 * v) % 7, (2 * v + 1) % 7
         masks.append(jnp.where(pair_group == jnp.where(second, b % 4, a % 4), 1.0, 0.0).astype(BF))
-    steps = sums_ref.shape[0] // 256
-    cuts = min(CUTS, steps)
-    parts = [pl.ds(c * steps // cuts * PERIOD, steps // cuts * PERIOD) for c in range(cuts)]
+    wide = 2 * PERIOD
+    steps = sums_ref.shape[0] // 512
+    edges = [0, *(e * steps // 8 for e in CUTS)]
+    parts = [pl.ds(a * wide, (b - a) * wide) for a, b in zip(edges, edges[1:]) if b > a]
+    spans = [range(a, b) for a, b in zip(edges, edges[1:]) if b > a]
     for cut, part in enumerate(parts):
-
-        @pl.loop(cut * steps // cuts, (cut + 1) * steps // cuts)
-        def _(k):
-            first = place(16 * k, sizes)
-            tiles = []
-            for d in range(16):
-                at_d = pl.multiple_of(16 * (first + place(d, sizes)), 16)
-                x = sums_ref[pl.ds(at_d, 16), :]
-                tiles += [x[0:8]] * 4 + [x[8:16]] * 3
-            rows = []
-            for v in range(56):
-                pair = jnp.concatenate(tiles[2 * v : 2 * v + 2], axis=0)
-                rows.append(pair * masks[v % 7])
-            right = jnp.concatenate(rows, axis=0)
-            both = dot(side, right, 1, 1)
-            columns = pl.ds(pl.multiple_of(k * PERIOD, 128), PERIOD)
-            value = grad[:, columns].astype(F32) - (both[0:R] + both[R : 2 * R])
-            resid[:, columns] = value.astype(BF)
+        for k in spans[cut]:
+            halves = []
+            for half in range(2):
+                tiles = []
+                for d in range(32 * k + 16 * half, 32 * k + 16 * half + 16):
+                    at_d = 16 * place(d, sizes)
+                    x = sums_ref[at_d : at_d + 16, :]
+                    tiles += [x[0:8]] * 4 + [x[8:16]] * 3
+                rows = []
+                for v in range(56):
+                    pair = jnp.concatenate(tiles[2 * v : 2 * v + 2], axis=0)
+                    rows.append(pair * masks[v % 7])
+                halves.append(jnp.concatenate(rows, axis=0))
+            both = dot(side, jnp.concatenate(halves, axis=1), 1, 1)
+            for half in range(2):
+                product = both[64 * half : 64 * half + R] + both[64 * half + R : 64 * half + 64]
+                columns = pl.ds(k * wide + half * PERIOD, PERIOD)
+                resid[:, columns] = (grad[:, columns].astype(F32) - product).astype(BF)
 
         @pl.when(at == 0)
         def _():
@@ -302,22 +315,17 @@
 
 
 def own_kernel(
-    sizes, sums_ref, own_ref, other_ref, gg_ref, gu_ref,
-    ng_ref, nu_ref, fg_ref, fu_ref, other_grad_ref, rg_ref, ru_ref,
-    grad, resid, sem_in, sem_out,
+    sizes, sums_ref, own_ref, other_ref, grad,
+    ng_ref, nu_ref, fg_ref, fu_ref, rg_ref, ru_ref, resid, sem_out,
 ):
     core = lax.axis_index("outer")
-    pick(core, gg_ref.at[0], gu_ref.at[0], grad, sem_in.at[0], True)
-    pick(core, gu_ref.at[0], gg_ref.at[0], other_grad_ref, sem_in.at[1], True)
     own, other = own_ref[0:R], other_ref[0:R]
     gate, up = jnp.where(core == 0, own, other), jnp.where(core == 0, other, own)
     ng_ref[...] = gate[:, 0:W]
     nu_ref[...] = up[:, 0:W]
     fg_ref[...] = gate[:, 64 : 64 + R]
     fu_ref[...] = up[:, 64 : 64 + R]
-    pick(core, gg_ref.at[0], gu_ref.at[0], grad, sem_in.at[0], False)
     residual(sizes, sums_ref, own_ref[R : 2 * R], grad, resid, rg_ref, ru_ref, core, sem_out)
-    pick(core, gu_ref.at[0], gg_ref.at[0], other_grad_ref, sem_in.at[1], False)
 
 
 def other_kernel(sizes, sums_ref, other_ref, grad, rg_in, ru_in, rg_ref, ru_ref, resid, sem_out):
@@ -419,36 +427,34 @@
         4,
     )(parts)
     line = gather_far(block)
-    (own,) = call(
+    natural = shape((R, columns), BF)
+    own, own_grad, other_grad = call(
         solve_kernel,
-        (shape((2 * R, 128), F32),),
-        [pltpu.VMEM((128, 128), F32), pltpu.VMEM((R, 128), F32)],
+        (shape((2 * R, 128), F32), natural, natural),
+        [pltpu.VMEM((128, 128), F32), pltpu.VMEM((R, 128), F32), dma((2,))],
+        "vvvhh",
         "vvv",
-        "v",
         1 << 26,
         4,
-    )(line, kept, left)
+    )(line, kept, left, grad_gate, grad_up)
     other = lax.ppermute(own, "outer", swap)
     sums, other = lax.optimization_barrier((gather_near(line), other))
     sums_other = lax.ppermute(sums, "outer", swap)
     working = pltpu.VMEM((R, columns), BF)
     resids = (shape(grad_gate.shape, BF), shape(grad_gate.shape, BF))
-    *small, other_grad, rg, ru = call(
+    *small, rg, ru = call(
         functools.partial(own_kernel, sizes),
-        (
-            shape((R, W), F32), shape((R, W), F32), shape((R, R), F32), shape((R, R), F32),
-            shape((R, columns), BF), *resids,
-        ),
-        [working, working, dma((2,)), dma((CUTS,))],
-        "vvvhh",
-        "vvvvvhh",
+        (shape((R, W), F32), shape((R, W), F32), shape((R, R), F32), shape((R, R), F32), *resids),
+        [working, dma((len(CUTS),))],
+        "vvvv",
+        "vvvvhh",
         1 << 26,
         12,
-    )(sums, own, other, grad_gate, grad_up)
+    )(sums, own, other, own_grad)
     rg, ru = call(
         functools.partial(other_kernel, sizes),
         resids,
-        [working, dma((CUTS,))],
+        [working, dma((len(CUTS),))],
         "vvvhh",
         "hh",
         1 << 26,

time: 136 us -> 130 us (0.956)
  Pallas kernels: 22.9 us -> 17.9 us
    pallas_call x8, Pallas kernels: 22.9 us -> 17.9 us  [pinned(): run(*(pltpu.with_memory_space_constraint(x, pltpu.HBM) if s == 'h' and (n...]
  transfers between devices with their start and end apart: 5 -> 5, of which waited for: 4 -> 4; matrix products, arithmetic and copies ran while one was open for 0% -> 0% of each run, Pallas kernels for 11% -> 9%
where the time goes in v5:
time: 130 us; the launch traced here: 129 us
  blocking collectives  73.8 us (57%)
  starting transfers between devices  27.7 us (21%)
  Pallas kernels  17.9 us (14%)
  waiting for transfers between devices  6.68 us (5%)
  local copies, waits for them, and re-layouts  2.35 us (2%)
    all_to_all x4, blocking collectives, exchange(): return lax.all_to_all(x, axes, 0, 0, tiled=True)  73.8 us
    pallas_call x8, Pallas kernels, pinned(): run(*(pltpu.with_memory_space_constraint(x, pltpu.HBM) if s == 'h' and (n...  17.9 us
    all_to_all x2, starting transfers between devices, exchange(): return lax.all_to_all(x, axes, 0, 0, tiled=True)  8.84 us
    ppermute x1, starting transfers between devices, local(): sums_other = lax.ppermute(sums, 'outer', swap)  7.49 us
    ppermute x1, starting transfers between devices, local(): other = lax.ppermute(own, 'outer', swap)  7.13 us
    ppermute x1, starting transfers between devices, local(): other = lax.ppermute(send, 'outer', swap)  4.24 us
    all_to_all x2, waiting for transfers between devices, exchange(): return lax.all_to_all(x, axes, 0, 0, tiled=True)  3.76 us
  transfers between devices with their start and end apart: 5, of which 4 were waited for; matrix products, arithmetic and copies ran while one was open for 0% of the time, Pallas kernels for 9%

profile of v5, /device:TPU:1, one launch (start us, length us, event | category | flops | bytes accessed | tf_op | source)
XLA Modules:
  0.0 129.1 jit_solution(360162513055105924)
XLA Ops:
  0.6 1.2 shard_map.91
  1.9 27.3 %all_to_all.30 = bf16[16,16,128]{2,1,0:T(8,128)(2,1)S(1)} all-to-all(bf16[16,16,128]{2,1,0:T(8,128)(2,1)S(1)} %get-tuple-element.27), channel_id=1, replica_groups=mesh['outer'=2,'yq'=4,'yp'=2,'zq'=4,'zp'=2,'x'=4] {'yq','zq'}, dimensions={0} | all-to-all | bytes 131072 | tf_op jit(solution)/shard_map/all_to_all | solution.py:379
  29.2 1.2 broadcast_in_dim.15
  30.4 5.2 %all-to-all-start.1 = ((bf16[16,256,128]{2,1,0:T(8,128)(2,1)}), bf16[16,256,128]{2,1,0:T(8,128)(2,1)S(1)}, u32[]{:S(2)}, u32[]{:S(2)}) async-start(bf16[16,256,128]{2,1,0:T(8,128)(2,1)} %broadcast_in_dim.15), calls=%async_computation.1 | async-start | bytes 2097152 | tf_op jit(solution)/shard_map/all_to_all | solution.py:379
  35.6 4.2 %collective-permute-start = (bf16[32,14336]{1,0:T(8,128)(2,1)S(1)}, bf16[32,14336]{1,0:T(8,128)(2,1)S(1)}, u32[]{:S(2)}, u32[]{:S(2)}) collective-permute-start(bf16[32,14336]{1,0:T(8,128)(2,1)S(1)} %get-tuple-element.28), channel_id=1, source_target_pairs={{0,256},{256,0},{1,257},{257,1},{2,258},{258,2},{3,259},{259,3},{4... | collective-permute-start | bytes 2752520 | tf_op jit(solution)/shard_map/ppermute | solution.py:397
  39.8 2.1 %collective-permute-done.other_ref = bf16[32,14336]{1,0:T(8,128)(2,1)S(1)} collective-permute-done((bf16[32,14336]{1,0:T(8,128)(2,1)S(1)}, bf16[32,14336]{1,0:T(8,128)(2,1)S(1)}, u32[]{:S(2)}, u32[]{:S(2)}) %collective-permute-start) | collective-permute-done | bytes 917536 | tf_op jit(solution)/shard_map/ppermute | solution.py:397
  41.9 6.3 %shard_map.92 = (bf16[4096,256]{1,0:T(8,128)(2,1)}, bf16[256,4096]{1,0:T(8,128)(2,1)S(1)}) custom-call(bf16[1,32,14336]{2,1,0:T(8,128)(2,1)} %gg_ref.5, bf16[1,32,14336]{2,1,0:T(8,128)(2,1)} %gu_ref.5, bf16[32,14336]{1,0:T(8,128)(2,1)S(1)} %collective-permute-done.other_ref), custom_call_target="tpu_custom_call" | custom-call | flops 67108864 | bytes 4194304 | tf_op jit(solution)/shard_map/pallas_call | solution.py:356
  48.2 2.3 %all-to-all-done.1 = bf16[16,256,128]{2,1,0:T(8,128)(2,1)S(1)} async-done(((bf16[16,256,128]{2,1,0:T(8,128)(2,1)}), bf16[16,256,128]{2,1,0:T(8,128)(2,1)S(1)}, u32[]{:S(2)}, u32[]{:S(2)}) %all-to-all-start.1) | async-done | bytes 1048608 | tf_op jit(solution)/shard_map/all_to_all | solution.py:379
  50.5 2.8 %shard_map.93 = (bf16[4096,128]{1,0:T(8,128)(2,1)S(1)}, bf16[32,128]{1,0:T(8,128)(2,1)S(1)}) custom-call(bf16[4096,128]{1,0:T(8,128)(2,1)S(1)} %bitcast.6, bf16[256,4096]{1,0:T(8,128)(2,1)S(1)} %get-tuple-element.29.turned_ref, bf16[4096,256]{1,0:T(8,128)(2,1)} %get-tuple-element.30.packed_ref), custom_call_target="tpu_custom_call" | custom-call | flops 67108864 | bytes 4194304 | tf_op jit(solution)/shard_map/pallas_call | solution.py:356
  53.4 18.7 %all_to_all.31.parts_ref = bf16[16,256,128]{2,1,0:T(8,128)(2,1)S(1)} all-to-all(bf16[16,256,128]{2,1,0:T(8,128)(2,1)S(1)} %bitcast.9), channel_id=1, replica_groups=mesh['outer'=2,'yq'=4,'yp'=2,'zq'=4,'zp'=2,'x'=4] {'yp','zp','x'}, dimensions={0} | all-to-all | bytes 2097152 | tf_op jit(solution)/shard_map/all_to_all | solution.py:379
  72.0 0.3 shard_map.94
  72.3 13.9 %all_to_all.32.parts_ref = bf16[16,16,128]{2,1,0:T(8,128)(2,1)S(1)} all-to-all(bf16[16,16,128]{2,1,0:T(8,128)(2,1)S(1)} %bitcast.12), channel_id=1, replica_groups=mesh['outer'=2,'yq'=4,'yp'=2,'zq'=4,'zp'=2,'x'=4] {'yq','zq'}, dimensions={0} | all-to-all | bytes 131072 | tf_op jit(solution)/shard_map/all_to_all | solution.py:379
  86.2 13.9 %all_to_all.33 = bf16[16,16,128]{2,1,0:T(8,128)(2,1)S(1)} all-to-all(bf16[16,16,128]{2,1,0:T(8,128)(2,1)S(1)} %get-tuple-element.32), channel_id=1, replica_groups=mesh['outer'=2,'yq'=4,'yp'=2,'zq'=4,'zp'=2,'x'=4] {'yq','zq'}, dimensions={0} | all-to-all | bytes 131072 | tf_op jit(solution)/shard_map/all_to_all | solution.py:379
  100.1 1.2 broadcast_in_dim.17
  101.3 3.7 %all-to-all-start.5 = ((bf16[16,256,128]{2,1,0:T(8,128)(2,1)}), bf16[16,256,128]{2,1,0:T(8,128)(2,1)S(1)}, u32[]{:S(2)}, u32[]{:S(2)}) async-start(bf16[16,256,128]{2,1,0:T(8,128)(2,1)} %broadcast_in_dim.17), calls=%async_computation.5 | async-start | bytes 2097152 | tf_op jit(solution)/shard_map/all_to_all | solution.py:379
  105.0 2.8 %shard_map.96 = (f32[64,128]{1,0:T(8,128)S(1)}, bf16[32,14336]{1,0:T(8,128)(2,1)S(1)}, bf16[32,14336]{1,0:T(8,128)(2,1)S(1)}) custom-call(bf16[256,128]{1,0:T(8,128)(2,1)S(1)} %bitcast.11, f32[16,128]{1,0:T(8,128)S(1)} %get-tuple-element.33.kept_ref, bf16[32,128]{1,0:T(8,128)(2,1)S(1)} %get-tuple-element.34.left_ref, bf16[1,32,14336]{2,1,0:T(8,128)(2,1)} %gg_ref.5, ...), custom_call_target="tpu_custom_call" | custom-call | flops 67108864 | bytes 4194304 | tf_op jit(solution)/shard_map/pallas_call | solution.py:356
  107.8 7.1 %collective-permute-start.1 = (f32[64,128]{1,0:T(8,128)S(1)}, f32[64,128]{1,0:T(8,128)S(1)}, u32[]{:S(2)}, u32[]{:S(2)}) collective-permute-start(f32[64,128]{1,0:T(8,128)S(1)} %get-tuple-element.35.own_ref), channel_id=1, source_target_pairs={{0,256},{256,0},{1,257},{257,1},{2,258},{258,2},{3,259},{259,3},{4... | collective-permute-start | bytes 98312 | tf_op jit(solution)/shard_map/ppermute | solution.py:440
  114.9 0.8 collective-permute-done.1.other_ref
  115.8 1.5 %all-to-all-done.5 = bf16[16,256,128]{2,1,0:T(8,128)(2,1)S(1)} async-done(((bf16[16,256,128]{2,1,0:T(8,128)(2,1)}), bf16[16,256,128]{2,1,0:T(8,128)(2,1)S(1)}, u32[]{:S(2)}, u32[]{:S(2)}) %all-to-all-start.5) | async-done | bytes 1048608 | tf_op jit(solution)/shard_map/all_to_all | solution.py:379
  117.2 7.5 %collective-permute-start.2 = (bf16[4096,128]{1,0:T(8,128)(2,1)S(1)}, bf16[4096,128]{1,0:T(8,128)(2,1)S(1)}, u32[]{:S(2)}, u32[]{:S(2)}) collective-permute-start(bf16[4096,128]{1,0:T(8,128)(2,1)S(1)} %bitcast.7), channel_id=1, source_target_pairs={{0,256},{256,0},{1,257},{257,1},{2,258},{258,2},{3,259},{259,3},{4... | collective-permute-start | bytes 3145736 | tf_op jit(solution)/shard_map/ppermute | solution.py:442
  124.7 2.5 %shard_map.97 = (f32[32,56]{1,0:T(8,128)}, f32[32,56]{1,0:T(8,128)}, f32[32,32]{1,0:T(8,128)}, f32[32,32]{1,0:T(8,128)}, bf16[1,32,14336]{2,1,0:T(8,128)(2,1)}, /*index=5*/bf16[1,32,14336]{2,1,0:T(8,128)(2,1)}) custom-call(bf16[4096,128]{1,0:T(8,128)(2,1)S(1)} %bitcast.8, f32[64,128]{1,0:T(8,128)S(1)} %get-tuple-element.35.own_ref, ...), custom_call_target="tpu_custom_call" | custom-call | flops 67108864 | bytes 4194304 | tf_op jit(solution)/shard_map/pallas_call | solution.py:356
  127.2 0.0 collective-permute-done.2.sums_ref
  127.2 1.9 %shard_map.98 = (bf16[1,32,14336]{2,1,0:T(8,128)(2,1)}, bf16[1,32,14336]{2,1,0:T(8,128)(2,1)}) custom-call(bf16[4096,128]{1,0:T(8,128)(2,1)S(1)} %collective-permute-done.2.sums_ref, f32[64,128]{1,0:T(8,128)S(1)} %collective-permute-done.1.other_ref, bf16[32,14336]{1,0:T(8,128)(2,1)S(1)} %get-tuple-element.43.grad, ...), custom_call_target="tpu_custom_call", output_to_operand_aliasing={{0}: (3, {}), {1}: (4, {})} | custom-call | flops 67108864 | bytes 4194304 | tf_op jit(solution)/shard_map/pallas_call | solution.py:356
  (1 shorter events, 0.0 us)
Async XLA Ops:
  30.4 20.2 %all-to-all-start.1 = ((bf16[16,256,128]{2,1,0:T(8,128)(2,1)}), bf16[16,256,128]{2,1,0:T(8,128)(2,1)S(1)}, u32[]{:S(2)}, u32[]{:S(2)}) async-start(bf16[16,256,128]{2,1,0:T(8,128)(2,1)} %broadcast_in_dim.15), calls=%async_computation.1 | async-start | bytes 2097152 | tf_op jit(solution)/shard_map/all_to_all | solution.py:379
  35.6 6.3 %collective-permute-start = (bf16[32,14336]{1,0:T(8,128)(2,1)S(1)}, bf16[32,14336]{1,0:T(8,128)(2,1)S(1)}, u32[]{:S(2)}, u32[]{:S(2)}) collective-permute-start(bf16[32,14336]{1,0:T(8,128)(2,1)S(1)} %get-tuple-element.28), channel_id=1, source_target_pairs={{0,256},{256,0},{1,257},{257,1},{2,258},{258,2},{3,259},{259,3},{4... | collective-permute-start | bytes 2752520 | tf_op jit(solution)/shard_map/ppermute | solution.py:397
  101.3 15.9 %all-to-all-start.5 = ((bf16[16,256,128]{2,1,0:T(8,128)(2,1)}), bf16[16,256,128]{2,1,0:T(8,128)(2,1)S(1)}, u32[]{:S(2)}, u32[]{:S(2)}) async-start(bf16[16,256,128]{2,1,0:T(8,128)(2,1)} %broadcast_in_dim.17), calls=%async_computation.5 | async-start | bytes 2097152 | tf_op jit(solution)/shard_map/all_to_all | solution.py:379
  107.8 8.0 %collective-permute-start.1 = (f32[64,128]{1,0:T(8,128)S(1)}, f32[64,128]{1,0:T(8,128)S(1)}, u32[]{:S(2)}, u32[]{:S(2)}) collective-permute-start(f32[64,128]{1,0:T(8,128)S(1)} %get-tuple-element.35.own_ref), channel_id=1, source_target_pairs={{0,256},{256,0},{1,257},{257,1},{2,258},{258,2},{3,259},{259,3},{4... | collective-permute-start | bytes 98312 | tf_op jit(solution)/shard_map/ppermute | solution.py:440
  117.2 10.0 %collective-permute-start.2 = (bf16[4096,128]{1,0:T(8,128)(2,1)S(1)}, bf16[4096,128]{1,0:T(8,128)(2,1)S(1)}, u32[]{:S(2)}, u32[]{:S(2)}) collective-permute-start(bf16[4096,128]{1,0:T(8,128)(2,1)S(1)} %bitcast.7), channel_id=1, source_target_pairs={{0,256},{256,0},{1,257},{257,1},{2,258},{258,2},{3,259},{259,3},{4... | collective-permute-start | bytes 3145736 | tf_op jit(solution)/shard_map/ppermute | solution.py:442

commit v6 on v5

--- a/solution.py
+++ b/solution.py
@@ -8,9 +8,9 @@
 from jax.sharding import Mesh
 from jax.sharding import PartitionSpec as P
 
-ROW = ("yq", "yp", "zq", "zp", "x")
-NEAR = ("yp", "zp", "x")
-FAR = ("yq", "zq")
+ROW = ("yq", "yp", "zq", "zp", "xq", "xp")
+ALL = ("outer", *ROW)
+FAR = ("yq", "zq", "xq")
 BF = jnp.bfloat16
 F32 = jnp.float32
 R = 32
@@ -22,13 +22,40 @@
 
 
 def place(d, sizes):
-    _, yp, zq, zp, x = sizes
-    at_x, d = d % x, d // x
-    at_zp, d = d % zp, d // zp
-    at_zq, d = d % zq, d // zq
-    at_yp, at_yq = d % yp, d // yp
-    near = (at_yp * zp + at_zp) * x + at_x
-    return (near * sizes[0] + at_yq) * zq + at_zq
+    at = []
+    for size in sizes[::-1]:
+        at.append(d % size)
+        d = d // size
+    xp, xq, zp, zq, yp, yq = at
+    near = (yp * sizes[3] + zp) * sizes[5] + xp
+    return ((near * sizes[0] + yq) * sizes[2] + zq) * sizes[4] + xq
+
+
+def near_groups(sizes):
+    rows = sizes[0] * sizes[1], sizes[2] * sizes[3], sizes[4] * sizes[5]
+    found = []
+    for core in range(2):
+        lines = []
+        for n, (many, few) in zip(rows, (sizes[0:2], sizes[2:4], sizes[4:6])):
+            shift = core if few == 2 else 0
+            lines.append(
+                [
+                    sorted(((few * q + i + shift) % n for i in range(few)), key=lambda v: v % few)
+                    for q in range(many)
+                ]
+            )
+        for ys in lines[0]:
+            for zs in lines[1]:
+                for xs in lines[2]:
+                    found.append(
+                        [
+                            ((core * rows[0] + y) * rows[1] + z) * rows[2] + x
+                            for y in ys
+                            for z in zs
+                            for x in xs
+                        ]
+                    )
+    return found
 
 
 def groups(shape):
@@ -147,10 +174,11 @@
     row = lax.broadcasted_iota(jnp.int32, (TILE, 128), 0)
     empty = jnp.zeros((TILE, 128), F32)
     extra = []
-    for a in range(R // 2):
+    each = R // far
+    for f in range(far):
         tile = empty
-        for s in range(6):
-            at = 2 * a + s // 3
+        for s in range(3 * each):
+            at = each * f + s // 3
             tile = jnp.where(row == s, terms[s % 3][at : at + 1], tile)
         extra.append(tile)
     tiles = []
@@ -206,7 +234,7 @@
 
 
 def solve_kernel(
-    line_ref, kept_ref, left_ref, gg_ref, gu_ref, out_ref, grad_ref, other_grad_ref, tiles, grams, sem
+    far, line_ref, kept_ref, left_ref, gg_ref, gu_ref, out_ref, grad_ref, other_grad_ref, tiles, grams, sem
 ):
     core = lax.axis_index("outer")
     pick(core, gg_ref.at[0], gu_ref.at[0], grad_ref, sem.at[0], True)
@@ -215,14 +243,14 @@
     group = groups((R, 128))
     row = lax.broadcasted_iota(jnp.int32, (R, 128), 0)
     lane = lax.broadcasted_iota(jnp.int32, (R, 128), 1)
-    half = R // 2
-    for f in range(half):
+    each = R // far
+    for f in range(far):
         tiles[8 * f : 8 * f + 8] = line_ref[16 * f : 16 * f + 16].astype(F32)[8:16]
-    for odd in range(2):
-        gram = tiles[pl.ds(3 * odd, half, stride=8), :]
+    for i in range(each):
+        gram = tiles[pl.ds(3 * i, far, stride=8), :]
         for s in range(1, 3):
-            gram = gram + tiles[pl.ds(3 * odd + s, half, stride=8), :]
-        grams[pl.ds(odd, half, stride=2), :] = gram
+            gram = gram + tiles[pl.ds(3 * i + s, far, stride=8), :]
+        grams[pl.ds(i, far, stride=each), :] = gram
     m = jnp.where(group == 0, pltpu.roll(grams[...], 32, 1), 0.0)
     m = jnp.where((group == 1) & (row == lane % R), 1.0, m)
     pivots = jnp.ones((R, 128), F32)
@@ -260,6 +288,7 @@
     pick(core, gu_ref.at[0], gg_ref.at[0], other_grad_ref, sem.at[1], False)
 
 
+SIZES = (4, 2, 4, 2, 2, 2)
 CUTS = (4, 7, 8)
 
 
@@ -369,21 +398,26 @@
 
 def local(grad_gate, grad_up, basis_gate, basis_up):
     sizes = tuple(lax.axis_size(a) for a in ROW)
-    near, far = lax.axis_size(NEAR), lax.axis_size(FAR)
+    far = lax.axis_size(FAR)
+    near = sizes[1] * sizes[3] * sizes[5]
+    pairs = near_groups(sizes)
     columns = grad_gate.shape[2]
     packed_rows = 16 * near * far
     swap = [(0, 1), (1, 0)]
     dma = pltpu.SemaphoreType.DMA
 
-    def exchange(x, axes):
-        return lax.all_to_all(x, axes, 0, 0, tiled=True)
+    def exchange_far(x):
+        return lax.all_to_all(x, FAR, 0, 0, tiled=True)
+
+    def exchange_near(x):
+        return lax.all_to_all(x, ALL, 0, 0, tiled=True, axis_index_groups=pairs)
 
     def gather_far(block):
-        return exchange(block, FAR).reshape(16 * far, 128)
+        return exchange_far(block).reshape(16 * far, 128)
 
     def gather_near(line):
         copies = jnp.broadcast_to(line[None], (near, 16 * far, 128))
-        return exchange(copies, NEAR).reshape(packed_rows, 128)
+        return exchange_near(copies).reshape(packed_rows, 128)
 
     block, send = call(
         prepare_kernel,
@@ -414,9 +448,9 @@
         1 << 26,
         16,
     )(basis, turned, packed)
-    parts = exchange(sums.reshape(near, 16 * far, 128), NEAR)
+    parts = exchange_near(sums.reshape(near, 16 * far, 128))
     (halfway,) = call(halfway_kernel, (shape((16 * far, 128), BF),), [], "v", "v", 1 << 20, 8)(parts)
-    parts = exchange(halfway.reshape(far, 16, 128), FAR)
+    parts = exchange_far(halfway.reshape(far, 16, 128))
     block, kept = call(
         total_kernel,
         (shape((far, 16, 128), BF), shape((16, 128), F32)),
@@ -429,9 +463,9 @@
     line = gather_far(block)
     natural = shape((R, columns), BF)
     own, own_grad, other_grad = call(
-        solve_kernel,
+        functools.partial(solve_kernel, far),
         (shape((2 * R, 128), F32), natural, natural),
-        [pltpu.VMEM((128, 128), F32), pltpu.VMEM((R, 128), F32), dma((2,))],
+        [pltpu.VMEM((8 * far, 128), F32), pltpu.VMEM((R, 128), F32), dma((2,))],
         "vvvhh",
         "vvv",
         1 << 26,
@@ -466,7 +500,7 @@
 
 def solution(mesh):
     rows = mesh.shape["row"]
-    sizes = (4, 2, 4, 2, 4) if rows == 256 else (4, 1, 4, 1, rows // 16)
+    sizes = SIZES if rows == 256 else (2, 2, 4, 1, 2, rows // 32)
     finer = Mesh(mesh.devices.reshape(mesh.shape["outer"], *sizes), ("outer", *ROW))
     return jax.shard_map(
         local,

time: 130 us -> 134 us (1.031)
  blocking collectives: 73.8 us -> 88.3 us
  starting transfers between devices: 27.7 us -> 14.9 us
  waiting for transfers between devices: 6.68 us -> 9.65 us
    all_to_all x4, blocking collectives: 73.8 us -> 88.3 us  [the longest x3 68.8 us: exchange_far(): return lax.all_to_all(x, FAR, 0, 0, tiled=True)]
    ppermute x1, starting transfers between devices: 7.49 us -> 1.91 us  [local(): sums_other = lax.ppermute(sums, 'outer', swap)]
    ppermute x1, starting transfers between devices: 7.13 us -> 1.92 us  [local(): other = lax.ppermute(own, 'outer', swap)]
    all_to_all x2, waiting for transfers between devices: 3.76 us -> 6.29 us  [exchange_near(): return lax.all_to_all(x, ALL, 0, 0, tiled=True, axis_index_groups=pairs)]
    all_to_all x2, starting transfers between devices: 8.84 us -> 7.11 us  [exchange_near(): return lax.all_to_all(x, ALL, 0, 0, tiled=True, axis_index_groups=pairs)]
where the time goes in v6:
time: 134 us
  blocking collectives  88.3 us (66%)
  Pallas kernels  18 us (13%)
  starting transfers between devices  14.9 us (11%)
  waiting for transfers between devices  9.65 us (7%)
  local copies, waits for them, and re-layouts  2.21 us (2%)
    all_to_all x3, blocking collectives, exchange_far(): return lax.all_to_all(x, FAR, 0, 0, tiled=True)  68.8 us
    all_to_all x1, blocking collectives, exchange_near(): return lax.all_to_all(x, ALL, 0, 0, tiled=True, axis_index_groups=pairs)  19.6 us
    pallas_call x8, Pallas kernels, pinned(): run(*(pltpu.with_memory_space_constraint(x, pltpu.HBM) if s == 'h' and (n...  18 us
    all_to_all x2, starting transfers between devices, exchange_near(): return lax.all_to_all(x, ALL, 0, 0, tiled=True, axis_index_groups=pairs)  7.11 us
    all_to_all x2, waiting for transfers between devices, exchange_near(): return lax.all_to_all(x, ALL, 0, 0, tiled=True, axis_index_groups=pairs)  6.29 us
    ppermute x1, starting transfers between devices, local(): other = lax.ppermute(send, 'outer', swap)  3.92 us
  transfers between devices with their start and end apart: 5, of which 4 were waited for; matrix products, arithmetic and copies ran while one was open for 0% of the time, Pallas kernels for 9%

profile of v6, /device:TPU:1, one launch (start us, length us, event | category | flops | bytes accessed | tf_op | source)
XLA Modules:
  0.0 133.8 jit_solution(7553812309485224847)
XLA Ops:
  0.6 1.2 shard_map.91
  1.9 32.4 %all_to_all.30 = bf16[32,16,128]{2,1,0:T(8,128)(2,1)S(1)} all-to-all(bf16[32,16,128]{2,1,0:T(8,128)(2,1)S(1)} %get-tuple-element.27), channel_id=1, replica_groups=mesh['outer'=2,'yq'=4,'yp'=2,'zq'=4,'zp'=2,'xq'=2,'xp'=2] {'yq','zq','xq'}, dimensions={0} | all-to-all | bytes 262144 | tf_op jit(solution)/shard_map/all_to_all | solution.py:410
  34.2 1.1 broadcast_in_dim.15
  35.3 3.6 %all-to-all-start.1 = ((bf16[8,512,128]{2,1,0:T(8,128)(2,1)}), bf16[8,512,128]{2,1,0:T(8,128)(2,1)S(1)}, u32[]{:S(2)}, u32[]{:S(2)}) async-start(bf16[8,512,128]{2,1,0:T(8,128)(2,1)} %broadcast_in_dim.15), calls=%async_computation.1 | async-start | bytes 2097152 | tf_op jit(solution)/shard_map/all_to_all | solution.py:413
  38.9 3.9 %collective-permute-start = (bf16[32,14336]{1,0:T(8,128)(2,1)S(1)}, bf16[32,14336]{1,0:T(8,128)(2,1)S(1)}, u32[]{:S(2)}, u32[]{:S(2)}) collective-permute-start(bf16[32,14336]{1,0:T(8,128)(2,1)S(1)} %get-tuple-element.28), channel_id=1, source_target_pairs={{0,256},{256,0},{1,257},{257,1},{2,258},{258,2},{3,259},{259,3},{4... | collective-permute-start | bytes 2752520 | tf_op jit(solution)/shard_map/ppermute | solution.py:431
  42.8 2.1 %collective-permute-done.other_ref = bf16[32,14336]{1,0:T(8,128)(2,1)S(1)} collective-permute-done((bf16[32,14336]{1,0:T(8,128)(2,1)S(1)}, bf16[32,14336]{1,0:T(8,128)(2,1)S(1)}, u32[]{:S(2)}, u32[]{:S(2)}) %collective-permute-start) | collective-permute-done | bytes 917536 | tf_op jit(solution)/shard_map/ppermute | solution.py:431
  44.9 6.3 %shard_map.92 = (bf16[4096,256]{1,0:T(8,128)(2,1)}, bf16[256,4096]{1,0:T(8,128)(2,1)S(1)}) custom-call(bf16[1,32,14336]{2,1,0:T(8,128)(2,1)} %gg_ref.5, bf16[1,32,14336]{2,1,0:T(8,128)(2,1)} %gu_ref.5, bf16[32,14336]{1,0:T(8,128)(2,1)S(1)} %collective-permute-done.other_ref), custom_call_target="tpu_custom_call" | custom-call | flops 67108864 | bytes 4194304 | tf_op jit(solution)/shard_map/pallas_call | solution.py:385
  51.2 0.0 all-to-all-done.1
  51.2 2.8 %shard_map.93 = (bf16[4096,128]{1,0:T(8,128)(2,1)S(1)}, bf16[32,128]{1,0:T(8,128)(2,1)S(1)}) custom-call(bf16[4096,128]{1,0:T(8,128)(2,1)S(1)} %bitcast.6, bf16[256,4096]{1,0:T(8,128)(2,1)S(1)} %get-tuple-element.29.turned_ref, bf16[4096,256]{1,0:T(8,128)(2,1)} %get-tuple-element.30.packed_ref), custom_call_target="tpu_custom_call" | custom-call | flops 67108864 | bytes 4194304 | tf_op jit(solution)/shard_map/pallas_call | solution.py:385
  54.1 19.6 %all_to_all.31.parts_ref = bf16[8,512,128]{2,1,0:T(8,128)(2,1)S(1)} all-to-all(bf16[8,512,128]{2,1,0:T(8,128)(2,1)S(1)} %bitcast.11), channel_id=1, replica_groups={{0,1,4,5,32,33,36,37},{2,3,6,7,34,35,38,39},{8,9,12,13,40,41,44,45},{10..., dimensions={0} | all-to-all | bytes 2097152 | tf_op jit(solution)/shard_map/all_to_all | solution.py:413
  73.6 0.3 shard_map.94
  74.0 19.8 %all_to_all.32.parts_ref = bf16[32,16,128]{2,1,0:T(8,128)(2,1)S(1)} all-to-all(bf16[32,16,128]{2,1,0:T(8,128)(2,1)S(1)} %bitcast.12), channel_id=1, replica_groups=mesh['outer'=2,'yq'=4,'yp'=2,'zq'=4,'zp'=2,'xq'=2,'xp'=2] {'yq','zq','xq'}, dimensions={0} | all-to-all | bytes 262144 | tf_op jit(solution)/shard_map/all_to_all | solution.py:410
  93.8 0.1 shard_map.95
  93.9 16.6 %all_to_all.33 = bf16[32,16,128]{2,1,0:T(8,128)(2,1)S(1)} all-to-all(bf16[32,16,128]{2,1,0:T(8,128)(2,1)S(1)} %get-tuple-element.32), channel_id=1, replica_groups=mesh['outer'=2,'yq'=4,'yp'=2,'zq'=4,'zp'=2,'xq'=2,'xp'=2] {'yq','zq','xq'}, dimensions={0} | all-to-all | bytes 262144 | tf_op jit(solution)/shard_map/all_to_all | solution.py:410
  110.5 1.1 broadcast_in_dim.17
  111.6 3.6 %all-to-all-start.5 = ((bf16[8,512,128]{2,1,0:T(8,128)(2,1)}), bf16[8,512,128]{2,1,0:T(8,128)(2,1)S(1)}, u32[]{:S(2)}, u32[]{:S(2)}) async-start(bf16[8,512,128]{2,1,0:T(8,128)(2,1)} %broadcast_in_dim.17), calls=%async_computation.5 | async-start | bytes 2097152 | tf_op jit(solution)/shard_map/all_to_all | solution.py:413
  115.1 2.8 %shard_map.96 = (f32[64,128]{1,0:T(8,128)S(1)}, bf16[32,14336]{1,0:T(8,128)(2,1)S(1)}, bf16[32,14336]{1,0:T(8,128)(2,1)S(1)}) custom-call(bf16[512,128]{1,0:T(8,128)(2,1)S(1)} %bitcast.10, f32[16,128]{1,0:T(8,128)S(1)} %get-tuple-element.33.kept_ref, bf16[32,128]{1,0:T(8,128)(2,1)S(1)} %get-tuple-element.34.left_ref, bf16[1,32,14336]{2,1,0:T(8,128)(2,1)} %gg_ref.5, ...), custom_call_target="tpu_custom_call" | custom-call | flops 67108864 | bytes 4194304 | tf_op jit(solution)/shard_map/pallas_call | solution.py:385
  118.0 1.9 %collective-permute-start.1 = (f32[64,128]{1,0:T(8,128)S(1)}, f32[64,128]{1,0:T(8,128)S(1)}, u32[]{:S(2)}, u32[]{:S(2)}) collective-permute-start(f32[64,128]{1,0:T(8,128)S(1)} %get-tuple-element.35.own_ref), channel_id=1, source_target_pairs={{0,256},{256,0},{1,257},{257,1},{2,258},{258,2},{3,259},{259,3},{4... | collective-permute-start | bytes 98312 | tf_op jit(solution)/shard_map/ppermute | solution.py:474
  119.9 1.2 collective-permute-done.1.other_ref
  121.1 6.3 %all-to-all-done.5 = bf16[8,512,128]{2,1,0:T(8,128)(2,1)S(1)} async-done(((bf16[8,512,128]{2,1,0:T(8,128)(2,1)}), bf16[8,512,128]{2,1,0:T(8,128)(2,1)S(1)}, u32[]{:S(2)}, u32[]{:S(2)}) %all-to-all-start.5) | async-done | bytes 1048608 | tf_op jit(solution)/shard_map/all_to_all | solution.py:413
  127.3 1.9 %collective-permute-start.2 = (bf16[4096,128]{1,0:T(8,128)(2,1)S(1)}, bf16[4096,128]{1,0:T(8,128)(2,1)S(1)}, u32[]{:S(2)}, u32[]{:S(2)}) collective-permute-start(bf16[4096,128]{1,0:T(8,128)(2,1)S(1)} %bitcast.7), channel_id=1, source_target_pairs={{0,256},{256,0},{1,257},{257,1},{2,258},{258,2},{3,259},{259,3},{4... | collective-permute-start | bytes 3145736 | tf_op jit(solution)/shard_map/ppermute | solution.py:476
  129.3 2.5 %shard_map.97 = (f32[32,56]{1,0:T(8,128)}, f32[32,56]{1,0:T(8,128)}, f32[32,32]{1,0:T(8,128)}, f32[32,32]{1,0:T(8,128)}, bf16[1,32,14336]{2,1,0:T(8,128)(2,1)}, /*index=5*/bf16[1,32,14336]{2,1,0:T(8,128)(2,1)}) custom-call(bf16[4096,128]{1,0:T(8,128)(2,1)S(1)} %bitcast.8, f32[64,128]{1,0:T(8,128)S(1)} %get-tuple-element.35.own_ref, ...), custom_call_target="tpu_custom_call" | custom-call | flops 67108864 | bytes 4194304 | tf_op jit(solution)/shard_map/pallas_call | solution.py:385
  131.8 0.1 collective-permute-done.2.sums_ref
  131.9 1.9 %shard_map.98 = (bf16[1,32,14336]{2,1,0:T(8,128)(2,1)}, bf16[1,32,14336]{2,1,0:T(8,128)(2,1)}) custom-call(bf16[4096,128]{1,0:T(8,128)(2,1)S(1)} %collective-permute-done.2.sums_ref, f32[64,128]{1,0:T(8,128)S(1)} %collective-permute-done.1.other_ref, bf16[32,14336]{1,0:T(8,128)(2,1)S(1)} %get-tuple-element.43.grad, ...), custom_call_target="tpu_custom_call", output_to_operand_aliasing={{0}: (3, {}), {1}: (4, {})} | custom-call | flops 67108864 | bytes 4194304 | tf_op jit(solution)/shard_map/pallas_call | solution.py:385
Async XLA Ops:
  35.3 15.9 %all-to-all-start.1 = ((bf16[8,512,128]{2,1,0:T(8,128)(2,1)}), bf16[8,512,128]{2,1,0:T(8,128)(2,1)S(1)}, u32[]{:S(2)}, u32[]{:S(2)}) async-start(bf16[8,512,128]{2,1,0:T(8,128)(2,1)} %broadcast_in_dim.15), calls=%async_computation.1 | async-start | bytes 2097152 | tf_op jit(solution)/shard_map/all_to_all | solution.py:413
  38.9 6.0 %collective-permute-start = (bf16[32,14336]{1,0:T(8,128)(2,1)S(1)}, bf16[32,14336]{1,0:T(8,128)(2,1)S(1)}, u32[]{:S(2)}, u32[]{:S(2)}) collective-permute-start(bf16[32,14336]{1,0:T(8,128)(2,1)S(1)} %get-tuple-element.28), channel_id=1, source_target_pairs={{0,256},{256,0},{1,257},{257,1},{2,258},{258,2},{3,259},{259,3},{4... | collective-permute-start | bytes 2752520 | tf_op jit(solution)/shard_map/ppermute | solution.py:431
  111.6 15.8 %all-to-all-start.5 = ((bf16[8,512,128]{2,1,0:T(8,128)(2,1)}), bf16[8,512,128]{2,1,0:T(8,128)(2,1)S(1)}, u32[]{:S(2)}, u32[]{:S(2)}) async-start(bf16[8,512,128]{2,1,0:T(8,128)(2,1)} %broadcast_in_dim.17), calls=%async_computation.5 | async-start | bytes 2097152 | tf_op jit(solution)/shard_map/all_to_all | solution.py:413
  118.0 3.1 %collective-permute-start.1 = (f32[64,128]{1,0:T(8,128)S(1)}, f32[64,128]{1,0:T(8,128)S(1)}, u32[]{:S(2)}, u32[]{:S(2)}) collective-permute-start(f32[64,128]{1,0:T(8,128)S(1)} %get-tuple-element.35.own_ref), channel_id=1, source_target_pairs={{0,256},{256,0},{1,257},{257,1},{2,258},{258,2},{3,259},{259,3},{4... | collective-permute-start | bytes 98312 | tf_op jit(solution)/shard_map/ppermute | solution.py:474
  127.3 4.5 %collective-permute-start.2 = (bf16[4096,128]{1,0:T(8,128)(2,1)S(1)}, bf16[4096,128]{1,0:T(8,128)(2,1)S(1)}, u32[]{:S(2)}, u32[]{:S(2)}) collective-permute-start(bf16[4096,128]{1,0:T(8,128)(2,1)S(1)} %bitcast.7), channel_id=1, source_target_pairs={{0,256},{256,0},{1,257},{257,1},{2,258},{258,2},{3,259},{259,3},{4... | collective-permute-start | bytes 3145736 | tf_op jit(solution)/shard_map/ppermute | solution.py:476

commit v7 on v6

--- a/solution.py
+++ b/solution.py
@@ -217,6 +217,14 @@
     out = summed(parts_ref, 0.5)
     block_ref[...] = jnp.broadcast_to(out.astype(BF)[None], block_ref.shape)
     kept_ref[...] = out
+
+
+def copies_kernel(line_ref, out_ref, sem):
+    copies = [pltpu.make_async_copy(line_ref, out_ref.at[k], sem.at[k]) for k in range(out_ref.shape[0])]
+    for copy in copies:
+        copy.start()
+    for copy in copies:
+        copy.wait()
 
 
 def pick(core, first, second, to, sem, start):
@@ -288,7 +296,7 @@
     pick(core, gu_ref.at[0], gg_ref.at[0], other_grad_ref, sem.at[1], False)
 
 
-SIZES = (4, 2, 4, 2, 2, 2)
+SIZES = (4, 2, 4, 2, 1, 4)
 CUTS = (4, 7, 8)
 
 
@@ -416,7 +424,8 @@
         return exchange_far(block).reshape(16 * far, 128)
 
     def gather_near(line):
-        copies = jnp.broadcast_to(line[None], (near, 16 * far, 128))
+        outs = (shape((near, 16 * far, 128), BF),)
+        (copies,) = call(copies_kernel, outs, [dma((near,))], "v", "h", 1 << 20, 2)(line)
         return exchange_near(copies).reshape(packed_rows, 128)
 
     block, send = call(

time: 134 us -> 136 us (1.015)
  blocking collectives: 88.3 us -> 81.7 us
  starting transfers between devices: 14.9 us -> 21.3 us
  local copies, waits for them, and re-layouts: 2.21 us -> 0 us
  Pallas kernels: 18 us -> 20.1 us
  waiting for transfers between devices: 9.65 us -> 11.3 us
    all_to_all x3, blocking collectives: 68.8 us -> 60.3 us  [exchange_far(): return lax.all_to_all(x, FAR, 0, 0, tiled=True)]
    ppermute x1, starting transfers between devices: 1.91 us -> 4.36 us  [local(): sums_other = lax.ppermute(sums, 'outer', swap)]
    broadcast_in_dim x2 -> x0, local copies, waits for them, and re-layouts: 2.21 us -> none  [gather_near(): copies = jnp.broadcast_to(line[None], (near, 16 * far, 128))]
    pallas_call x8 -> x10, Pallas kernels: 18 us -> 20.1 us  [pinned(): run(*(pltpu.with_memory_space_constraint(x, pltpu.HBM) if s == 'h' and (n...]
    all_to_all x2, waiting for transfers between devices: 6.29 us -> 8.33 us  [exchange_near(): return lax.all_to_all(x, ALL, 0, 0, tiled=True, axis_index_groups=pairs)]
    ppermute x1, starting transfers between devices: 1.92 us -> 3.81 us  [local(): other = lax.ppermute(own, 'outer', swap)]
    all_to_all x1, blocking collectives: 19.6 us -> 21.4 us  [exchange_near(): return lax.all_to_all(x, ALL, 0, 0, tiled=True, axis_index_groups=pairs)]
where the time goes in v7:
time: 136 us; the launch traced here: 135 us
  blocking collectives  81.7 us (60%)
  starting transfers between devices  21.3 us (16%)
  Pallas kernels  20.1 us (15%)
  waiting for transfers between devices  11.3 us (8%)
    all_to_all x3, blocking collectives, exchange_far(): return lax.all_to_all(x, FAR, 0, 0, tiled=True)  60.3 us
    all_to_all x1, blocking collectives, exchange_near(): return lax.all_to_all(x, ALL, 0, 0, tiled=True, axis_index_groups=pairs)  21.4 us
    pallas_call x10, Pallas kernels, pinned(): run(*(pltpu.with_memory_space_constraint(x, pltpu.HBM) if s == 'h' and (n...  20.1 us
    all_to_all x2, starting transfers between devices, exchange_near(): return lax.all_to_all(x, ALL, 0, 0, tiled=True, axis_index_groups=pairs)  8.4 us
    all_to_all x2, waiting for transfers between devices, exchange_near(): return lax.all_to_all(x, ALL, 0, 0, tiled=True, axis_index_groups=pairs)  8.33 us
    ppermute x1, starting transfers between devices, local(): other = lax.ppermute(send, 'outer', swap)  4.7 us
    ppermute x1, starting transfers between devices, local(): sums_other = lax.ppermute(sums, 'outer', swap)  4.36 us
    ppermute x1, starting transfers between devices, local(): other = lax.ppermute(own, 'outer', swap)  3.81 us
  transfers between devices with their start and end apart: 5, of which 4 were waited for; matrix products, arithmetic and copies ran while one was open for 0% of the time, Pallas kernels for 9%

profile of v7, /device:TPU:1, one launch (start us, length us, event | category | flops | bytes accessed | tf_op | source)
XLA Modules:
  0.0 135.1 jit_solution(16785925028933283506)
XLA Ops:
  0.6 1.2 shard_map.91
  1.9 27.3 %all_to_all.30 = bf16[16,16,128]{2,1,0:T(8,128)(2,1)S(1)} all-to-all(bf16[16,16,128]{2,1,0:T(8,128)(2,1)S(1)} %get-tuple-element.27), channel_id=1, replica_groups=mesh['outer'=2,'yq'=4,'yp'=2,'zq'=4,'zp'=2,'xq'=1,'xp'=4] {'yq','zq','xq'}, dimensions={0} | all-to-all | bytes 131072 | tf_op jit(solution)/shard_map/all_to_all | solution.py:418
  29.2 1.1 shard_map.92
  30.3 4.7 %all-to-all-start.1 = ((bf16[16,256,128]{2,1,0:T(8,128)(2,1)}), bf16[16,256,128]{2,1,0:T(8,128)(2,1)S(1)}, u32[]{:S(2)}, u32[]{:S(2)}) async-start(bf16[16,256,128]{2,1,0:T(8,128)(2,1)} %shard_map.92), calls=%async_computation.1 | async-start | bytes 2097152 | tf_op jit(solution)/shard_map/all_to_all | solution.py:421
  35.1 4.7 %collective-permute-start = (bf16[32,14336]{1,0:T(8,128)(2,1)S(1)}, bf16[32,14336]{1,0:T(8,128)(2,1)S(1)}, u32[]{:S(2)}, u32[]{:S(2)}) collective-permute-start(bf16[32,14336]{1,0:T(8,128)(2,1)S(1)} %get-tuple-element.28), channel_id=1, source_target_pairs={{0,256},{256,0},{1,257},{257,1},{2,258},{258,2},{3,259},{259,3},{4... | collective-permute-start | bytes 2752520 | tf_op jit(solution)/shard_map/ppermute | solution.py:440
  39.8 2.1 %collective-permute-done.other_ref = bf16[32,14336]{1,0:T(8,128)(2,1)S(1)} collective-permute-done((bf16[32,14336]{1,0:T(8,128)(2,1)S(1)}, bf16[32,14336]{1,0:T(8,128)(2,1)S(1)}, u32[]{:S(2)}, u32[]{:S(2)}) %collective-permute-start) | collective-permute-done | bytes 917536 | tf_op jit(solution)/shard_map/ppermute | solution.py:440
  41.9 6.3 %shard_map.93 = (bf16[4096,256]{1,0:T(8,128)(2,1)}, bf16[256,4096]{1,0:T(8,128)(2,1)S(1)}) custom-call(bf16[1,32,14336]{2,1,0:T(8,128)(2,1)} %gg_ref.5, bf16[1,32,14336]{2,1,0:T(8,128)(2,1)} %gu_ref.5, bf16[32,14336]{1,0:T(8,128)(2,1)S(1)} %collective-permute-done.other_ref), custom_call_target="tpu_custom_call" | custom-call | flops 67108864 | bytes 4194304 | tf_op jit(solution)/shard_map/pallas_call | solution.py:393
  48.2 1.7 %all-to-all-done.1 = bf16[16,256,128]{2,1,0:T(8,128)(2,1)S(1)} async-done(((bf16[16,256,128]{2,1,0:T(8,128)(2,1)}), bf16[16,256,128]{2,1,0:T(8,128)(2,1)S(1)}, u32[]{:S(2)}, u32[]{:S(2)}) %all-to-all-start.1) | async-done | bytes 1048608 | tf_op jit(solution)/shard_map/all_to_all | solution.py:421
  49.9 2.8 %shard_map.94 = (bf16[4096,128]{1,0:T(8,128)(2,1)S(1)}, bf16[32,128]{1,0:T(8,128)(2,1)S(1)}) custom-call(bf16[4096,128]{1,0:T(8,128)(2,1)S(1)} %bitcast.6, bf16[256,4096]{1,0:T(8,128)(2,1)S(1)} %get-tuple-element.29.turned_ref, bf16[4096,256]{1,0:T(8,128)(2,1)} %get-tuple-element.30.packed_ref), custom_call_target="tpu_custom_call" | custom-call | flops 67108864 | bytes 4194304 | tf_op jit(solution)/shard_map/pallas_call | solution.py:393
  52.7 21.4 %all_to_all.31.parts_ref = bf16[16,256,128]{2,1,0:T(8,128)(2,1)S(1)} all-to-all(bf16[16,256,128]{2,1,0:T(8,128)(2,1)S(1)} %bitcast.9), channel_id=1, replica_groups={{0,1,2,3,4,5,6,7,32,33,34,35,36,37,38,39},{8,9,10,11,12,13,14,15,40,41,..., dimensions={0} | all-to-all | bytes 2097152 | tf_op jit(solution)/shard_map/all_to_all | solution.py:421
  74.2 0.3 shard_map.95
  74.4 19.0 %all_to_all.32.parts_ref = bf16[16,16,128]{2,1,0:T(8,128)(2,1)S(1)} all-to-all(bf16[16,16,128]{2,1,0:T(8,128)(2,1)S(1)} %bitcast.13), channel_id=1, replica_groups=mesh['outer'=2,'yq'=4,'yp'=2,'zq'=4,'zp'=2,'xq'=1,'xp'=4] {'yq','zq','xq'}, dimensions={0} | all-to-all | bytes 131072 | tf_op jit(solution)/shard_map/all_to_all | solution.py:418
  93.4 14.0 %all_to_all.33 = bf16[16,16,128]{2,1,0:T(8,128)(2,1)S(1)} all-to-all(bf16[16,16,128]{2,1,0:T(8,128)(2,1)S(1)} %get-tuple-element.32), channel_id=1, replica_groups=mesh['outer'=2,'yq'=4,'yp'=2,'zq'=4,'zp'=2,'xq'=1,'xp'=4] {'yq','zq','xq'}, dimensions={0} | all-to-all | bytes 131072 | tf_op jit(solution)/shard_map/all_to_all | solution.py:418
  107.4 1.1 shard_map.97
  108.5 3.7 %all-to-all-start.5 = ((bf16[16,256,128]{2,1,0:T(8,128)(2,1)}), bf16[16,256,128]{2,1,0:T(8,128)(2,1)S(1)}, u32[]{:S(2)}, u32[]{:S(2)}) async-start(bf16[16,256,128]{2,1,0:T(8,128)(2,1)} %shard_map.97), calls=%async_computation.5 | async-start | bytes 2097152 | tf_op jit(solution)/shard_map/all_to_all | solution.py:421
  112.2 2.8 %shard_map.98 = (f32[64,128]{1,0:T(8,128)S(1)}, bf16[32,14336]{1,0:T(8,128)(2,1)S(1)}, bf16[32,14336]{1,0:T(8,128)(2,1)S(1)}) custom-call(bf16[256,128]{1,0:T(8,128)(2,1)S(1)} %bitcast.11, f32[16,128]{1,0:T(8,128)S(1)} %get-tuple-element.33.kept_ref, bf16[32,128]{1,0:T(8,128)(2,1)S(1)} %get-tuple-element.34.left_ref, bf16[1,32,14336]{2,1,0:T(8,128)(2,1)} %gg_ref.5, ...), custom_call_target="tpu_custom_call" | custom-call | flops 67108864 | bytes 4194304 | tf_op jit(solution)/shard_map/pallas_call | solution.py:393
  115.0 3.8 %collective-permute-start.1 = (f32[64,128]{1,0:T(8,128)S(1)}, f32[64,128]{1,0:T(8,128)S(1)}, u32[]{:S(2)}, u32[]{:S(2)}) collective-permute-start(f32[64,128]{1,0:T(8,128)S(1)} %get-tuple-element.35.own_ref), channel_id=1, source_target_pairs={{0,256},{256,0},{1,257},{257,1},{2,258},{258,2},{3,259},{259,3},{4... | collective-permute-start | bytes 98312 | tf_op jit(solution)/shard_map/ppermute | solution.py:483
  118.8 0.8 collective-permute-done.1.other_ref
  119.7 6.6 %all-to-all-done.5 = bf16[16,256,128]{2,1,0:T(8,128)(2,1)S(1)} async-done(((bf16[16,256,128]{2,1,0:T(8,128)(2,1)}), bf16[16,256,128]{2,1,0:T(8,128)(2,1)S(1)}, u32[]{:S(2)}, u32[]{:S(2)}) %all-to-all-start.5) | async-done | bytes 1048608 | tf_op jit(solution)/shard_map/all_to_all | solution.py:421
  126.3 4.4 %collective-permute-start.2 = (bf16[4096,128]{1,0:T(8,128)(2,1)S(1)}, bf16[4096,128]{1,0:T(8,128)(2,1)S(1)}, u32[]{:S(2)}, u32[]{:S(2)}) collective-permute-start(bf16[4096,128]{1,0:T(8,128)(2,1)S(1)} %bitcast.7), channel_id=1, source_target_pairs={{0,256},{256,0},{1,257},{257,1},{2,258},{258,2},{3,259},{259,3},{4... | collective-permute-start | bytes 3145736 | tf_op jit(solution)/shard_map/ppermute | solution.py:485
  130.7 2.5 %shard_map.99 = (f32[32,56]{1,0:T(8,128)}, f32[32,56]{1,0:T(8,128)}, f32[32,32]{1,0:T(8,128)}, f32[32,32]{1,0:T(8,128)}, bf16[1,32,14336]{2,1,0:T(8,128)(2,1)}, /*index=5*/bf16[1,32,14336]{2,1,0:T(8,128)(2,1)}) custom-call(bf16[4096,128]{1,0:T(8,128)(2,1)S(1)} %bitcast.8, f32[64,128]{1,0:T(8,128)S(1)} %get-tuple-element.35.own_ref, ...), custom_call_target="tpu_custom_call" | custom-call | flops 67108864 | bytes 4194304 | tf_op jit(solution)/shard_map/pallas_call | solution.py:393
  133.2 0.0 collective-permute-done.2.sums_ref
  133.2 1.9 %shard_map.100 = (bf16[1,32,14336]{2,1,0:T(8,128)(2,1)}, bf16[1,32,14336]{2,1,0:T(8,128)(2,1)}) custom-call(bf16[4096,128]{1,0:T(8,128)(2,1)S(1)} %collective-permute-done.2.sums_ref, f32[64,128]{1,0:T(8,128)S(1)} %collective-permute-done.1.other_ref, bf16[32,14336]{1,0:T(8,128)(2,1)S(1)} %get-tuple-element.43.grad, ...), custom_call_target="tpu_custom_call", output_to_operand_aliasing={{0}: (3, {}), {1}: (4, {})} | custom-call | flops 67108864 | bytes 4194304 | tf_op jit(solution)/shard_map/pallas_call | solution.py:393
  (1 shorter events, 0.0 us)
Async XLA Ops:
  30.3 19.6 %all-to-all-start.1 = ((bf16[16,256,128]{2,1,0:T(8,128)(2,1)}), bf16[16,256,128]{2,1,0:T(8,128)(2,1)S(1)}, u32[]{:S(2)}, u32[]{:S(2)}) async-start(bf16[16,256,128]{2,1,0:T(8,128)(2,1)} %shard_map.92), calls=%async_computation.1 | async-start | bytes 2097152 | tf_op jit(solution)/shard_map/all_to_all | solution.py:421
  35.1 6.8 %collective-permute-start = (bf16[32,14336]{1,0:T(8,128)(2,1)S(1)}, bf16[32,14336]{1,0:T(8,128)(2,1)S(1)}, u32[]{:S(2)}, u32[]{:S(2)}) collective-permute-start(bf16[32,14336]{1,0:T(8,128)(2,1)S(1)} %get-tuple-element.28), channel_id=1, source_target_pairs={{0,256},{256,0},{1,257},{257,1},{2,258},{258,2},{3,259},{259,3},{4... | collective-permute-start | bytes 2752520 | tf_op jit(solution)/shard_map/ppermute | solution.py:440
  108.5 17.8 %all-to-all-start.5 = ((bf16[16,256,128]{2,1,0:T(8,128)(2,1)}), bf16[16,256,128]{2,1,0:T(8,128)(2,1)S(1)}, u32[]{:S(2)}, u32[]{:S(2)}) async-start(bf16[16,256,128]{2,1,0:T(8,128)(2,1)} %shard_map.97), calls=%async_computation.5 | async-start | bytes 2097152 | tf_op jit(solution)/shard_map/all_to_all | solution.py:421
  115.0 4.7 %collective-permute-start.1 = (f32[64,128]{1,0:T(8,128)S(1)}, f32[64,128]{1,0:T(8,128)S(1)}, u32[]{:S(2)}, u32[]{:S(2)}) collective-permute-start(f32[64,128]{1,0:T(8,128)S(1)} %get-tuple-element.35.own_ref), channel_id=1, source_target_pairs={{0,256},{256,0},{1,257},{257,1},{2,258},{258,2},{3,259},{259,3},{4... | collective-permute-start | bytes 98312 | tf_op jit(solution)/shard_map/ppermute | solution.py:483
  126.3 6.9 %collective-permute-start.2 = (bf16[4096,128]{1,0:T(8,128)(2,1)S(1)}, bf16[4096,128]{1,0:T(8,128)(2,1)S(1)}, u32[]{:S(2)}, u32[]{:S(2)}) collective-permute-start(bf16[4096,128]{1,0:T(8,128)(2,1)S(1)} %bitcast.7), channel_id=1, source_target_pairs={{0,256},{256,0},{1,257},{257,1},{2,258},{258,2},{3,259},{259,3},{4... | collective-permute-start | bytes 3145736 | tf_op jit(solution)/shard_map/ppermute | solution.py:485

commit v8 on v5

--- a/solution.py
+++ b/solution.py
@@ -9,8 +9,8 @@
 from jax.sharding import PartitionSpec as P
 
 ROW = ("yq", "yp", "zq", "zp", "x")
-NEAR = ("yp", "zp", "x")
-FAR = ("yq", "zq")
+NEAR = ("x", "yp", "zp")
+FAR = ("zq", "yq")
 BF = jnp.bfloat16
 F32 = jnp.float32
 R = 32
@@ -27,8 +27,8 @@
     at_zp, d = d % zp, d // zp
     at_zq, d = d % zq, d // zq
     at_yp, at_yq = d % yp, d // yp
-    near = (at_yp * zp + at_zp) * x + at_x
-    return (near * sizes[0] + at_yq) * zq + at_zq
+    near = (at_x * yp + at_yp) * zp + at_zp
+    return (near * zq + at_zq) * sizes[0] + at_yq
 
 
 def groups(shape):

time: 130 us -> 129 us (level)
    ppermute x1, starting transfers between devices: 7.13 us -> 5.8 us  [local(): other = lax.ppermute(own, 'outer', swap)]
where the time goes in v8:
time: 129 us
  blocking collectives  74.8 us (58%)
  starting transfers between devices  26.9 us (21%)
  Pallas kernels  17.9 us (14%)
  waiting for transfers between devices  6.02 us (5%)
  local copies, waits for them, and re-layouts  2.35 us (2%)
    all_to_all x4, blocking collectives, exchange(): return lax.all_to_all(x, axes, 0, 0, tiled=True)  74.8 us
    pallas_call x8, Pallas kernels, pinned(): run(*(pltpu.with_memory_space_constraint(x, pltpu.HBM) if s == 'h' and (n...  17.9 us
    all_to_all x2, starting transfers between devices, exchange(): return lax.all_to_all(x, axes, 0, 0, tiled=True)  10 us
    ppermute x1, starting transfers between devices, local(): sums_other = lax.ppermute(sums, 'outer', swap)  6.84 us
    ppermute x1, starting transfers between devices, local(): other = lax.ppermute(own, 'outer', swap)  5.8 us
    ppermute x1, starting transfers between devices, local(): other = lax.ppermute(send, 'outer', swap)  4.25 us
    all_to_all x2, waiting for transfers between devices, exchange(): return lax.all_to_all(x, axes, 0, 0, tiled=True)  3.1 us
  transfers between devices with their start and end apart: 5, of which 4 were waited for; matrix products, arithmetic and copies ran while one was open for 0% of the time, Pallas kernels for 9%

profile of v8, /device:TPU:1, one launch (start us, length us, event | category | flops | bytes accessed | tf_op | source)
XLA Modules:
  0.0 128.7 jit_solution(3774300340648203909)
XLA Ops:
  0.6 1.2 shard_map.91
  1.9 27.3 %all_to_all.30 = bf16[16,16,128]{2,1,0:T(8,128)(2,1)S(1)} all-to-all(bf16[16,16,128]{2,1,0:T(8,128)(2,1)S(1)} %get-tuple-element.27), channel_id=1, replica_groups=mesh['outer'=2,'yq'=4,'yp'=2,'zq'=4,'zp'=2,'x'=4] {'zq','yq'}, dimensions={0} | all-to-all | bytes 131072 | tf_op jit(solution)/shard_map/all_to_all | solution.py:379
  29.2 1.2 broadcast_in_dim.15
  30.4 5.2 %all-to-all-start.1 = ((bf16[16,256,128]{2,1,0:T(8,128)(2,1)}), bf16[16,256,128]{2,1,0:T(8,128)(2,1)S(1)}, u32[]{:S(2)}, u32[]{:S(2)}) async-start(bf16[16,256,128]{2,1,0:T(8,128)(2,1)} %broadcast_in_dim.15), calls=%async_computation.1 | async-start | bytes 2097152 | tf_op jit(solution)/shard_map/all_to_all | solution.py:379
  35.6 4.2 %collective-permute-start = (bf16[32,14336]{1,0:T(8,128)(2,1)S(1)}, bf16[32,14336]{1,0:T(8,128)(2,1)S(1)}, u32[]{:S(2)}, u32[]{:S(2)}) collective-permute-start(bf16[32,14336]{1,0:T(8,128)(2,1)S(1)} %get-tuple-element.28), channel_id=1, source_target_pairs={{0,256},{256,0},{1,257},{257,1},{2,258},{258,2},{3,259},{259,3},{4... | collective-permute-start | bytes 2752520 | tf_op jit(solution)/shard_map/ppermute | solution.py:397
  39.8 2.1 %collective-permute-done.other_ref = bf16[32,14336]{1,0:T(8,128)(2,1)S(1)} collective-permute-done((bf16[32,14336]{1,0:T(8,128)(2,1)S(1)}, bf16[32,14336]{1,0:T(8,128)(2,1)S(1)}, u32[]{:S(2)}, u32[]{:S(2)}) %collective-permute-start) | collective-permute-done | bytes 917536 | tf_op jit(solution)/shard_map/ppermute | solution.py:397
  41.9 6.3 %shard_map.92 = (bf16[4096,256]{1,0:T(8,128)(2,1)}, bf16[256,4096]{1,0:T(8,128)(2,1)S(1)}) custom-call(bf16[1,32,14336]{2,1,0:T(8,128)(2,1)} %gg_ref.5, bf16[1,32,14336]{2,1,0:T(8,128)(2,1)} %gu_ref.5, bf16[32,14336]{1,0:T(8,128)(2,1)S(1)} %collective-permute-done.other_ref), custom_call_target="tpu_custom_call" | custom-call | flops 67108864 | bytes 4194304 | tf_op jit(solution)/shard_map/pallas_call | solution.py:356
  48.2 0.8 all-to-all-done.1
  49.0 2.8 %shard_map.93 = (bf16[4096,128]{1,0:T(8,128)(2,1)S(1)}, bf16[32,128]{1,0:T(8,128)(2,1)S(1)}) custom-call(bf16[4096,128]{1,0:T(8,128)(2,1)S(1)} %bitcast.6, bf16[256,4096]{1,0:T(8,128)(2,1)S(1)} %get-tuple-element.29.turned_ref, bf16[4096,256]{1,0:T(8,128)(2,1)} %get-tuple-element.30.packed_ref), custom_call_target="tpu_custom_call" | custom-call | flops 67108864 | bytes 4194304 | tf_op jit(solution)/shard_map/pallas_call | solution.py:356
  51.9 19.7 %all_to_all.31.parts_ref = bf16[16,256,128]{2,1,0:T(8,128)(2,1)S(1)} all-to-all(bf16[16,256,128]{2,1,0:T(8,128)(2,1)S(1)} %bitcast.9), channel_id=1, replica_groups=mesh['outer'=2,'yq'=4,'yp'=2,'zq'=4,'zp'=2,'x'=4] {'x','yp','zp'}, dimensions={0} | all-to-all | bytes 2097152 | tf_op jit(solution)/shard_map/all_to_all | solution.py:379
  71.6 0.3 shard_map.94
  71.9 13.9 %all_to_all.32.parts_ref = bf16[16,16,128]{2,1,0:T(8,128)(2,1)S(1)} all-to-all(bf16[16,16,128]{2,1,0:T(8,128)(2,1)S(1)} %bitcast.12), channel_id=1, replica_groups=mesh['outer'=2,'yq'=4,'yp'=2,'zq'=4,'zp'=2,'x'=4] {'zq','yq'}, dimensions={0} | all-to-all | bytes 131072 | tf_op jit(solution)/shard_map/all_to_all | solution.py:379
  85.8 13.9 %all_to_all.33 = bf16[16,16,128]{2,1,0:T(8,128)(2,1)S(1)} all-to-all(bf16[16,16,128]{2,1,0:T(8,128)(2,1)S(1)} %get-tuple-element.32), channel_id=1, replica_groups=mesh['outer'=2,'yq'=4,'yp'=2,'zq'=4,'zp'=2,'x'=4] {'zq','yq'}, dimensions={0} | all-to-all | bytes 131072 | tf_op jit(solution)/shard_map/all_to_all | solution.py:379
  99.6 1.2 broadcast_in_dim.17
  100.8 4.8 %all-to-all-start.5 = ((bf16[16,256,128]{2,1,0:T(8,128)(2,1)}), bf16[16,256,128]{2,1,0:T(8,128)(2,1)S(1)}, u32[]{:S(2)}, u32[]{:S(2)}) async-start(bf16[16,256,128]{2,1,0:T(8,128)(2,1)} %broadcast_in_dim.17), calls=%async_computation.5 | async-start | bytes 2097152 | tf_op jit(solution)/shard_map/all_to_all | solution.py:379
  105.6 2.8 %shard_map.96 = (f32[64,128]{1,0:T(8,128)S(1)}, bf16[32,14336]{1,0:T(8,128)(2,1)S(1)}, bf16[32,14336]{1,0:T(8,128)(2,1)S(1)}) custom-call(bf16[256,128]{1,0:T(8,128)(2,1)S(1)} %bitcast.11, f32[16,128]{1,0:T(8,128)S(1)} %get-tuple-element.33.kept_ref, bf16[32,128]{1,0:T(8,128)(2,1)S(1)} %get-tuple-element.34.left_ref, bf16[1,32,14336]{2,1,0:T(8,128)(2,1)} %gg_ref.5, ...), custom_call_target="tpu_custom_call" | custom-call | flops 67108864 | bytes 4194304 | tf_op jit(solution)/shard_map/pallas_call | solution.py:356
  108.5 5.8 %collective-permute-start.1 = (f32[64,128]{1,0:T(8,128)S(1)}, f32[64,128]{1,0:T(8,128)S(1)}, u32[]{:S(2)}, u32[]{:S(2)}) collective-permute-start(f32[64,128]{1,0:T(8,128)S(1)} %get-tuple-element.35.own_ref), channel_id=1, source_target_pairs={{0,256},{256,0},{1,257},{257,1},{2,258},{258,2},{3,259},{259,3},{4... | collective-permute-start | bytes 98312 | tf_op jit(solution)/shard_map/ppermute | solution.py:440
  114.3 0.8 collective-permute-done.1.other_ref
  115.1 2.3 %all-to-all-done.5 = bf16[16,256,128]{2,1,0:T(8,128)(2,1)S(1)} async-done(((bf16[16,256,128]{2,1,0:T(8,128)(2,1)}), bf16[16,256,128]{2,1,0:T(8,128)(2,1)S(1)}, u32[]{:S(2)}, u32[]{:S(2)}) %all-to-all-start.5) | async-done | bytes 1048608 | tf_op jit(solution)/shard_map/all_to_all | solution.py:379
  117.4 6.8 %collective-permute-start.2 = (bf16[4096,128]{1,0:T(8,128)(2,1)S(1)}, bf16[4096,128]{1,0:T(8,128)(2,1)S(1)}, u32[]{:S(2)}, u32[]{:S(2)}) collective-permute-start(bf16[4096,128]{1,0:T(8,128)(2,1)S(1)} %bitcast.7), channel_id=1, source_target_pairs={{0,256},{256,0},{1,257},{257,1},{2,258},{258,2},{3,259},{259,3},{4... | collective-permute-start | bytes 3145736 | tf_op jit(solution)/shard_map/ppermute | solution.py:442
  124.3 2.5 %shard_map.97 = (f32[32,56]{1,0:T(8,128)}, f32[32,56]{1,0:T(8,128)}, f32[32,32]{1,0:T(8,128)}, f32[32,32]{1,0:T(8,128)}, bf16[1,32,14336]{2,1,0:T(8,128)(2,1)}, /*index=5*/bf16[1,32,14336]{2,1,0:T(8,128)(2,1)}) custom-call(bf16[4096,128]{1,0:T(8,128)(2,1)S(1)} %bitcast.8, f32[64,128]{1,0:T(8,128)S(1)} %get-tuple-element.35.own_ref, ...), custom_call_target="tpu_custom_call" | custom-call | flops 67108864 | bytes 4194304 | tf_op jit(solution)/shard_map/pallas_call | solution.py:356
  126.8 0.0 collective-permute-done.2.sums_ref
  126.8 1.9 %shard_map.98 = (bf16[1,32,14336]{2,1,0:T(8,128)(2,1)}, bf16[1,32,14336]{2,1,0:T(8,128)(2,1)}) custom-call(bf16[4096,128]{1,0:T(8,128)(2,1)S(1)} %collective-permute-done.2.sums_ref, f32[64,128]{1,0:T(8,128)S(1)} %collective-permute-done.1.other_ref, bf16[32,14336]{1,0:T(8,128)(2,1)S(1)} %get-tuple-element.43.grad, ...), custom_call_target="tpu_custom_call", output_to_operand_aliasing={{0}: (3, {}), {1}: (4, {})} | custom-call | flops 67108864 | bytes 4194304 | tf_op jit(solution)/shard_map/pallas_call | solution.py:356
  (1 shorter events, 0.0 us)
Async XLA Ops:
  30.4 18.7 %all-to-all-start.1 = ((bf16[16,256,128]{2,1,0:T(8,128)(2,1)}), bf16[16,256,128]{2,1,0:T(8,128)(2,1)S(1)}, u32[]{:S(2)}, u32[]{:S(2)}) async-start(bf16[16,256,128]{2,1,0:T(8,128)(2,1)} %broadcast_in_dim.15), calls=%async_computation.1 | async-start | bytes 2097152 | tf_op jit(solution)/shard_map/all_to_all | solution.py:379
  35.6 6.3 %collective-permute-start = (bf16[32,14336]{1,0:T(8,128)(2,1)S(1)}, bf16[32,14336]{1,0:T(8,128)(2,1)S(1)}, u32[]{:S(2)}, u32[]{:S(2)}) collective-permute-start(bf16[32,14336]{1,0:T(8,128)(2,1)S(1)} %get-tuple-element.28), channel_id=1, source_target_pairs={{0,256},{256,0},{1,257},{257,1},{2,258},{258,2},{3,259},{259,3},{4... | collective-permute-start | bytes 2752520 | tf_op jit(solution)/shard_map/ppermute | solution.py:397
  100.8 16.6 %all-to-all-start.5 = ((bf16[16,256,128]{2,1,0:T(8,128)(2,1)}), bf16[16,256,128]{2,1,0:T(8,128)(2,1)S(1)}, u32[]{:S(2)}, u32[]{:S(2)}) async-start(bf16[16,256,128]{2,1,0:T(8,128)(2,1)} %broadcast_in_dim.17), calls=%async_computation.5 | async-start | bytes 2097152 | tf_op jit(solution)/shard_map/all_to_all | solution.py:379
  108.5 6.6 %collective-permute-start.1 = (f32[64,128]{1,0:T(8,128)S(1)}, f32[64,128]{1,0:T(8,128)S(1)}, u32[]{:S(2)}, u32[]{:S(2)}) collective-permute-start(f32[64,128]{1,0:T(8,128)S(1)} %get-tuple-element.35.own_ref), channel_id=1, source_target_pairs={{0,256},{256,0},{1,257},{257,1},{2,258},{258,2},{3,259},{259,3},{4... | collective-permute-start | bytes 98312 | tf_op jit(solution)/shard_map/ppermute | solution.py:440
  117.4 9.4 %collective-permute-start.2 = (bf16[4096,128]{1,0:T(8,128)(2,1)S(1)}, bf16[4096,128]{1,0:T(8,128)(2,1)S(1)}, u32[]{:S(2)}, u32[]{:S(2)}) collective-permute-start(bf16[4096,128]{1,0:T(8,128)(2,1)S(1)} %bitcast.7), channel_id=1, source_target_pairs={{0,256},{256,0},{1,257},{257,1},{2,258},{258,2},{3,259},{259,3},{4... | collective-permute-start | bytes 3145736 | tf_op jit(solution)/shard_map/ppermute | solution.py:442

commit v9 on v8

--- a/solution.py
+++ b/solution.py
@@ -223,7 +223,7 @@
         for s in range(1, 3):
             gram = gram + tiles[pl.ds(3 * odd + s, half, stride=8), :]
         grams[pl.ds(odd, half, stride=2), :] = gram
-    m = jnp.where(group == 0, pltpu.roll(grams[...], 32, 1), 0.0)
+    m = jnp.where(group == 0, pltpu.roll(grams[0:R], 32, 1), 0.0)
     m = jnp.where((group == 1) & (row == lane % R), 1.0, m)
     pivots = jnp.ones((R, 128), F32)
     for first in range(0, R, BLOCK):
@@ -431,7 +431,7 @@
     own, own_grad, other_grad = call(
         solve_kernel,
         (shape((2 * R, 128), F32), natural, natural),
-        [pltpu.VMEM((128, 128), F32), pltpu.VMEM((R, 128), F32), dma((2,))],
+        [pltpu.VMEM((136, 128), F32), pltpu.VMEM((R + 8, 128), F32), dma((2,))],
         "vvvhh",
         "vvv",
         1 << 26,

time: 129 us -> 129 us (level)
  no operation moved by 1% of the time
where the time goes in v9:
time: 129 us
  blocking collectives  74.8 us (58%)
  starting transfers between devices  26.9 us (21%)
  Pallas kernels  17.9 us (14%)
  waiting for transfers between devices  6.02 us (5%)
  local copies, waits for them, and re-layouts  2.35 us (2%)
    all_to_all x4, blocking collectives, exchange(): return lax.all_to_all(x, axes, 0, 0, tiled=True)  74.8 us
    pallas_call x8, Pallas kernels, pinned(): run(*(pltpu.with_memory_space_constraint(x, pltpu.HBM) if s == 'h' and (n...  17.9 us
    all_to_all x2, starting transfers between devices, exchange(): return lax.all_to_all(x, axes, 0, 0, tiled=True)  10 us
    ppermute x1, starting transfers between devices, local(): sums_other = lax.ppermute(sums, 'outer', swap)  6.84 us
    ppermute x1, starting transfers between devices, local(): other = lax.ppermute(own, 'outer', swap)  5.8 us
    ppermute x1, starting transfers between devices, local(): other = lax.ppermute(send, 'outer', swap)  4.25 us
    all_to_all x2, waiting for transfers between devices, exchange(): return lax.all_to_all(x, axes, 0, 0, tiled=True)  3.1 us
  transfers between devices with their start and end apart: 5, of which 4 were waited for; matrix products, arithmetic and copies ran while one was open for 0% of the time, Pallas kernels for 9%

profile of v9, /device:TPU:1, one launch (start us, length us, event | category | flops | bytes accessed | tf_op | source)
XLA Modules:
  0.0 128.7 jit_solution(5216229557444201632)
XLA Ops:
  0.6 1.2 shard_map.91
  1.9 27.3 %all_to_all.30 = bf16[16,16,128]{2,1,0:T(8,128)(2,1)S(1)} all-to-all(bf16[16,16,128]{2,1,0:T(8,128)(2,1)S(1)} %get-tuple-element.27), channel_id=1, replica_groups=mesh['outer'=2,'yq'=4,'yp'=2,'zq'=4,'zp'=2,'x'=4] {'zq','yq'}, dimensions={0} | all-to-all | bytes 131072 | tf_op jit(solution)/shard_map/all_to_all | solution.py:379
  29.2 1.2 broadcast_in_dim.15
  30.4 5.2 %all-to-all-start.1 = ((bf16[16,256,128]{2,1,0:T(8,128)(2,1)}), bf16[16,256,128]{2,1,0:T(8,128)(2,1)S(1)}, u32[]{:S(2)}, u32[]{:S(2)}) async-start(bf16[16,256,128]{2,1,0:T(8,128)(2,1)} %broadcast_in_dim.15), calls=%async_computation.1 | async-start | bytes 2097152 | tf_op jit(solution)/shard_map/all_to_all | solution.py:379
  35.6 4.2 %collective-permute-start = (bf16[32,14336]{1,0:T(8,128)(2,1)S(1)}, bf16[32,14336]{1,0:T(8,128)(2,1)S(1)}, u32[]{:S(2)}, u32[]{:S(2)}) collective-permute-start(bf16[32,14336]{1,0:T(8,128)(2,1)S(1)} %get-tuple-element.28), channel_id=1, source_target_pairs={{0,256},{256,0},{1,257},{257,1},{2,258},{258,2},{3,259},{259,3},{4... | collective-permute-start | bytes 2752520 | tf_op jit(solution)/shard_map/ppermute | solution.py:397
  39.8 2.1 %collective-permute-done.other_ref = bf16[32,14336]{1,0:T(8,128)(2,1)S(1)} collective-permute-done((bf16[32,14336]{1,0:T(8,128)(2,1)S(1)}, bf16[32,14336]{1,0:T(8,128)(2,1)S(1)}, u32[]{:S(2)}, u32[]{:S(2)}) %collective-permute-start) | collective-permute-done | bytes 917536 | tf_op jit(solution)/shard_map/ppermute | solution.py:397
  41.9 6.3 %shard_map.92 = (bf16[4096,256]{1,0:T(8,128)(2,1)}, bf16[256,4096]{1,0:T(8,128)(2,1)S(1)}) custom-call(bf16[1,32,14336]{2,1,0:T(8,128)(2,1)} %gg_ref.5, bf16[1,32,14336]{2,1,0:T(8,128)(2,1)} %gu_ref.5, bf16[32,14336]{1,0:T(8,128)(2,1)S(1)} %collective-permute-done.other_ref), custom_call_target="tpu_custom_call" | custom-call | flops 67108864 | bytes 4194304 | tf_op jit(solution)/shard_map/pallas_call | solution.py:356
  48.2 0.8 all-to-all-done.1
  49.0 2.8 %shard_map.93 = (bf16[4096,128]{1,0:T(8,128)(2,1)S(1)}, bf16[32,128]{1,0:T(8,128)(2,1)S(1)}) custom-call(bf16[4096,128]{1,0:T(8,128)(2,1)S(1)} %bitcast.6, bf16[256,4096]{1,0:T(8,128)(2,1)S(1)} %get-tuple-element.29.turned_ref, bf16[4096,256]{1,0:T(8,128)(2,1)} %get-tuple-element.30.packed_ref), custom_call_target="tpu_custom_call" | custom-call | flops 67108864 | bytes 4194304 | tf_op jit(solution)/shard_map/pallas_call | solution.py:356
  51.9 19.7 %all_to_all.31.parts_ref = bf16[16,256,128]{2,1,0:T(8,128)(2,1)S(1)} all-to-all(bf16[16,256,128]{2,1,0:T(8,128)(2,1)S(1)} %bitcast.9), channel_id=1, replica_groups=mesh['outer'=2,'yq'=4,'yp'=2,'zq'=4,'zp'=2,'x'=4] {'x','yp','zp'}, dimensions={0} | all-to-all | bytes 2097152 | tf_op jit(solution)/shard_map/all_to_all | solution.py:379
  71.6 0.3 shard_map.94
  71.9 13.9 %all_to_all.32.parts_ref = bf16[16,16,128]{2,1,0:T(8,128)(2,1)S(1)} all-to-all(bf16[16,16,128]{2,1,0:T(8,128)(2,1)S(1)} %bitcast.12), channel_id=1, replica_groups=mesh['outer'=2,'yq'=4,'yp'=2,'zq'=4,'zp'=2,'x'=4] {'zq','yq'}, dimensions={0} | all-to-all | bytes 131072 | tf_op jit(solution)/shard_map/all_to_all | solution.py:379
  85.8 13.9 %all_to_all.33 = bf16[16,16,128]{2,1,0:T(8,128)(2,1)S(1)} all-to-all(bf16[16,16,128]{2,1,0:T(8,128)(2,1)S(1)} %get-tuple-element.32), channel_id=1, replica_groups=mesh['outer'=2,'yq'=4,'yp'=2,'zq'=4,'zp'=2,'x'=4] {'zq','yq'}, dimensions={0} | all-to-all | bytes 131072 | tf_op jit(solution)/shard_map/all_to_all | solution.py:379
  99.6 1.2 broadcast_in_dim.17
  100.8 4.8 %all-to-all-start.5 = ((bf16[16,256,128]{2,1,0:T(8,128)(2,1)}), bf16[16,256,128]{2,1,0:T(8,128)(2,1)S(1)}, u32[]{:S(2)}, u32[]{:S(2)}) async-start(bf16[16,256,128]{2,1,0:T(8,128)(2,1)} %broadcast_in_dim.17), calls=%async_computation.5 | async-start | bytes 2097152 | tf_op jit(solution)/shard_map/all_to_all | solution.py:379
  105.6 2.8 %shard_map.96 = (f32[64,128]{1,0:T(8,128)S(1)}, bf16[32,14336]{1,0:T(8,128)(2,1)S(1)}, bf16[32,14336]{1,0:T(8,128)(2,1)S(1)}) custom-call(bf16[256,128]{1,0:T(8,128)(2,1)S(1)} %bitcast.11, f32[16,128]{1,0:T(8,128)S(1)} %get-tuple-element.33.kept_ref, bf16[32,128]{1,0:T(8,128)(2,1)S(1)} %get-tuple-element.34.left_ref, bf16[1,32,14336]{2,1,0:T(8,128)(2,1)} %gg_ref.5, ...), custom_call_target="tpu_custom_call" | custom-call | flops 67108864 | bytes 4194304 | tf_op jit(solution)/shard_map/pallas_call | solution.py:356
  108.5 5.8 %collective-permute-start.1 = (f32[64,128]{1,0:T(8,128)S(1)}, f32[64,128]{1,0:T(8,128)S(1)}, u32[]{:S(2)}, u32[]{:S(2)}) collective-permute-start(f32[64,128]{1,0:T(8,128)S(1)} %get-tuple-element.35.own_ref), channel_id=1, source_target_pairs={{0,256},{256,0},{1,257},{257,1},{2,258},{258,2},{3,259},{259,3},{4... | collective-permute-start | bytes 98312 | tf_op jit(solution)/shard_map/ppermute | solution.py:440
  114.3 0.8 collective-permute-done.1.other_ref
  115.1 2.3 %all-to-all-done.5 = bf16[16,256,128]{2,1,0:T(8,128)(2,1)S(1)} async-done(((bf16[16,256,128]{2,1,0:T(8,128)(2,1)}), bf16[16,256,128]{2,1,0:T(8,128)(2,1)S(1)}, u32[]{:S(2)}, u32[]{:S(2)}) %all-to-all-start.5) | async-done | bytes 1048608 | tf_op jit(solution)/shard_map/all_to_all | solution.py:379
  117.4 6.8 %collective-permute-start.2 = (bf16[4096,128]{1,0:T(8,128)(2,1)S(1)}, bf16[4096,128]{1,0:T(8,128)(2,1)S(1)}, u32[]{:S(2)}, u32[]{:S(2)}) collective-permute-start(bf16[4096,128]{1,0:T(8,128)(2,1)S(1)} %bitcast.7), channel_id=1, source_target_pairs={{0,256},{256,0},{1,257},{257,1},{2,258},{258,2},{3,259},{259,3},{4... | collective-permute-start | bytes 3145736 | tf_op jit(solution)/shard_map/ppermute | solution.py:442
  124.3 2.5 %shard_map.97 = (f32[32,56]{1,0:T(8,128)}, f32[32,56]{1,0:T(8,128)}, f32[32,32]{1,0:T(8,128)}, f32[32,32]{1,0:T(8,128)}, bf16[1,32,14336]{2,1,0:T(8,128)(2,1)}, /*index=5*/bf16[1,32,14336]{2,1,0:T(8,128)(2,1)}) custom-call(bf16[4096,128]{1,0:T(8,128)(2,1)S(1)} %bitcast.8, f32[64,128]{1,0:T(8,128)S(1)} %get-tuple-element.35.own_ref, ...), custom_call_target="tpu_custom_call" | custom-call | flops 67108864 | bytes 4194304 | tf_op jit(solution)/shard_map/pallas_call | solution.py:356
  126.8 0.0 collective-permute-done.2.sums_ref
  126.8 1.9 %shard_map.98 = (bf16[1,32,14336]{2,1,0:T(8,128)(2,1)}, bf16[1,32,14336]{2,1,0:T(8,128)(2,1)}) custom-call(bf16[4096,128]{1,0:T(8,128)(2,1)S(1)} %collective-permute-done.2.sums_ref, f32[64,128]{1,0:T(8,128)S(1)} %collective-permute-done.1.other_ref, bf16[32,14336]{1,0:T(8,128)(2,1)S(1)} %get-tuple-element.43.grad, ...), custom_call_target="tpu_custom_call", output_to_operand_aliasing={{0}: (3, {}), {1}: (4, {})} | custom-call | flops 67108864 | bytes 4194304 | tf_op jit(solution)/shard_map/pallas_call | solution.py:356
  (1 shorter events, 0.0 us)
Async XLA Ops:
  30.4 18.7 %all-to-all-start.1 = ((bf16[16,256,128]{2,1,0:T(8,128)(2,1)}), bf16[16,256,128]{2,1,0:T(8,128)(2,1)S(1)}, u32[]{:S(2)}, u32[]{:S(2)}) async-start(bf16[16,256,128]{2,1,0:T(8,128)(2,1)} %broadcast_in_dim.15), calls=%async_computation.1 | async-start | bytes 2097152 | tf_op jit(solution)/shard_map/all_to_all | solution.py:379
  35.6 6.3 %collective-permute-start = (bf16[32,14336]{1,0:T(8,128)(2,1)S(1)}, bf16[32,14336]{1,0:T(8,128)(2,1)S(1)}, u32[]{:S(2)}, u32[]{:S(2)}) collective-permute-start(bf16[32,14336]{1,0:T(8,128)(2,1)S(1)} %get-tuple-element.28), channel_id=1, source_target_pairs={{0,256},{256,0},{1,257},{257,1},{2,258},{258,2},{3,259},{259,3},{4... | collective-permute-start | bytes 2752520 | tf_op jit(solution)/shard_map/ppermute | solution.py:397
  100.8 16.6 %all-to-all-start.5 = ((bf16[16,256,128]{2,1,0:T(8,128)(2,1)}), bf16[16,256,128]{2,1,0:T(8,128)(2,1)S(1)}, u32[]{:S(2)}, u32[]{:S(2)}) async-start(bf16[16,256,128]{2,1,0:T(8,128)(2,1)} %broadcast_in_dim.17), calls=%async_computation.5 | async-start | bytes 2097152 | tf_op jit(solution)/shard_map/all_to_all | solution.py:379
  108.5 6.6 %collective-permute-start.1 = (f32[64,128]{1,0:T(8,128)S(1)}, f32[64,128]{1,0:T(8,128)S(1)}, u32[]{:S(2)}, u32[]{:S(2)}) collective-permute-start(f32[64,128]{1,0:T(8,128)S(1)} %get-tuple-element.35.own_ref), channel_id=1, source_target_pairs={{0,256},{256,0},{1,257},{257,1},{2,258},{258,2},{3,259},{259,3},{4... | collective-permute-start | bytes 98312 | tf_op jit(solution)/shard_map/ppermute | solution.py:440
  117.4 9.4 %collective-permute-start.2 = (bf16[4096,128]{1,0:T(8,128)(2,1)S(1)}, bf16[4096,128]{1,0:T(8,128)(2,1)S(1)}, u32[]{:S(2)}, u32[]{:S(2)}) collective-permute-start(bf16[4096,128]{1,0:T(8,128)(2,1)S(1)} %bitcast.7), channel_id=1, source_target_pairs={{0,256},{256,0},{1,257},{257,1},{2,258},{258,2},{3,259},{259,3},{4... | collective-permute-start | bytes 3145736 | tf_op jit(solution)/shard_map/ppermute | solution.py:442
